TPU v7x, 256 devices: a whole 4x4x8 slice. The times are simulated.
256 devices in a mesh: lat: 16 (over y, z_hi), lon: 8 (over z_lo, x), comp: 2 (over core).
Axes of the slice: x: 4, y: 4, z: 8 (z_hi: 4, z_lo: 2; z = z_hi * 2 + z_lo), core: 2. Of those that a mesh axis runs over, the one named last changes fastest.
Arguments:
- atm_state: bfloat16 [384, 1024, 384], P('lat', ('lon', 'comp')), may hold values from -6 to 6
- ocean_state: bfloat16 [384, 1024, 256], P(('lat', 'comp'), 'lon'), may hold values from -6 to 6
- wet_mask: int32 [384, 1024], P(('lat', 'comp'), 'lon'), may hold values 0 or 1
- legendre: bfloat16 [512, 384, 384], P(('lat', 'lon', 'comp')), may hold values from -4 to 4
- quad_weight: float32 [384], replicated, may hold values from 0.5 to 2
- spec_real: bfloat16 [384, 384], replicated, may hold values from -0.3125 to 0.3125
- spec_imag: bfloat16 [384, 384], replicated, may hold values from -0.3125 to 0.3125
- degree_gain: float32 [384], replicated, may hold values from 0.5 to 2
- atm_gain: float32 [2, 384], replicated, may hold values from 0.1 to 1.9
- atm_up: bfloat16 [384, 768], replicated, may hold values from -0.3125 to 0.3125
- atm_down: bfloat16 [768, 384], replicated, may hold values from -0.21875 to 0.21875
- atm_to_surface: bfloat16 [384, 32], replicated, may hold values from -0.3125 to 0.3125
- surface_to_atm: bfloat16 [32, 384], replicated, may hold values from -1 to 1
- ocean_to_surface: bfloat16 [256, 32], replicated, may hold values from -0.375 to 0.375
- surface_to_ocean: bfloat16 [32, 256], replicated, may hold values from -1 to 1
- ocean_kernel: bfloat16 [2, 7, 7, 256], replicated, may hold values from -0.875 to 0.875
- ocean_gain: float32 [2, 256], replicated, may hold values from 0.1 to 1.9
- ocean_up: bfloat16 [2, 256, 1024], replicated, may hold values from -0.375 to 0.375
- ocean_down: bfloat16 [2, 1024, 256], replicated, may hold values from -0.1875 to 0.1875
Outputs:
- atm_out: bfloat16 [384, 1024, 384], P('lat', ('lon', 'comp'))
- ocean_out: bfloat16 [384, 1024, 256], P(('lat', 'comp'), 'lon')
All inputs are finite; a program needn't handle non-finite values. No bound on the sum of `wet_mask` on one device may be relied on, other than what follows from the above.
Results may differ from a plain program's by a relative error of at most 0.01.
Values may be sent and summed in bfloat16 or wider, within the bound.
No kernel may reach another device: no remote copies, remote signals or barrier semaphores. Data moves between devices by JAX's collectives and lax.ppermute only.
A program may use at most 128 MiB of HBM per device.

v0:
```python
import math

import jax
import jax.numpy as jnp
import ml_dtypes
import numpy as np
from jax import lax
from jax.experimental import pallas as pl
from jax.experimental.pallas import tpu as pltpu
from jax.sharding import PartitionSpec as P

MODES = 512
STENCIL_TAPS = 7
OCEAN_DILATION = 2
LON_COMP = ("lon", "comp")
LON = ("lon",)
LAT_LON = ("lat", "lon")


epsilon = 1e-05


def wave_tables(lat_count, lon_count, circle, owned):
    rows = np.arange(lat_count * lon_count * owned)
    block = circle // (2 * lon_count)
    where = np.arange(lon_count * block)
    forward, inverse = [], []
    row_sets = [rows // owned * 2 * owned + q * owned + rows % owned for q in range(2)]
    place_sets = [(where // block * 2 + q) * block + where % block for q in range(2)]

    def waves(row, place):
        phase = (row[:, None] // 2) * place[None, :] % circle
        angle = phase.astype(np.float32) * np.float32(2.0 * math.pi / circle)
        return np.where((row % 2 == 0)[:, None], np.cos(angle), -np.sin(angle)).astype(np.float32)

    for own in range(2):
        order = (own, 1 - own)
        f = np.concatenate([waves(row_sets[own], place_sets[q]) for q in order], 1)
        forward.append(f / np.float32(math.sqrt(circle)))
        g = []
        for q in order:
            factor = np.where(row_sets[q] // 2 == 0, 1.0, 2.0).astype(np.float32)
            g.append((waves(row_sets[q], place_sets[own]) * factor[:, None]).T)
        inverse.append(np.concatenate(g, 1) / np.float32(math.sqrt(circle)))
    return (
        np.stack(forward).astype(ml_dtypes.bfloat16),
        np.stack(inverse).astype(ml_dtypes.bfloat16),
    )


def forward_kernel(table_ref, own_ref, other_ref, out_ref):
    groups, lats, span, width = own_ref.shape
    half = groups * span
    for i in range(lats):
        total = jnp.dot(
            table_ref[:, :half],
            own_ref[:, i].reshape(half, width),
            preferred_element_type=jnp.float32,
        ) + jnp.dot(
            table_ref[:, half:],
            other_ref[:, i].reshape(half, width),
            preferred_element_type=jnp.float32,
        )
        out_ref[:, i] = total.astype(jnp.bfloat16).reshape(
            out_ref.shape[0], out_ref.shape[2], width
        )


def inverse_kernel(table_ref, own_ref, other_ref, out_ref):
    owners, lats, owned, width = own_ref.shape
    half = owners * owned
    for i in range(lats):
        total = jnp.dot(
            table_ref[:, :half],
            own_ref[:, i].reshape(half, width),
            preferred_element_type=jnp.float32,
        ) + jnp.dot(
            table_ref[:, half:],
            other_ref[:, i].reshape(half, width),
            preferred_element_type=jnp.float32,
        )
        out_ref[:, i] = total.astype(jnp.bfloat16).reshape(
            out_ref.shape[0], out_ref.shape[2], width
        )


def filter_kernel(
    weighted_ref, turned_ref, spectrum_ref, real_ref, imag_ref, gain_ref, out_ref, rows_ref
):
    count = weighted_ref.shape[0]
    lats, owned, width = spectrum_ref.shape
    block = 64
    side = block * owned
    r = lax.broadcasted_iota(jnp.int32, (side, side), 0)
    s = lax.broadcasted_iota(jnp.int32, (side, side), 1)
    pick = jnp.where((r % block) * owned + r // block == s, 1.0, 0.0).astype(jnp.bfloat16)
    back = jnp.where((s % block) * owned + s // block == r, 1.0, 0.0).astype(jnp.bfloat16)
    for b in range(lats // block):
        piece = spectrum_ref[b * block : (b + 1) * block].reshape(side, width)
        moved = jnp.dot(pick, piece, preferred_element_type=jnp.float32).astype(jnp.bfloat16)
        for p in range(owned):
            rows_ref[p, b * block : (b + 1) * block] = moved[p * block : (p + 1) * block]
    real, imag, gain = real_ref[...], imag_ref[...], gain_ref[...]
    for m in range(count):
        parts = [
            jnp.dot(
                weighted_ref[m], rows_ref[2 * m + q], preferred_element_type=jnp.float32
            ).astype(jnp.bfloat16)
            for q in range(2)
        ]
        mixed_real = jnp.dot(parts[0], real, preferred_element_type=jnp.float32) - jnp.dot(
            parts[1], imag, preferred_element_type=jnp.float32
        )
        mixed_imag = jnp.dot(parts[0], imag, preferred_element_type=jnp.float32) + jnp.dot(
            parts[1], real, preferred_element_type=jnp.float32
        )
        for q, mixed in enumerate((mixed_real, mixed_imag)):
            filtered = (mixed * gain).astype(jnp.bfloat16)
            rows_ref[2 * m + q] = jnp.dot(
                turned_ref[m], filtered, preferred_element_type=jnp.float32
            ).astype(jnp.bfloat16)
    for b in range(lats // block):
        piece = jnp.concatenate(
            [rows_ref[p, b * block : (b + 1) * block] for p in range(owned)], axis=0
        )
        moved = jnp.dot(back, piece, preferred_element_type=jnp.float32).astype(jnp.bfloat16)
        out_ref[b * block : (b + 1) * block] = moved.reshape(block, owned, width)


def call(kernel, shape, *args, scratch=(), limit=16, scalars=0):
    spaces = [pltpu.SMEM] * scalars + [pltpu.VMEM] * (len(args) - scalars)
    return pl.pallas_call(
        kernel,
        out_shape=jax.ShapeDtypeStruct(shape, jnp.bfloat16),
        in_specs=[pl.BlockSpec(memory_space=space) for space in spaces],
        out_specs=pl.BlockSpec(memory_space=pltpu.VMEM),
        scratch_shapes=list(scratch),
        compiler_params=pltpu.CompilerParams(vmem_limit_bytes=limit * 2**20),
    )(*args)


def gelu(x):
    inner = x * (math.sqrt(2.0 / math.pi) + (math.sqrt(2.0 / math.pi) * 0.044715) * (x * x))
    half = 0.5 * x
    return half + half * jnp.tanh(inner)


def normalised(values, gain):
    centred = values - jnp.mean(values, axis=-1, keepdims=True)
    spread = jnp.mean(centred * centred, axis=-1, keepdims=True)
    return (centred * lax.rsqrt(spread + epsilon) * gain).astype(jnp.bfloat16)


def prologue_kernel(atm_ref, flux_ref, out_weight_ref, gain_ref, normed_ref):
    rows, lon_dev, width = atm_ref.shape
    forced = atm_ref[...].reshape(rows * lon_dev, width).astype(jnp.float32) + jnp.dot(
        flux_ref[...], out_weight_ref[...], preferred_element_type=jnp.float32
    )
    normed_ref[...] = normalised(forced, gain_ref[...]).reshape(rows, lon_dev, width)


def epilogue_kernel(
    atm_ref, flux_ref, spectral_ref, out_weight_ref, gain_ref, up_ref, down_ref, out_ref
):
    rows, lon_dev, width = atm_ref.shape
    side = rows * lon_dev
    forced = atm_ref[...].reshape(side, width).astype(jnp.float32) + jnp.dot(
        flux_ref[...], out_weight_ref[...], preferred_element_type=jnp.float32
    )
    mixed = forced + spectral_ref[...].reshape(side, width).astype(jnp.float32)
    normed = normalised(mixed, gain_ref[...])
    hidden = gelu(jnp.dot(normed, up_ref[...], preferred_element_type=jnp.float32))
    total = mixed + jnp.dot(
        hidden.astype(jnp.bfloat16), down_ref[...], preferred_element_type=jnp.float32
    )
    out_ref[...] = total.astype(jnp.bfloat16).reshape(rows, lon_dev, width)


def by_rows(kernel, atm, flux, spectral, weights, rows=4):
    lat_dev, lon_dev, width = atm.shape
    field = pl.BlockSpec((rows, lon_dev, width), lambda i: (i, 0, 0))
    fields = [atm, flux] + ([] if spectral is None else [spectral])
    specs = [field, pl.BlockSpec((rows * lon_dev, flux.shape[1]), lambda i: (i, 0))]
    specs += [] if spectral is None else [field]
    specs += [pl.BlockSpec(w.shape, lambda i: (0, 0)) for w in weights]
    return pl.pallas_call(
        kernel,
        grid=(lat_dev // rows,),
        out_shape=jax.ShapeDtypeStruct(atm.shape, jnp.bfloat16),
        in_specs=specs,
        out_specs=field,
        compiler_params=pltpu.CompilerParams(vmem_limit_bytes=16 * 2**20),
    )(*fields, *weights)


HALO = 16
LEAD = 8
LANES = 128
REACH = STENCIL_TAPS // 2 * OCEAN_DILATION


def ocean_rows(field, kern, gain, up, down, sums, out_ref, group, edges):
    blocks = field.shape[0]
    rows, cols, width = out_ref.shape
    stride = cols // 8
    each = stride // OCEAN_DILATION

    def step(g, carry):
        top = g * group
        for r in range(group):
            for lane in range(blocks):
                part = slice(lane * LANES, (lane + 1) * LANES)
                for parity in range(OCEAN_DILATION):
                    acc = [None] * each
                    for a in range(STENCIL_TAPS):
                        row = top + r + a * OCEAN_DILATION
                        first = LEAD - REACH + parity
                        loads = [
                            field[lane, row, pl.ds(first + OCEAN_DILATION * q, 8, stride=stride), :]
                            for q in range(each + STENCIL_TAPS - 1)
                        ]
                        for b in range(STENCIL_TAPS):
                            weight = kern[a * STENCIL_TAPS + b, :, part]
                            for q in range(each):
                                term = loads[q + b] * weight
                                acc[q] = term if acc[q] is None else acc[q] + term
                    for q in range(each):
                        at = pl.ds(parity + OCEAN_DILATION * q, 8, stride=stride)
                        sums[lane, r, at, :] = acc[q]
        side = group * cols
        stencil = jnp.concatenate(
            [sums[lane].reshape(side, LANES) for lane in range(blocks)], axis=1
        )
        normed = normalised(stencil, gain[...])
        hidden = gelu(jnp.dot(normed, up[...], preferred_element_type=jnp.float32))
        total = jnp.dot(
            hidden.astype(jnp.bfloat16), down[...], preferred_element_type=jnp.float32
        )
        for r in range(group):
            centre = jnp.concatenate(
                [field[lane, top + r + REACH, LEAD : LEAD + cols, :] for lane in range(blocks)],
                axis=1,
            )
            value = centre + total[r * cols : (r + 1) * cols]
            if edges is not None:
                row = edges[0] + top + r
                low, high = -edges[2], edges[3] - edges[2]
                high = jnp.where((row >= 0) & (row < edges[1]), high, low)
                col = lax.broadcasted_iota(jnp.int32, value.shape, 0)
                value = jnp.where((col >= low) & (col < high), value, 0.0)
            out_ref[top + r] = value.astype(jnp.bfloat16)
        return carry

    lax.fori_loop(0, rows // group, step, 0)


def first_ocean_kernel(
    edges_ref,
    centre_ref,
    north_ref,
    south_ref,
    west_ref,
    east_ref,
    nw_ref,
    ne_ref,
    sw_ref,
    se_ref,
    kern_ref,
    gain_ref,
    up_ref,
    down_ref,
    out_ref,
    field,
    sums,
):
    rows, cols, width = centre_ref.shape
    columns = (slice(0, HALO), slice(HALO, HALO + cols), slice(HALO + cols, cols + 2 * HALO))
    grid = (
        (nw_ref, north_ref, ne_ref),
        (west_ref, centre_ref, east_ref),
        (sw_ref, south_ref, se_ref),
    )
    for y, line in enumerate(grid):
        for x, ref in enumerate(line):
            for lane in range(width // LANES):
                field[lane, y * rows : (y + 1) * rows, columns[x], :] = ref[
                    :, :, lane * LANES : (lane + 1) * LANES
                ].astype(jnp.float32)
    edges = [edges_ref[n] for n in range(4)]
    ocean_rows(field, kern_ref, gain_ref, up_ref, down_ref, sums, out_ref, sums.shape[1], edges)


def second_ocean_kernel(
    first_ref, kern_ref, gain_ref, up_ref, down_ref, out_ref, field, sums
):
    for lane in range(field.shape[0]):
        field[lane] = first_ref[:, :, lane * LANES : (lane + 1) * LANES].astype(jnp.float32)
    ocean_rows(field, kern_ref, gain_ref, up_ref, down_ref, sums, out_ref, sums.shape[1], None)


def shifted(block, dy, dx):
    axes = ("lat", "lon", "comp")
    tall = lax.axis_size("lat") * lax.axis_size("comp")
    broad = lax.axis_size("lon")

    def place(y, x):
        return (y // 2 * broad + x) * 2 + y % 2

    pairs = [
        (place(y, x), place(y + dy, x + dx))
        for y in range(tall)
        for x in range(broad)
        if 0 <= y + dy < tall and 0 <= x + dx < broad
    ]
    return lax.ppermute(block, axes, pairs)


def local(
    atm_state,
    ocean_state,
    wet_mask,
    legendre,
    quad_weight,
    spec_real,
    spec_imag,
    degree_gain,
    atm_gain,
    atm_up,
    atm_down,
    atm_to_surface,
    surface_to_atm,
    ocean_to_surface,
    surface_to_ocean,
    ocean_kernel,
    ocean_gain,
    ocean_up,
    ocean_down,
):
    lat_count = lax.axis_size("lat")
    lon_count = lax.axis_size("lon")
    lat_dev, lon_dev, width = atm_state.shape
    sea_rows, sea_cols, sea_width = ocean_state.shape
    lat_total = lat_dev * lat_count
    circle = lon_dev * lon_count * 2
    owned = 2 * legendre.shape[0]
    owners = lat_count * lon_count
    lats = lat_dev // lon_count
    me = lax.axis_index("comp")
    swap = [(0, 1), (1, 0)]
    forward, inverse = wave_tables(lat_count, lon_count, circle, owned)
    forward = lax.dynamic_index_in_dim(jnp.asarray(forward), me, 0, keepdims=False)
    inverse = lax.dynamic_index_in_dim(jnp.asarray(inverse), me, 0, keepdims=False)
    wet = wet_mask.astype(jnp.float32)[:, :, None]
    ocean_flux = (
        jnp.dot(ocean_state, ocean_to_surface, preferred_element_type=jnp.float32) * wet
    ).astype(jnp.bfloat16)
    atm_flux = jnp.dot(atm_state, atm_to_surface, preferred_element_type=jnp.float32).astype(
        jnp.bfloat16
    )

    def halves(mine, dim):
        low, high = jnp.split(mine, 2, axis=dim)
        return (jnp.where(me == 0, low, high), jnp.where(me == 0, high, low))

    def together(kept, got, dim):
        low = jnp.where(me == 0, kept, got)
        high = jnp.where(me == 0, got, kept)
        return jnp.concatenate([low, high], axis=dim)

    kept_ocean, sent_ocean = halves(ocean_flux, 1)
    kept_atm, sent_atm = halves(atm_flux, 0)
    got = lax.ppermute(jnp.stack([sent_ocean, sent_atm]), "comp", swap)
    flux_here = together(kept_ocean, got[0], 0).reshape(lat_dev * lon_dev, -1)
    flux_sea = together(kept_atm, got[1], 1)
    normed = by_rows(
        prologue_kernel, atm_state, flux_here, None, (surface_to_atm, atm_gain[:1])
    )
    ocean_in = (
        ocean_state.astype(jnp.float32)
        + wet * jnp.dot(flux_sea, surface_to_ocean, preferred_element_type=jnp.float32)
    ).astype(jnp.bfloat16)
    normed, ocean_in = lax.optimization_barrier((normed, ocean_in))
    rings = lax.all_to_all(
        normed.reshape(lon_count, lats, lon_dev, width), "lon", 0, 0, tiled=True
    )
    west, east = ocean_in[:, -HALO:], ocean_in[:, :HALO]
    pieces = (
        shifted(ocean_in, 1, 0),
        shifted(ocean_in, -1, 0),
        shifted(west, 0, 1),
        shifted(east, 0, -1),
        shifted(west, 1, 1),
        shifted(east, 1, -1),
        shifted(west, -1, 1),
        shifted(east, -1, -1),
    )
    rings, pieces = lax.optimization_barrier((rings, pieces))
    weighted = (legendre.astype(jnp.float32) * (quad_weight / lat_total)).astype(jnp.bfloat16)
    turned = jnp.swapaxes(legendre, 1, 2)
    spectrum = call(
        forward_kernel,
        (owners, lats, owned, width),
        forward,
        rings,
        lax.ppermute(rings, "comp", swap),
    )
    spectrum, pieces = lax.optimization_barrier((spectrum, pieces))
    edges = jnp.stack(
        [
            lax.axis_index(("lat", "comp")) * sea_rows - REACH,
            jnp.int32(lat_total),
            lax.axis_index("lon") * sea_cols - LEAD,
            jnp.int32(circle),
        ]
    ).astype(jnp.int32)
    kernels = jnp.broadcast_to(
        ocean_kernel.astype(jnp.float32).reshape(2, STENCIL_TAPS**2, 1, sea_width),
        (2, STENCIL_TAPS**2, 8, sea_width),
    )
    lanes = sea_width // LANES
    reached = (sea_rows + 2 * REACH, sea_cols + 2 * LEAD, sea_width)
    first = call(
        first_ocean_kernel,
        reached,
        edges,
        ocean_in,
        *pieces,
        kernels[0],
        ocean_gain[:1],
        ocean_up[0],
        ocean_down[0],
        scratch=[
            pltpu.VMEM((lanes, 3 * sea_rows, sea_cols + 2 * HALO, LANES), jnp.float32),
            pltpu.VMEM((lanes, 2, reached[1], LANES), jnp.float32),
        ],
        scalars=1,
    )
    gathered = lax.all_to_all(spectrum, LAT_LON, 0, 0, tiled=True)
    gathered, first = lax.optimization_barrier((gathered, first))
    filtered = call(
        filter_kernel,
        (lat_total, owned, width),
        weighted,
        turned,
        gathered.reshape(lat_total, owned, width),
        spec_real,
        spec_imag,
        degree_gain[:, None],
        scratch=[pltpu.VMEM((owned, lat_total, width), jnp.bfloat16)],
    )
    filtered, first = lax.optimization_barrier((filtered, first))
    current = call(
        second_ocean_kernel,
        (sea_rows, sea_cols, sea_width),
        first,
        kernels[1],
        ocean_gain[1:],
        ocean_up[1],
        ocean_down[1],
        scratch=[
            pltpu.VMEM((lanes, *reached[:2], LANES), jnp.float32),
            pltpu.VMEM((lanes, 2, sea_cols, LANES), jnp.float32),
        ],
    )
    returned = lax.all_to_all(
        filtered.reshape(owners, lats, owned, width), LAT_LON, 0, 0, tiled=True
    )
    returned, current = lax.optimization_barrier((returned, current))
    spatial = call(
        inverse_kernel,
        (lon_count, lats, lon_dev, width),
        inverse,
        returned,
        lax.ppermute(returned, "comp", swap),
    )
    spectral = lax.all_to_all(spatial, "lon", 0, 0, tiled=True).reshape(lat_dev, lon_dev, width)
    atm_out = by_rows(
        epilogue_kernel,
        atm_state,
        flux_here,
        spectral,
        (surface_to_atm, atm_gain[1:], atm_up, atm_down),
    )
    ocean_out = jnp.where(wet_mask[:, :, None] == 1, current, ocean_state)
    return (atm_out, ocean_out)


def solution(mesh):
    placed = (
        P("lat", LON_COMP, None),
        P(("lat", "comp"), LON, None),
        P(("lat", "comp"), LON),
        P(("lat", "lon", "comp"), None, None),
        P(),
        P(),
        P(),
        P(),
        P(),
        P(),
        P(),
        P(),
        P(),
        P(),
        P(),
        P(),
        P(),
        P(),
        P(),
    )
    return jax.shard_map(
        local,
        mesh=mesh,
        in_specs=placed,
        out_specs=(P("lat", LON_COMP, None), P(("lat", "comp"), LON, None)),
        check_vma=False,
    )
```

profile of v0, /device:TPU:1, one launch (start us, length us, event | category | flops | bytes accessed | tf_op | source)
XLA Modules:
  0.0 218.6 jit_solution(16091989523690199728)
XLA Ops:
  1.4 2.1 convolution_convert_fusion
  4.1 3.3 %collective-permute-start = (bf16[2,12,64,32]{2,3,1,0:T(8,128)(2,1)S(1)}, bf16[2,12,64,32]{2,3,1,0:T(8,128)(2,1)S(1)}, u32[]{:S(2)}, u32[]{:S(2)}) collective-permute-start(bf16[2,12,64,32]{2,3,1,0:T(8,128)(2,1)S(1)} %pad_maximum_fusion), channel_id=1, source_target_pairs={{0,1},{1,0},{2,3},{3,2},{4,5},{5,4},{6,7},{7,6},{8,9},{9,8},{10,11... | collective-permute-start | bytes 294920 | tf_op jit(solution)/shard_map/ppermute | solution.py:372
  8.9 2.2 %shard_map.212 = bf16[24,64,384]{2,1,0:T(8,128)(2,1)S(1)} custom-call(bf16[24,64,384]{2,1,0:T(8,128)(2,1)S(1)} %copy-done.1, bf16[1536,32]{1,0:T(8,128)(2,1)S(1)} %bitcast.50, bf16[32,384]{1,0:T(8,128)(2,1)S(1)} %copy-done.22, f32[1,384]{1,0:T(1,128)S(1)} %get-tuple-element.69.gain_ref), custom_call_target="tpu_custom_call" | custom-call | tf_op jit(solution)/shard_map/pallas_call | solution.py:186
  12.2 3.6 %all-to-all-start = ((bf16[8,3,64,384]{3,2,1,0:T(8,128)(2,1)}), bf16[8,3,64,384]{3,2,1,0:T(8,128)(2,1)S(1)}, u32[]{:S(2)}, u32[]{:S(2)}) async-start(bf16[8,3,64,384]{3,2,1,0:T(8,128)(2,1)} %bitcast.47), calls=%async_computation | async-start | bytes 2359296 | tf_op jit(solution)/shard_map/all_to_all | solution.py:383
  15.8 5.4 %collective-permute-start.1 = (bf16[12,128,256]{2,1,0:T(8,128)(2,1)S(1)}, bf16[12,128,256]{2,1,0:T(8,128)(2,1)S(1)}, u32[]{:S(2)}, u32[]{:S(2)}) collective-permute-start(bf16[12,128,256]{2,1,0:T(8,128)(2,1)S(1)} %add_convert_fusion.centre_ref), channel_id=1, source_target_pairs={{0,1},{2,3},{4,5},{6,7},{8,9},{10,11},{12,13},{14,15},{1,16},{3,18... | collective-permute-start | bytes 2359304 | tf_op jit(solution)/shard_map/ppermute | solution.py:315
  21.3 1.9 collective-permute-start.2
  23.2 3.7 %collective-permute-start.3 = (bf16[12,16,256]{2,1,0:T(8,128)(2,1)S(1)}, bf16[12,16,256]{2,1,0:T(8,128)(2,1)S(1)}, u32[]{:S(2)}, u32[]{:S(2)}) collective-permute-start(bf16[12,16,256]{2,1,0:T(8,128)(2,1)S(1)} %get-tuple-element.61), channel_id=1, source_target_pairs={{0,2},{2,4},{4,6},{6,8},{8,10},{10,12},{12,14},{1,3},{3,5},{5,7},{... | collective-permute-start | bytes 294920 | tf_op jit(solution)/shard_map/ppermute | solution.py:315
  28.2 6.9 %collective-permute-start.5 = (bf16[12,16,256]{2,1,0:T(8,128)(2,1)S(1)}, bf16[12,16,256]{2,1,0:T(8,128)(2,1)S(1)}, u32[]{:S(2)}, u32[]{:S(2)}) collective-permute-start(bf16[12,16,256]{2,1,0:T(8,128)(2,1)S(1)} %get-tuple-element.61), channel_id=1, source_target_pairs={{0,3},{2,5},{4,7},{6,9},{8,11},{10,13},{12,15},{1,18},{3,20},{5,22... | collective-permute-start | bytes 294920 | tf_op jit(solution)/shard_map/ppermute | solution.py:315
  37.7 4.3 %collective-permute-start.7 = (bf16[12,16,256]{2,1,0:T(8,128)(2,1)S(1)}, bf16[12,16,256]{2,1,0:T(8,128)(2,1)S(1)}, u32[]{:S(2)}, u32[]{:S(2)}) collective-permute-start(bf16[12,16,256]{2,1,0:T(8,128)(2,1)S(1)} %get-tuple-element.61), channel_id=1, source_target_pairs={{1,2},{3,4},{5,6},{7,8},{9,10},{11,12},{13,14},{16,3},{18,5},{20,7... | collective-permute-start | bytes 294920 | tf_op jit(solution)/shard_map/ppermute | solution.py:315
  42.0 6.3 %collective-permute-done.5.nw_ref = bf16[12,16,256]{2,1,0:T(8,128)(2,1)S(1)} collective-permute-done((bf16[12,16,256]{2,1,0:T(8,128)(2,1)S(1)}, bf16[12,16,256]{2,1,0:T(8,128)(2,1)S(1)}, u32[]{:S(2)}, u32[]{:S(2)}) %collective-permute-start.5) | collective-permute-done | bytes 98336 | tf_op jit(solution)/shard_map/ppermute | solution.py:315
  51.5 5.9 %collective-permute-done.8.se_ref = bf16[12,16,256]{2,1,0:T(8,128)(2,1)S(1)} collective-permute-done((bf16[12,16,256]{2,1,0:T(8,128)(2,1)S(1)}, bf16[12,16,256]{2,1,0:T(8,128)(2,1)S(1)}, u32[]{:S(2)}, u32[]{:S(2)}) %collective-permute-start.8) | collective-permute-done | bytes 98336 | tf_op jit(solution)/shard_map/ppermute | solution.py:315
  62.8 3.1 %shard_map.213 = bf16[128,3,4,384]{3,2,1,0:T(4,128)(2,1)S(1)} custom-call(bf16[512,1024]{1,0:T(8,128)(2,1)S(1)} %dynamic-slice_bitcast_fusion.table_ref, bf16[8,3,64,384]{3,2,1,0:T(8,128)(2,1)S(1)} %all-to-all-done.own_ref, bf16[8,3,64,384]{3,2,1,0:T(8,128)(2,1)} %collective-permute-done.9.other_ref), custom_call_target="tpu_custom_call" | custom-call | tf_op jit(solution)/shard_map/pallas_call | solution.py:132
  66.9 29.1 %all-to-all-start.1 = ((bf16[128,3,4,384]{3,2,1,0:T(4,128)(2,1)}), bf16[128,3,4,384]{3,2,1,0:T(4,128)(2,1)}, u32[]{:S(2)}, u32[]{:S(2)}) async-start(bf16[128,3,4,384]{3,2,1,0:T(4,128)(2,1)} %copy-done.2), calls=%async_computation.1 | async-start | bytes 2359296 | tf_op jit(solution)/shard_map/all_to_all | solution.py:438
  102.9 22.6 %shard_map.214.first_ref = bf16[24,144,256]{2,1,0:T(8,128)(2,1)S(1)} custom-call(s32[4]{0:T(128)S(1)} %pad_add_fusion.edges_ref, bf16[12,128,256]{2,1,0:T(8,128)(2,1)S(1)} %copy-done.6, bf16[12,128,256]{2,1,0:T(8,128)(2,1)S(1)} %copy-done.15, bf16[12,128,256]{2,1,0:T(8,128)(2,1)S(1)} %copy-done.17, bf16[12,16,256]{2,1,0:T(8,128)(2,1)S(1)} %copy-done.24, ...), custom_call_target="tpu_custom_call" | custom-call | tf_op jit(solution)/shard_map/pallas_call | solution.py:132
  131.2 5.3 %shard_map.215 = bf16[384,4,384]{2,1,0:T(4,128)(2,1)S(1)} custom-call(bf16[2,384,384]{2,1,0:T(8,128)(2,1)S(1)} %copy-done.11, bf16[2,384,384]{2,1,0:T(8,128)(2,1)S(1)} %bitcast.52, bf16[384,4,384]{2,1,0:T(4,128)(2,1)} %bitcast.16.spectrum_ref, bf16[384,384]{1,0:T(8,128)(2,1)S(1)} %copy-done.20, bf16[384,384]{1,0:T(8,128)(2,1)S(1)} %copy-done.21, ...), custom_call_target="tpu_custom_call" | custom-call | tf_op jit(solution)/shard_map/pallas_call | solution.py:132
  137.5 12.8 %all-to-all-start.2 = ((bf16[128,3,4,384]{3,2,1,0:T(4,128)(2,1)}), bf16[128,3,4,384]{3,2,1,0:T(4,128)(2,1)}, u32[]{:S(2)}, u32[]{:S(2)}) async-start(bf16[128,3,4,384]{3,2,1,0:T(4,128)(2,1)} %bitcast.48), calls=%async_computation.2 | async-start | bytes 2359296 | tf_op jit(solution)/shard_map/all_to_all | solution.py:465
  153.6 12.1 %shard_map.216 = bf16[12,128,256]{2,1,0:T(8,128)(2,1)S(1)} custom-call(bf16[24,144,256]{2,1,0:T(8,128)(2,1)S(1)} %shard_map.214.first_ref, f32[49,8,256]{2,1,0:T(8,128)S(1)} %broadcast_in_dim.29.kern_ref, f32[1,256]{1,0:T(1,128)S(1)} %get-tuple-element.70.gain_ref, bf16[256,1024]{1,0:T(8,128)(2,1)S(1)} %copy-done.12, ...), custom_call_target="tpu_custom_call" | custom-call | tf_op jit(solution)/shard_map/pallas_call | solution.py:132
  166.6 13.2 %all-to-all-done.2.own_ref = bf16[128,3,4,384]{3,2,1,0:T(4,128)(2,1)} async-done(((bf16[128,3,4,384]{3,2,1,0:T(4,128)(2,1)}), bf16[128,3,4,384]{3,2,1,0:T(4,128)(2,1)}, u32[]{:S(2)}, u32[]{:S(2)}) %all-to-all-start.2) | async-done | bytes 1179680 | tf_op jit(solution)/shard_map/all_to_all | solution.py:465
  179.8 3.9 %collective-permute-start.10 = (bf16[128,3,4,384]{3,2,1,0:T(4,128)(2,1)}, bf16[128,3,4,384]{3,2,1,0:T(4,128)(2,1)S(1)}, u32[]{:S(2)}, u32[]{:S(2)}) collective-permute-start(bf16[128,3,4,384]{3,2,1,0:T(4,128)(2,1)} %all-to-all-done.2.own_ref), channel_id=1, source_target_pairs={{0,1},{1,0},{2,3},{3,2},{4,5},{5,4},{6,7},{7,6},{8,9},{9,8},{10,11... | collective-permute-start | bytes 3538952 | tf_op jit(solution)/shard_map/ppermute | solution.py:474
  186.3 4.1 %shard_map.217 = bf16[8,3,64,384]{3,2,1,0:T(8,128)(2,1)} custom-call(bf16[512,1024]{1,0:T(8,128)(2,1)S(1)} %dynamic-slice_bitcast_fusion.1.table_ref, bf16[128,3,4,384]{3,2,1,0:T(4,128)(2,1)} %all-to-all-done.2.own_ref, bf16[128,3,4,384]{3,2,1,0:T(4,128)(2,1)S(1)} %collective-permute-done.10.other_ref), custom_call_target="tpu_custom_call" | custom-call | tf_op jit(solution)/shard_map/pallas_call | solution.py:132
  190.4 3.7 %all-to-all-start.3 = ((bf16[8,3,64,384]{3,2,1,0:T(8,128)(2,1)}), bf16[8,3,64,384]{3,2,1,0:T(8,128)(2,1)S(1)}, u32[]{:S(2)}, u32[]{:S(2)}) async-start(bf16[8,3,64,384]{3,2,1,0:T(8,128)(2,1)} %shard_map.217), calls=%async_computation.3 | async-start | bytes 2359296 | tf_op jit(solution)/shard_map/all_to_all | solution.py:476
  194.2 2.6 %broadcast_select_fusion = bf16[12,128,256]{2,1,0:T(8,128)(2,1)} fusion(bf16[12,128,256]{2,1,0:T(8,128)(2,1)} %copy-done.9, bf16[12,128,256]{2,1,0:T(8,128)(2,1)} %param.22, pred[12,128]{1,0:T(8,128)(4,1)S(1)} %broadcast_compare_fusion), kind=kLoop, calls=%fused_computation.7 | loop fusion | flops 393216 | bytes 2360832 | tf_op jit(solution)/shard_map/jit(_where)/select_n | solution.py:484
  196.8 13.7 %all-to-all-done.3 = bf16[8,3,64,384]{3,2,1,0:T(8,128)(2,1)S(1)} async-done(((bf16[8,3,64,384]{3,2,1,0:T(8,128)(2,1)}), bf16[8,3,64,384]{3,2,1,0:T(8,128)(2,1)S(1)}, u32[]{:S(2)}, u32[]{:S(2)}) %all-to-all-start.3) | async-done | bytes 1179680 | tf_op jit(solution)/shard_map/all_to_all | solution.py:476
  211.5 7.1 %shard_map.218 = bf16[24,64,384]{2,1,0:T(8,128)(2,1)} custom-call(bf16[24,64,384]{2,1,0:T(8,128)(2,1)S(1)} %copy-done.1, bf16[1536,32]{1,0:T(8,128)(2,1)S(1)} %bitcast.51, bf16[24,64,384]{2,1,0:T(8,128)(2,1)S(1)} %bitcast.49, bf16[32,384]{1,0:T(8,128)(2,1)S(1)} %copy-done.22, f32[1,384]{1,0:T(1,128)S(1)} %get-tuple-element.68.gain_ref, ...), custom_call_target="tpu_custom_call" | custom-call | tf_op jit(solution)/shard_map/pallas_call | solution.py:186
  (138 shorter events, 38.5 us)
Async XLA Ops:
  3.6 3.9 %copy-start.44 = (f32[2,384]{1,0:T(2,128)S(1)}, f32[2,384]{1,0:T(2,128)}, u32[]{:S(2)}) copy-start(f32[2,384]{1,0:T(2,128)} %param.29) | copy-start | bytes 9220
  4.0 4.9 %copy-start.1 = (bf16[24,64,384]{2,1,0:T(8,128)(2,1)S(1)}, bf16[24,64,384]{2,1,0:T(8,128)(2,1)}, u32[]{:S(2)}) copy-start(bf16[24,64,384]{2,1,0:T(8,128)(2,1)} %atm_ref.3) | copy-start | bytes 3538948
  4.0 4.9 %copy-start.22 = (bf16[32,384]{1,0:T(8,128)(2,1)S(1)}, bf16[32,384]{1,0:T(8,128)(2,1)}, u32[]{:S(2)}) copy-start(bf16[32,384]{1,0:T(8,128)(2,1)} %out_weight_ref.3) | copy-start | bytes 73732
  4.1 4.4 %collective-permute-start = (bf16[2,12,64,32]{2,3,1,0:T(8,128)(2,1)S(1)}, bf16[2,12,64,32]{2,3,1,0:T(8,128)(2,1)S(1)}, u32[]{:S(2)}, u32[]{:S(2)}) collective-permute-start(bf16[2,12,64,32]{2,3,1,0:T(8,128)(2,1)S(1)} %pad_maximum_fusion), channel_id=1, source_target_pairs={{0,1},{1,0},{2,3},{3,2},{4,5},{5,4},{6,7},{7,6},{8,9},{9,8},{10,11... | collective-permute-start | bytes 294920 | tf_op jit(solution)/shard_map/ppermute | solution.py:372
  12.2 11.0 %copy-start.5 = (bf16[12,128,256]{2,1,0:T(8,128)(2,1)}, bf16[12,128,256]{2,1,0:T(8,128)(2,1)S(1)}, u32[]{:S(2)}) copy-start(bf16[12,128,256]{2,1,0:T(8,128)(2,1)S(1)} %add_convert_fusion.centre_ref) | copy-start | bytes 2359300
  12.2 47.6 %all-to-all-start = ((bf16[8,3,64,384]{3,2,1,0:T(8,128)(2,1)}), bf16[8,3,64,384]{3,2,1,0:T(8,128)(2,1)S(1)}, u32[]{:S(2)}, u32[]{:S(2)}) async-start(bf16[8,3,64,384]{3,2,1,0:T(8,128)(2,1)} %bitcast.47), calls=%async_computation | async-start | bytes 2359296 | tf_op jit(solution)/shard_map/all_to_all | solution.py:383
  15.8 42.2 %collective-permute-start.1 = (bf16[12,128,256]{2,1,0:T(8,128)(2,1)S(1)}, bf16[12,128,256]{2,1,0:T(8,128)(2,1)S(1)}, u32[]{:S(2)}, u32[]{:S(2)}) collective-permute-start(bf16[12,128,256]{2,1,0:T(8,128)(2,1)S(1)} %add_convert_fusion.centre_ref), channel_id=1, source_target_pairs={{0,1},{2,3},{4,5},{6,7},{8,9},{10,11},{12,13},{14,15},{1,16},{3,18... | collective-permute-start | bytes 2359304 | tf_op jit(solution)/shard_map/ppermute | solution.py:315
  21.3 37.6 %collective-permute-start.2 = (bf16[12,128,256]{2,1,0:T(8,128)(2,1)S(1)}, bf16[12,128,256]{2,1,0:T(8,128)(2,1)S(1)}, u32[]{:S(2)}, u32[]{:S(2)}) collective-permute-start(bf16[12,128,256]{2,1,0:T(8,128)(2,1)S(1)} %add_convert_fusion.centre_ref), channel_id=1, source_target_pairs={{1,0},{3,2},{5,4},{7,6},{9,8},{11,10},{13,12},{15,14},{16,1},{18,3... | collective-permute-start | bytes 2359304 | tf_op jit(solution)/shard_map/ppermute | solution.py:315
  23.2 11.9 %collective-permute-start.3 = (bf16[12,16,256]{2,1,0:T(8,128)(2,1)S(1)}, bf16[12,16,256]{2,1,0:T(8,128)(2,1)S(1)}, u32[]{:S(2)}, u32[]{:S(2)}) collective-permute-start(bf16[12,16,256]{2,1,0:T(8,128)(2,1)S(1)} %get-tuple-element.61), channel_id=1, source_target_pairs={{0,2},{2,4},{4,6},{6,8},{8,10},{10,12},{12,14},{1,3},{3,5},{5,7},{... | collective-permute-start | bytes 294920 | tf_op jit(solution)/shard_map/ppermute | solution.py:315
  26.9 10.1 %collective-permute-start.4 = (bf16[12,16,256]{2,1,0:T(8,128)(2,1)S(1)}, bf16[12,16,256]{2,1,0:T(8,128)(2,1)S(1)}, u32[]{:S(2)}, u32[]{:S(2)}) collective-permute-start(bf16[12,16,256]{2,1,0:T(8,128)(2,1)S(1)} %get-tuple-element.60), channel_id=1, source_target_pairs={{2,0},{4,2},{6,4},{8,6},{10,8},{12,10},{14,12},{3,1},{5,3},{7,5},{... | collective-permute-start | bytes 294920 | tf_op jit(solution)/shard_map/ppermute | solution.py:315
  28.2 20.1 %collective-permute-start.5 = (bf16[12,16,256]{2,1,0:T(8,128)(2,1)S(1)}, bf16[12,16,256]{2,1,0:T(8,128)(2,1)S(1)}, u32[]{:S(2)}, u32[]{:S(2)}) collective-permute-start(bf16[12,16,256]{2,1,0:T(8,128)(2,1)S(1)} %get-tuple-element.61), channel_id=1, source_target_pairs={{0,3},{2,5},{4,7},{6,9},{8,11},{10,13},{12,15},{1,18},{3,20},{5,22... | collective-permute-start | bytes 294920 | tf_op jit(solution)/shard_map/ppermute | solution.py:315
  35.8 14.4 %collective-permute-start.6 = (bf16[12,16,256]{2,1,0:T(8,128)(2,1)S(1)}, bf16[12,16,256]{2,1,0:T(8,128)(2,1)S(1)}, u32[]{:S(2)}, u32[]{:S(2)}) collective-permute-start(bf16[12,16,256]{2,1,0:T(8,128)(2,1)S(1)} %get-tuple-element.60), channel_id=1, source_target_pairs={{2,1},{4,3},{6,5},{8,7},{10,9},{12,11},{14,13},{3,16},{5,18},{7,20... | collective-permute-start | bytes 294920 | tf_op jit(solution)/shard_map/ppermute | solution.py:315
  37.7 13.1 %collective-permute-start.7 = (bf16[12,16,256]{2,1,0:T(8,128)(2,1)S(1)}, bf16[12,16,256]{2,1,0:T(8,128)(2,1)S(1)}, u32[]{:S(2)}, u32[]{:S(2)}) collective-permute-start(bf16[12,16,256]{2,1,0:T(8,128)(2,1)S(1)} %get-tuple-element.61), channel_id=1, source_target_pairs={{1,2},{3,4},{5,6},{7,8},{9,10},{11,12},{13,14},{16,3},{18,5},{20,7... | collective-permute-start | bytes 294920 | tf_op jit(solution)/shard_map/ppermute | solution.py:315
  48.9 8.5 %collective-permute-start.8 = (bf16[12,16,256]{2,1,0:T(8,128)(2,1)S(1)}, bf16[12,16,256]{2,1,0:T(8,128)(2,1)S(1)}, u32[]{:S(2)}, u32[]{:S(2)}) collective-permute-start(bf16[12,16,256]{2,1,0:T(8,128)(2,1)S(1)} %get-tuple-element.60), channel_id=1, source_target_pairs={{3,0},{5,2},{7,4},{9,6},{11,8},{13,10},{15,12},{18,1},{20,3},{22,5... | collective-permute-start | bytes 294920 | tf_op jit(solution)/shard_map/ppermute | solution.py:315
  59.8 3.0 %collective-permute-start.9 = (bf16[8,3,64,384]{3,2,1,0:T(8,128)(2,1)S(1)}, bf16[8,3,64,384]{3,2,1,0:T(8,128)(2,1)}, u32[]{:S(2)}, u32[]{:S(2)}) collective-permute-start(bf16[8,3,64,384]{3,2,1,0:T(8,128)(2,1)S(1)} %all-to-all-done.own_ref), channel_id=1, source_target_pairs={{0,1},{1,0},{2,3},{3,2},{4,5},{5,4},{6,7},{7,6},{8,9},{9,8},{10,11... | collective-permute-start | bytes 3538952 | tf_op jit(solution)/shard_map/ppermute | solution.py:405
  66.9 29.2 %copy-start.40 = (bf16[2,7,7,256]{3,0,2,1:T(2,128)(2,1)S(1)}, bf16[2,7,7,256]{3,0,2,1:T(2,128)(2,1)}, u32[]{:S(2)}) copy-start(bf16[2,7,7,256]{3,0,2,1:T(2,128)(2,1)} %param.36) | copy-start | bytes 150532
  66.9 30.0 %copy-start.37 = (bf16[2,384,384]{2,1,0:T(8,128)(2,1)S(1)}, bf16[2,384,384]{2,1,0:T(8,128)(2,1)}, u32[]{:S(2)}) copy-start(bf16[2,384,384]{2,1,0:T(8,128)(2,1)} %param.24) | copy-start | bytes 1769476
  66.9 59.3 %all-to-all-start.1 = ((bf16[128,3,4,384]{3,2,1,0:T(4,128)(2,1)}), bf16[128,3,4,384]{3,2,1,0:T(4,128)(2,1)}, u32[]{:S(2)}, u32[]{:S(2)}) async-start(bf16[128,3,4,384]{3,2,1,0:T(4,128)(2,1)} %copy-done.2), calls=%async_computation.1 | async-start | bytes 2359296 | tf_op jit(solution)/shard_map/all_to_all | solution.py:438
  137.5 42.3 %all-to-all-start.2 = ((bf16[128,3,4,384]{3,2,1,0:T(4,128)(2,1)}), bf16[128,3,4,384]{3,2,1,0:T(4,128)(2,1)}, u32[]{:S(2)}, u32[]{:S(2)}) async-start(bf16[128,3,4,384]{3,2,1,0:T(4,128)(2,1)} %bitcast.48), calls=%async_computation.2 | async-start | bytes 2359296 | tf_op jit(solution)/shard_map/all_to_all | solution.py:465
  179.8 6.5 %collective-permute-start.10 = (bf16[128,3,4,384]{3,2,1,0:T(4,128)(2,1)}, bf16[128,3,4,384]{3,2,1,0:T(4,128)(2,1)S(1)}, u32[]{:S(2)}, u32[]{:S(2)}) collective-permute-start(bf16[128,3,4,384]{3,2,1,0:T(4,128)(2,1)} %all-to-all-done.2.own_ref), channel_id=1, source_target_pairs={{0,1},{1,0},{2,3},{3,2},{4,5},{5,4},{6,7},{7,6},{8,9},{9,8},{10,11... | collective-permute-start | bytes 3538952 | tf_op jit(solution)/shard_map/ppermute | solution.py:474
  190.4 3.7 %copy-start.41 = (s32[12,128]{1,0:T(8,128)S(1)}, s32[12,128]{1,0:T(8,128)}, u32[]{:S(2)}) copy-start(s32[12,128]{1,0:T(8,128)} %param.23) | copy-start | bytes 18436
  190.4 20.0 %all-to-all-start.3 = ((bf16[8,3,64,384]{3,2,1,0:T(8,128)(2,1)}), bf16[8,3,64,384]{3,2,1,0:T(8,128)(2,1)S(1)}, u32[]{:S(2)}, u32[]{:S(2)}) async-start(bf16[8,3,64,384]{3,2,1,0:T(8,128)(2,1)} %shard_map.217), calls=%async_computation.3 | async-start | bytes 2359296 | tf_op jit(solution)/shard_map/all_to_all | solution.py:476
  194.1 16.3 %copy-start.8 = (bf16[24,64,32]{2,1,0:T(8,128)(2,1)S(1)}, bf16[24,64,32]{2,1,0:T(8,128)(2,1)}, u32[]{:S(2)}) copy-start(bf16[24,64,32]{2,1,0:T(8,128)(2,1)} %copy-done.7) | copy-start | bytes 294916
  194.2 16.3 %copy-start.18 = (bf16[384,768]{1,0:T(8,128)(2,1)S(1)}, bf16[384,768]{1,0:T(8,128)(2,1)}, u32[]{:S(2)}) copy-start(bf16[384,768]{1,0:T(8,128)(2,1)} %up_ref.1) | copy-start | bytes 1769476
  (39 other events, 58.9 us)
where the time goes:
time: 220 us; the launch traced here: 219 us
  starting transfers between devices  82.5 us (38%)
  Pallas kernels  56.4 us (26%)
  waiting for transfers between devices  43.8 us (20%)
  local copies, waits for them, and re-layouts  26.9 us (12%)
  other arithmetic  4.72 us (2%)
  matrix products  2.95 us (1%)
    pallas_call x5, Pallas kernels, call(): pl.pallas_call(kernel, out_shape=jax.ShapeDtypeStruct(shape, jnp.bfloat16...  47.1 us
    all_to_all x1, starting transfers between devices, local(): gathered = lax.all_to_all(spectrum, LAT_LON, 0, 0, tiled=True)  29.1 us
    ppermute x8, starting transfers between devices, shifted(): return lax.ppermute(block, axes, pairs)  26 us
    unnamed x97, local copies, waits for them, and re-layouts  19.2 us
    all_to_all x1, waiting for transfers between devices, local(): lax.all_to_all(spatial, 'lon', 0, 0, tiled=True)  13.7 us
    all_to_all x1, waiting for transfers between devices, local(): lax.all_to_all(filtered.reshape(owners, lats, owned, width), LAT_LON, 0,...  13.2 us
    all_to_all x1, starting transfers between devices, local(): lax.all_to_all(filtered.reshape(owners, lats, owned, width), LAT_LON, 0,...  12.8 us
    ppermute x8, waiting for transfers between devices, shifted(): return lax.ppermute(block, axes, pairs)  12.2 us
  transfers between devices with their start and end apart: 15, of which 8 were waited for; matrix products, arithmetic and copies ran while one was open for 6% of the time, Pallas kernels for 16%

commit v1 on v0

--- a/solution.py
+++ b/solution.py
@@ -48,94 +48,166 @@
     )
 
 
-def forward_kernel(table_ref, own_ref, other_ref, out_ref):
-    groups, lats, span, width = own_ref.shape
-    half = groups * span
+def waves_kernel(
+    table_hbm, own_hbm, other_hbm, out_hbm, table_ref, own_ref, other_ref, held, sems
+):
+    lats, width = own_ref.shape[0], own_ref.shape[3]
+    half = table_ref.shape[1] // 2
+    table = pltpu.make_async_copy(table_hbm, table_ref, sems.at[0])
+    table.start()
+    owns, others, sends = [], [], []
     for i in range(lats):
+        owns.append(pltpu.make_async_copy(own_hbm.at[:, i], own_ref.at[i], sems.at[1 + i]))
+        owns[-1].start()
+        at = sems.at[1 + lats + i]
+        others.append(pltpu.make_async_copy(other_hbm.at[:, i], other_ref.at[i], at))
+        others[-1].start()
+    table.wait()
+    for i in range(lats):
+        owns[i].wait()
         total = jnp.dot(
             table_ref[:, :half],
-            own_ref[:, i].reshape(half, width),
+            own_ref[i].reshape(half, width),
             preferred_element_type=jnp.float32,
-        ) + jnp.dot(
+        )
+        others[i].wait()
+        total += jnp.dot(
             table_ref[:, half:],
-            other_ref[:, i].reshape(half, width),
+            other_ref[i].reshape(half, width),
             preferred_element_type=jnp.float32,
         )
-        out_ref[:, i] = total.astype(jnp.bfloat16).reshape(
-            out_ref.shape[0], out_ref.shape[2], width
-        )
-
-
-def inverse_kernel(table_ref, own_ref, other_ref, out_ref):
-    owners, lats, owned, width = own_ref.shape
-    half = owners * owned
-    for i in range(lats):
-        total = jnp.dot(
-            table_ref[:, :half],
-            own_ref[:, i].reshape(half, width),
-            preferred_element_type=jnp.float32,
-        ) + jnp.dot(
-            table_ref[:, half:],
-            other_ref[:, i].reshape(half, width),
-            preferred_element_type=jnp.float32,
-        )
-        out_ref[:, i] = total.astype(jnp.bfloat16).reshape(
-            out_ref.shape[0], out_ref.shape[2], width
-        )
+        held[i] = total.astype(jnp.bfloat16).reshape(held.shape[1:])
+        at = sems.at[1 + 2 * lats + i]
+        sends.append(pltpu.make_async_copy(held.at[i], out_hbm.at[:, i], at))
+        sends[-1].start()
+    for send in sends:
+        send.wait()
+
+
+def waves(shape, table, own, other):
+    lats = shape[1]
+    return call(
+        waves_kernel,
+        shape,
+        table,
+        own,
+        other,
+        scratch=[
+            pltpu.VMEM(table.shape, jnp.bfloat16),
+            pltpu.VMEM((lats, own.shape[0], *own.shape[2:]), jnp.bfloat16),
+            pltpu.VMEM((lats, own.shape[0], *own.shape[2:]), jnp.bfloat16),
+            pltpu.VMEM((lats, shape[0], *shape[2:]), jnp.bfloat16),
+            pltpu.SemaphoreType.DMA((1 + 3 * lats,)),
+        ],
+        behind=3,
+        away=True,
+        room=1_300_000,
+    )
 
 
 def filter_kernel(
-    weighted_ref, turned_ref, spectrum_ref, real_ref, imag_ref, gain_ref, out_ref, rows_ref
+    gain_ref,
+    spectrum_hbm,
+    weighted_hbm,
+    turned_hbm,
+    real_hbm,
+    imag_hbm,
+    out_hbm,
+    spectrum_ref,
+    weighted_ref,
+    turned_ref,
+    real_ref,
+    imag_ref,
+    rows_ref,
+    held,
+    sems,
 ):
     count = weighted_ref.shape[0]
     lats, owned, width = spectrum_ref.shape
     block = 64
     side = block * owned
+    parts = lats // block
+    pairs = (
+        (weighted_hbm, weighted_ref),
+        (real_hbm, real_ref),
+        (imag_hbm, imag_ref),
+        (turned_hbm, turned_ref),
+    )
+    fetches = [
+        pltpu.make_async_copy(source, target, sems.at[n])
+        for n, (source, target) in enumerate(pairs)
+    ]
+    arrivals = []
+    for b in range(parts):
+        span = pl.ds(b * block, block)
+        at = sems.at[len(pairs) + b]
+        arrivals.append(pltpu.make_async_copy(spectrum_hbm.at[span], spectrum_ref.at[span], at))
+        arrivals[-1].start()
+    for fetch in fetches:
+        fetch.start()
     r = lax.broadcasted_iota(jnp.int32, (side, side), 0)
     s = lax.broadcasted_iota(jnp.int32, (side, side), 1)
     pick = jnp.where((r % block) * owned + r // block == s, 1.0, 0.0).astype(jnp.bfloat16)
     back = jnp.where((s % block) * owned + s // block == r, 1.0, 0.0).astype(jnp.bfloat16)
-    for b in range(lats // block):
+    for b in range(parts):
+        arrivals[b].wait()
         piece = spectrum_ref[b * block : (b + 1) * block].reshape(side, width)
         moved = jnp.dot(pick, piece, preferred_element_type=jnp.float32).astype(jnp.bfloat16)
         for p in range(owned):
             rows_ref[p, b * block : (b + 1) * block] = moved[p * block : (p + 1) * block]
-    real, imag, gain = real_ref[...], imag_ref[...], gain_ref[...]
+    gain = jnp.transpose(jnp.broadcast_to(gain_ref[...], (8, lats)))[:, :1]
+    for fetch in fetches:
+        fetch.wait()
+    real, imag = real_ref[...], imag_ref[...]
     for m in range(count):
-        parts = [
+        coeffs = [
             jnp.dot(
                 weighted_ref[m], rows_ref[2 * m + q], preferred_element_type=jnp.float32
             ).astype(jnp.bfloat16)
             for q in range(2)
         ]
-        mixed_real = jnp.dot(parts[0], real, preferred_element_type=jnp.float32) - jnp.dot(
-            parts[1], imag, preferred_element_type=jnp.float32
-        )
-        mixed_imag = jnp.dot(parts[0], imag, preferred_element_type=jnp.float32) + jnp.dot(
-            parts[1], real, preferred_element_type=jnp.float32
+        mixed_real = jnp.dot(coeffs[0], real, preferred_element_type=jnp.float32) - jnp.dot(
+            coeffs[1], imag, preferred_element_type=jnp.float32
+        )
+        mixed_imag = jnp.dot(coeffs[0], imag, preferred_element_type=jnp.float32) + jnp.dot(
+            coeffs[1], real, preferred_element_type=jnp.float32
         )
         for q, mixed in enumerate((mixed_real, mixed_imag)):
             filtered = (mixed * gain).astype(jnp.bfloat16)
             rows_ref[2 * m + q] = jnp.dot(
                 turned_ref[m], filtered, preferred_element_type=jnp.float32
             ).astype(jnp.bfloat16)
-    for b in range(lats // block):
+    sends = []
+    for b in range(parts):
         piece = jnp.concatenate(
             [rows_ref[p, b * block : (b + 1) * block] for p in range(owned)], axis=0
         )
         moved = jnp.dot(back, piece, preferred_element_type=jnp.float32).astype(jnp.bfloat16)
-        out_ref[b * block : (b + 1) * block] = moved.reshape(block, owned, width)
-
-
-def call(kernel, shape, *args, scratch=(), limit=16, scalars=0):
-    spaces = [pltpu.SMEM] * scalars + [pltpu.VMEM] * (len(args) - scalars)
+        span = pl.ds(b * block, block)
+        held[span] = moved.reshape(block, owned, width)
+        sends.append(
+            pltpu.make_async_copy(
+                held.at[span], out_hbm.at[span], sems.at[len(pairs) + parts + b]
+            )
+        )
+        sends[-1].start()
+    for send in sends:
+        send.wait()
+
+
+VMEM = 62_900_000
+
+
+def call(kernel, shape, *args, scratch=(), room=0, scalars=0, behind=0, away=False):
+    spaces = [pltpu.SMEM] * scalars + [pltpu.VMEM] * (len(args) - scalars - behind)
+    spaces += [pltpu.HBM] * behind
     return pl.pallas_call(
         kernel,
         out_shape=jax.ShapeDtypeStruct(shape, jnp.bfloat16),
         in_specs=[pl.BlockSpec(memory_space=space) for space in spaces],
-        out_specs=pl.BlockSpec(memory_space=pltpu.VMEM),
+        out_specs=pl.BlockSpec(memory_space=pltpu.HBM if away else pltpu.VMEM),
         scratch_shapes=list(scratch),
-        compiler_params=pltpu.CompilerParams(vmem_limit_bytes=limit * 2**20),
+        compiler_params=pltpu.CompilerParams(vmem_limit_bytes=VMEM - room),
     )(*args)
 
 
@@ -189,7 +261,7 @@
         out_shape=jax.ShapeDtypeStruct(atm.shape, jnp.bfloat16),
         in_specs=specs,
         out_specs=field,
-        compiler_params=pltpu.CompilerParams(vmem_limit_bytes=16 * 2**20),
+        compiler_params=pltpu.CompilerParams(vmem_limit_bytes=VMEM - 100_000),
     )(*fields, *weights)
 
 
@@ -259,12 +331,6 @@
     centre_ref,
     north_ref,
     south_ref,
-    west_ref,
-    east_ref,
-    nw_ref,
-    ne_ref,
-    sw_ref,
-    se_ref,
     kern_ref,
     gain_ref,
     up_ref,
@@ -274,18 +340,11 @@
     sums,
 ):
     rows, cols, width = centre_ref.shape
-    columns = (slice(0, HALO), slice(HALO, HALO + cols), slice(HALO + cols, cols + 2 * HALO))
-    grid = (
-        (nw_ref, north_ref, ne_ref),
-        (west_ref, centre_ref, east_ref),
-        (sw_ref, south_ref, se_ref),
-    )
-    for y, line in enumerate(grid):
-        for x, ref in enumerate(line):
-            for lane in range(width // LANES):
-                field[lane, y * rows : (y + 1) * rows, columns[x], :] = ref[
-                    :, :, lane * LANES : (lane + 1) * LANES
-                ].astype(jnp.float32)
+    for y, ref in enumerate((north_ref, centre_ref, south_ref)):
+        for lane in range(width // LANES):
+            field[lane, y * rows : (y + 1) * rows] = ref[
+                :, :, lane * LANES : (lane + 1) * LANES
+            ].astype(jnp.float32)
     edges = [edges_ref[n] for n in range(4)]
     ocean_rows(field, kern_ref, gain_ref, up_ref, down_ref, sums, out_ref, sums.shape[1], edges)
 
@@ -369,42 +428,59 @@
 
     kept_ocean, sent_ocean = halves(ocean_flux, 1)
     kept_atm, sent_atm = halves(atm_flux, 0)
-    got = lax.ppermute(jnp.stack([sent_ocean, sent_atm]), "comp", swap)
-    flux_here = together(kept_ocean, got[0], 0).reshape(lat_dev * lon_dev, -1)
-    flux_sea = together(kept_atm, got[1], 1)
+    got_ocean = lax.ppermute(sent_ocean, "comp", swap)
+    flux_here = together(kept_ocean, got_ocean, 0).reshape(lat_dev * lon_dev, -1)
     normed = by_rows(
         prologue_kernel, atm_state, flux_here, None, (surface_to_atm, atm_gain[:1])
     )
+    rings = lax.all_to_all(
+        normed.reshape(lon_count, lats, lon_dev, width), "lon", 0, 0, tiled=True
+    )
+    flux_sea = together(kept_atm, lax.ppermute(sent_atm, "comp", swap), 1)
     ocean_in = (
         ocean_state.astype(jnp.float32)
         + wet * jnp.dot(flux_sea, surface_to_ocean, preferred_element_type=jnp.float32)
     ).astype(jnp.bfloat16)
-    normed, ocean_in = lax.optimization_barrier((normed, ocean_in))
-    rings = lax.all_to_all(
-        normed.reshape(lon_count, lats, lon_dev, width), "lon", 0, 0, tiled=True
-    )
-    west, east = ocean_in[:, -HALO:], ocean_in[:, :HALO]
-    pieces = (
-        shifted(ocean_in, 1, 0),
-        shifted(ocean_in, -1, 0),
-        shifted(west, 0, 1),
-        shifted(east, 0, -1),
-        shifted(west, 1, 1),
-        shifted(east, 1, -1),
-        shifted(west, -1, 1),
-        shifted(east, -1, -1),
-    )
-    rings, pieces = lax.optimization_barrier((rings, pieces))
+    west = shifted(ocean_in[:, -HALO:], 0, 1)
+    east = shifted(ocean_in[:, :HALO], 0, -1)
+    broad = jnp.concatenate([west, ocean_in, east], axis=1)
+    rings, broad = lax.optimization_barrier((rings, broad))
     weighted = (legendre.astype(jnp.float32) * (quad_weight / lat_total)).astype(jnp.bfloat16)
     turned = jnp.swapaxes(legendre, 1, 2)
-    spectrum = call(
-        forward_kernel,
-        (owners, lats, owned, width),
-        forward,
-        rings,
-        lax.ppermute(rings, "comp", swap),
-    )
-    spectrum, pieces = lax.optimization_barrier((spectrum, pieces))
+    spectrum = waves(
+        (owners, lats, owned, width), forward, rings, lax.ppermute(rings, "comp", swap)
+    )
+    spectrum, broad = lax.optimization_barrier((spectrum, broad))
+    gathered = lax.all_to_all(spectrum, LAT_LON, 0, 0, tiled=True)
+    north = shifted(broad, 1, 0)
+    south = shifted(broad, -1, 0)
+    filtered = call(
+        filter_kernel,
+        (lat_total, owned, width),
+        degree_gain[None],
+        gathered.reshape(lat_total, owned, width),
+        weighted,
+        turned,
+        spec_real,
+        spec_imag,
+        scratch=[
+            pltpu.VMEM((lat_total, owned, width), jnp.bfloat16),
+            pltpu.VMEM(weighted.shape, jnp.bfloat16),
+            pltpu.VMEM(turned.shape, jnp.bfloat16),
+            pltpu.VMEM(spec_real.shape, jnp.bfloat16),
+            pltpu.VMEM(spec_imag.shape, jnp.bfloat16),
+            pltpu.VMEM((owned, lat_total, width), jnp.bfloat16),
+            pltpu.VMEM((lat_total, owned, width), jnp.bfloat16),
+            pltpu.SemaphoreType.DMA((4 + lat_total // 64 * 2,)),
+        ],
+        behind=5,
+        away=True,
+        room=100_000,
+    )
+    filtered, north, south = lax.optimization_barrier((filtered, north, south))
+    returned = lax.all_to_all(
+        filtered.reshape(owners, lats, owned, width), LAT_LON, 0, 0, tiled=True
+    )
     edges = jnp.stack(
         [
             lax.axis_index(("lat", "comp")) * sea_rows - REACH,
@@ -423,8 +499,9 @@
         first_ocean_kernel,
         reached,
         edges,
-        ocean_in,
-        *pieces,
+        broad,
+        north,
+        south,
         kernels[0],
         ocean_gain[:1],
         ocean_up[0],
@@ -435,20 +512,12 @@
         ],
         scalars=1,
     )
-    gathered = lax.all_to_all(spectrum, LAT_LON, 0, 0, tiled=True)
-    gathered, first = lax.optimization_barrier((gathered, first))
-    filtered = call(
-        filter_kernel,
-        (lat_total, owned, width),
-        weighted,
-        turned,
-        gathered.reshape(lat_total, owned, width),
-        spec_real,
-        spec_imag,
-        degree_gain[:, None],
-        scratch=[pltpu.VMEM((owned, lat_total, width), jnp.bfloat16)],
-    )
-    filtered, first = lax.optimization_barrier((filtered, first))
+    returned, first = lax.optimization_barrier((returned, first))
+    spatial = waves(
+        (lon_count, lats, lon_dev, width), inverse, returned, lax.ppermute(returned, "comp", swap)
+    )
+    spatial, first = lax.optimization_barrier((spatial, first))
+    spectral = lax.all_to_all(spatial, "lon", 0, 0, tiled=True).reshape(lat_dev, lon_dev, width)
     current = call(
         second_ocean_kernel,
         (sea_rows, sea_cols, sea_width),
@@ -462,18 +531,8 @@
             pltpu.VMEM((lanes, 2, sea_cols, LANES), jnp.float32),
         ],
     )
-    returned = lax.all_to_all(
-        filtered.reshape(owners, lats, owned, width), LAT_LON, 0, 0, tiled=True
-    )
-    returned, current = lax.optimization_barrier((returned, current))
-    spatial = call(
-        inverse_kernel,
-        (lon_count, lats, lon_dev, width),
-        inverse,
-        returned,
-        lax.ppermute(returned, "comp", swap),
-    )
-    spectral = lax.all_to_all(spatial, "lon", 0, 0, tiled=True).reshape(lat_dev, lon_dev, width)
+    ocean_out = jnp.where(wet_mask[:, :, None] == 1, current, ocean_state)
+    spectral, ocean_out = lax.optimization_barrier((spectral, ocean_out))
     atm_out = by_rows(
         epilogue_kernel,
         atm_state,
@@ -481,7 +540,6 @@
         spectral,
         (surface_to_atm, atm_gain[1:], atm_up, atm_down),
     )
-    ocean_out = jnp.where(wet_mask[:, :, None] == 1, current, ocean_state)
     return (atm_out, ocean_out)
 
 

time: 220 us -> 192 us (0.87)
  starting transfers between devices: 82.5 us -> 54.7 us
  Pallas kernels: 56.4 us -> 70.5 us
  local copies, waits for them, and re-layouts: 26.9 us -> 16.5 us
  waiting for transfers between devices: 43.8 us -> 39.4 us
    all_to_all x1, waiting for transfers between devices: 0.66 us -> 19.5 us  [local(): gathered = lax.all_to_all(spectrum, LAT_LON, 0, 0, tiled=True)]
    ppermute x8 -> x4, starting transfers between devices: 26 us -> 11.2 us  [shifted(): return lax.ppermute(block, axes, pairs)]
    all_to_all x1, starting transfers between devices: 29.1 us -> 14.4 us  [local(): gathered = lax.all_to_all(spectrum, LAT_LON, 0, 0, tiled=True)]
    unnamed x97 -> x37, local copies, waits for them, and re-layouts: 19.2 us -> 5.32 us
    all_to_all x1, waiting for transfers between devices: 13.7 us -> 0.01 us  [local(): lax.all_to_all(spatial, 'lon', 0, 0, tiled=True)]
    all_to_all x1, waiting for transfers between devices: 13.2 us -> 0.24 us  [local(): lax.all_to_all(filtered.reshape(owners, lats, owned, width), LAT_LON, 0,...]
    pallas_call x5, Pallas kernels: 47.1 us -> 56.4 us  [call(): pl.pallas_call(kernel, out_shape=jax.ShapeDtypeStruct(shape, jnp.bfloat16...]
    ppermute x8 -> x4, waiting for transfers between devices: 12.2 us -> 17.7 us  [shifted(): return lax.ppermute(block, axes, pairs)]
  transfers between devices with their start and end apart: 15 -> 12, of which waited for: 8 -> 10; matrix products, arithmetic and copies ran while one was open for 6% -> 10% of each run, Pallas kernels for 16% -> 25%
where the time goes in v1:
time: 192 us; the launch traced here: 191 us
  Pallas kernels  70.5 us (37%)
  starting transfers between devices  54.7 us (28%)
  waiting for transfers between devices  39.4 us (21%)
  local copies, waits for them, and re-layouts  16.5 us (9%)
  other arithmetic  5.98 us (3%)
  matrix products  2.83 us (1%)
    pallas_call x5, Pallas kernels, call(): pl.pallas_call(kernel, out_shape=jax.ShapeDtypeStruct(shape, jnp.bfloat16...  56.4 us
    all_to_all x1, waiting for transfers between devices, local(): gathered = lax.all_to_all(spectrum, LAT_LON, 0, 0, tiled=True)  19.5 us
    ppermute x4, waiting for transfers between devices, shifted(): return lax.ppermute(block, axes, pairs)  17.7 us
    all_to_all x1, starting transfers between devices, local(): gathered = lax.all_to_all(spectrum, LAT_LON, 0, 0, tiled=True)  14.4 us
    pallas_call x2, Pallas kernels, by_rows(): pl.pallas_call(kernel, grid=(lat_dev // rows,), out_shape=jax.ShapeDtypeS...  14.2 us
    all_to_all x1, starting transfers between devices, local(): lax.all_to_all(filtered.reshape(owners, lats, owned, width), LAT_LON, 0,...  12.2 us
    ppermute x4, starting transfers between devices, shifted(): return lax.ppermute(block, axes, pairs)  11.2 us
    unnamed x37, local copies, waits for them, and re-layouts  5.32 us
  transfers between devices with their start and end apart: 12, of which 10 were waited for; matrix products, arithmetic and copies ran while one was open for 10% of the time, Pallas kernels for 25%

profile of v1, /device:TPU:1, one launch (start us, length us, event | category | flops | bytes accessed | tf_op | source)
XLA Modules:
  0.0 190.9 jit_solution(698417368804364754)
XLA Ops:
  2.9 3.3 %collective-permute-start = (bf16[12,64,32]{1,2,0:T(8,128)(2,1)S(1)}, bf16[12,64,32]{1,2,0:T(8,128)(2,1)S(1)}, u32[]{:S(2)}, u32[]{:S(2)}) collective-permute-start(bf16[12,64,32]{1,2,0:T(8,128)(2,1)S(1)} %broadcast_select_fusion.7), channel_id=1, source_target_pairs={{0,1},{1,0},{2,3},{3,2},{4,5},{5,4},{6,7},{7,6},{8,9},{9,8},{10,11... | collective-permute-start | bytes 147464 | tf_op jit(solution)/shard_map/ppermute | solution.py:431
  8.3 5.4 %shard_map.212 = bf16[24,64,384]{2,1,0:T(8,128)(2,1)} custom-call(bf16[24,64,384]{2,1,0:T(8,128)(2,1)} %atm_ref.3, bf16[1536,32]{1,0:T(8,128)(2,1)} %bitcast.35, bf16[32,384]{1,0:T(8,128)(2,1)} %out_weight_ref.3, f32[1,384]{1,0:T(1,128)} %get-tuple-element.41.gain_ref), custom_call_target="tpu_custom_call" | custom-call | tf_op jit(solution)/shard_map/pallas_call | solution.py:258
  13.7 3.8 %all-to-all-start = ((bf16[8,3,64,384]{3,2,1,0:T(8,128)(2,1)}), bf16[8,3,64,384]{3,2,1,0:T(8,128)(2,1)S(1)}, u32[]{:S(2)}, u32[]{:S(2)}) async-start(bf16[8,3,64,384]{3,2,1,0:T(8,128)(2,1)} %bitcast.33), calls=%async_computation | async-start | bytes 2359296 | tf_op jit(solution)/shard_map/all_to_all | solution.py:436
  20.7 3.6 %collective-permute-start.2 = (bf16[12,16,256]{2,1,0:T(8,128)(2,1)S(1)}, bf16[12,16,256]{2,1,0:T(8,128)(2,1)S(1)}, u32[]{:S(2)}, u32[]{:S(2)}) collective-permute-start(bf16[12,16,256]{2,1,0:T(8,128)(2,1)S(1)} %get-tuple-element.34), channel_id=1, source_target_pairs={{0,2},{2,4},{4,6},{6,8},{8,10},{10,12},{12,14},{1,3},{3,5},{5,7},{... | collective-permute-start | bytes 294920 | tf_op jit(solution)/shard_map/ppermute | solution.py:374
  25.6 6.6 %collective-permute-done.2 = bf16[12,16,256]{2,1,0:T(8,128)(2,1)S(1)} collective-permute-done((bf16[12,16,256]{2,1,0:T(8,128)(2,1)S(1)}, bf16[12,16,256]{2,1,0:T(8,128)(2,1)S(1)}, u32[]{:S(2)}, u32[]{:S(2)}) %collective-permute-start.2) | collective-permute-done | bytes 98336 | tf_op jit(solution)/shard_map/ppermute | solution.py:374
  35.7 2.3 %dynamic-slice_bitcast_fusion.table_hbm = bf16[512,1024]{1,0:T(8,128)(2,1)} fusion(bf16[2,512,1024]{2,1,0:T(8,128)(2,1)} %constant.46.clone, s32[]{:T(128)S(6)} %select_n.50), kind=kLoop, calls=%fused_computation.5 | loop fusion | bytes 2097156 | tf_op jit(solution)/shard_map/jit(dynamic_index_in_dim)/squeeze | solution.py:410
  38.3 4.6 %shard_map.213 = bf16[128,3,4,384]{3,2,1,0:T(4,128)(2,1)} custom-call(bf16[512,1024]{1,0:T(8,128)(2,1)} %dynamic-slice_bitcast_fusion.table_hbm, bf16[8,3,64,384]{3,2,1,0:T(8,128)(2,1)} %copy-done.4, bf16[8,3,64,384]{3,2,1,0:T(8,128)(2,1)} %collective-permute-done.4.other_hbm), custom_call_target="tpu_custom_call" | custom-call | tf_op jit(solution)/shard_map/pallas_call | solution.py:204
  42.9 14.4 %all-to-all-start.1 = ((bf16[128,3,4,384]{3,2,1,0:T(4,128)(2,1)}), bf16[128,3,4,384]{3,2,1,0:T(4,128)(2,1)S(1)}, u32[]{:S(2)}, u32[]{:S(2)}) async-start(bf16[128,3,4,384]{3,2,1,0:T(4,128)(2,1)} %shard_map.213), calls=%async_computation.1 | async-start | bytes 2359296 | tf_op jit(solution)/shard_map/all_to_all | solution.py:454
  57.3 4.2 %collective-permute-start.5 = (bf16[12,160,256]{2,1,0:T(8,128)(2,1)S(1)}, bf16[12,160,256]{2,1,0:T(8,128)(2,1)}, u32[]{:S(2)}, u32[]{:S(2)}) collective-permute-start(bf16[12,160,256]{2,1,0:T(8,128)(2,1)S(1)} %pad_maximum_fusion.centre_ref), channel_id=1, source_target_pairs={{0,1},{2,3},{4,5},{6,7},{8,9},{10,11},{12,13},{14,15},{1,16},{3,18... | collective-permute-start | bytes 2949128 | tf_op jit(solution)/shard_map/ppermute | solution.py:374
  61.5 2.1 %collective-permute-start.6 = (bf16[12,160,256]{2,1,0:T(8,128)(2,1)S(1)}, bf16[12,160,256]{2,1,0:T(8,128)(2,1)}, u32[]{:S(2)}, u32[]{:S(2)}) collective-permute-start(bf16[12,160,256]{2,1,0:T(8,128)(2,1)S(1)} %pad_maximum_fusion.centre_ref), channel_id=1, source_target_pairs={{1,0},{3,2},{5,4},{7,6},{9,8},{11,10},{13,12},{15,14},{16,1},{18,3... | collective-permute-start | bytes 2949128 | tf_op jit(solution)/shard_map/ppermute | solution.py:374
  63.6 2.1 %copy.26 = bf16[2,384,384]{1,2,0:T(8,128)(2,1)} copy(bf16[2,384,384]{2,1,0:T(8,128)(2,1)} %param.24) | data formatting | bytes 1179648 | tf_op args[3]
  68.3 19.5 %all-to-all-done.1 = bf16[128,3,4,384]{3,2,1,0:T(4,128)(2,1)S(1)} async-done(((bf16[128,3,4,384]{3,2,1,0:T(4,128)(2,1)}), bf16[128,3,4,384]{3,2,1,0:T(4,128)(2,1)S(1)}, u32[]{:S(2)}, u32[]{:S(2)}) %all-to-all-start.1) | async-done | bytes 1179680 | tf_op jit(solution)/shard_map/all_to_all | solution.py:454
  88.9 7.4 %shard_map.214 = bf16[384,4,384]{2,1,0:T(4,128)(2,1)} custom-call(f32[1,384]{1,0:T(1,128)} %broadcast_in_dim.25.gain_ref, bf16[384,4,384]{2,1,0:T(4,128)(2,1)} %bitcast.32, bf16[2,384,384]{2,1,0:T(8,128)(2,1)} %multiply_convert_fusion.weighted_hbm, bf16[2,384,384]{2,1,0:T(8,128)(2,1)} %bitcast.37, bf16[384,384]{1,0:T(8,128)(2,1)} %real_hbm.1, ...), custom_call_target="tpu_custom_call" | custom-call | tf_op jit(solution)/shard_map/pallas_call | solution.py:204
  96.3 5.2 %collective-permute-done.5.north_ref = bf16[12,160,256]{2,1,0:T(8,128)(2,1)} collective-permute-done((bf16[12,160,256]{2,1,0:T(8,128)(2,1)S(1)}, bf16[12,160,256]{2,1,0:T(8,128)(2,1)}, u32[]{:S(2)}, u32[]{:S(2)}) %collective-permute-start.5) | collective-permute-done | bytes 983072 | tf_op jit(solution)/shard_map/ppermute | solution.py:374
  101.5 4.0 %collective-permute-done.6.south_ref = bf16[12,160,256]{2,1,0:T(8,128)(2,1)} collective-permute-done((bf16[12,160,256]{2,1,0:T(8,128)(2,1)S(1)}, bf16[12,160,256]{2,1,0:T(8,128)(2,1)}, u32[]{:S(2)}, u32[]{:S(2)}) %collective-permute-start.6) | collective-permute-done | bytes 983072 | tf_op jit(solution)/shard_map/ppermute | solution.py:374
  105.5 12.2 %all-to-all-start.2 = ((bf16[128,3,4,384]{3,2,1,0:T(4,128)(2,1)}), bf16[128,3,4,384]{3,2,1,0:T(4,128)(2,1)S(1)}, u32[]{:S(2)}, u32[]{:S(2)}) async-start(bf16[128,3,4,384]{3,2,1,0:T(4,128)(2,1)} %bitcast.31), calls=%async_computation.2 | async-start | bytes 2359296 | tf_op jit(solution)/shard_map/all_to_all | solution.py:481
  122.1 25.2 %shard_map.215.first_ref = bf16[24,144,256]{2,1,0:T(8,128)(2,1)} custom-call(s32[4]{0:T(128)} %pad_add_fusion.edges_ref, bf16[12,160,256]{2,1,0:T(8,128)(2,1)} %copy-done.7, bf16[12,160,256]{2,1,0:T(8,128)(2,1)} %collective-permute-done.5.north_ref, bf16[12,160,256]{2,1,0:T(8,128)(2,1)} %collective-permute-done.6.south_ref, ...), custom_call_target="tpu_custom_call" | custom-call | tf_op jit(solution)/shard_map/pallas_call | solution.py:204
  147.6 3.8 %collective-permute-start.7 = (bf16[128,3,4,384]{3,2,1,0:T(4,128)(2,1)S(1)}, bf16[128,3,4,384]{3,2,1,0:T(4,128)(2,1)S(1)}, u32[]{:S(2)}, u32[]{:S(2)}) collective-permute-start(bf16[128,3,4,384]{3,2,1,0:T(4,128)(2,1)S(1)} %all-to-all-done.2.own_hbm), channel_id=1, source_target_pairs={{0,1},{1,0},{2,3},{3,2},{4,5},{5,4},{6,7},{7,6},{8,9},{9,8},{10,11... | collective-permute-start | bytes 3538952 | tf_op jit(solution)/shard_map/ppermute | solution.py:517
  151.4 2.3 %dynamic-slice_bitcast_fusion.1.table_hbm = bf16[512,1024]{1,0:T(8,128)(2,1)} fusion(bf16[2,512,1024]{2,1,0:T(8,128)(2,1)} %constant.47.clone, s32[]{:T(128)S(6)} %select_n.50), kind=kLoop, calls=%fused_computation.6 | loop fusion | bytes 2097156 | tf_op jit(solution)/shard_map/jit(dynamic_index_in_dim)/squeeze | solution.py:411
  154.9 4.6 %shard_map.216 = bf16[8,3,64,384]{3,2,1,0:T(8,128)(2,1)} custom-call(bf16[512,1024]{1,0:T(8,128)(2,1)} %dynamic-slice_bitcast_fusion.1.table_hbm, bf16[128,3,4,384]{3,2,1,0:T(4,128)(2,1)} %copy-done.3, bf16[128,3,4,384]{3,2,1,0:T(4,128)(2,1)} %copy-done.8), custom_call_target="tpu_custom_call" | custom-call | tf_op jit(solution)/shard_map/pallas_call | solution.py:204
  159.5 3.8 %all-to-all-start.3 = ((bf16[8,3,64,384]{3,2,1,0:T(8,128)(2,1)}), bf16[8,3,64,384]{3,2,1,0:T(8,128)(2,1)S(1)}, u32[]{:S(2)}, u32[]{:S(2)}) async-start(bf16[8,3,64,384]{3,2,1,0:T(8,128)(2,1)} %shard_map.216), calls=%async_computation.3 | async-start | bytes 2359296 | tf_op jit(solution)/shard_map/all_to_all | solution.py:520
  164.1 14.6 %shard_map.217 = bf16[12,128,256]{2,1,0:T(8,128)(2,1)} custom-call(bf16[24,144,256]{2,1,0:T(8,128)(2,1)} %shard_map.215.first_ref, f32[49,8,256]{2,1,0:T(8,128)} %broadcast_in_dim.30.kern_ref, f32[1,256]{1,0:T(1,128)} %get-tuple-element.42.gain_ref, bf16[256,1024]{1,0:T(8,128)(2,1)} %get-tuple-element.32.up_ref, bf16[1024,256]{1,0:T(8,128)(2,1)} %get-tuple-element.30.down_ref), custom_call_target="tpu_custom_call" | custom-call | tf_op jit(solution)/shard_map/pallas_call | solution.py:204
  178.7 2.3 %broadcast_select_fusion = bf16[12,128,256]{2,1,0:T(8,128)(2,1)} fusion(bf16[12,128,256]{2,1,0:T(8,128)(2,1)} %shard_map.217, bf16[12,128,256]{2,1,0:T(8,128)(2,1)S(1)} %copy-done.2, pred[12,128]{1,0:T(8,128)(4,1)S(1)} %broadcast_compare_fusion), kind=kLoop, calls=%fused_computation.8 | loop fusion | flops 393216 | bytes 2360832 | tf_op jit(solution)/shard_map/jit(_where)/select_n | solution.py:534
  182.1 8.8 %shard_map.218 = bf16[24,64,384]{2,1,0:T(8,128)(2,1)} custom-call(bf16[24,64,384]{2,1,0:T(8,128)(2,1)} %atm_ref.3, bf16[1536,32]{1,0:T(8,128)(2,1)} %bitcast.36, bf16[24,64,384]{2,1,0:T(8,128)(2,1)} %bitcast.34, bf16[32,384]{1,0:T(8,128)(2,1)} %out_weight_ref.3, f32[1,384]{1,0:T(1,128)} %get-tuple-element.40.gain_ref, bf16[384,768]{1,0:T(8,128)(2,1)} %up_ref.1, ...), custom_call_target="tpu_custom_call" | custom-call | tf_op jit(solution)/shard_map/pallas_call | solution.py:258
  (74 shorter events, 23.9 us)
Async XLA Ops:
  0.6 16.9 %copy-start = (bf16[384,32]{0,1:T(8,128)(2,1)S(1)}, bf16[384,32]{0,1:T(8,128)(2,1)}, u32[]{:S(2)}) copy-start(bf16[384,32]{0,1:T(8,128)(2,1)} %param.32) | copy-start | bytes 73732
  0.6 5.6 %copy-start.14 = (f32[2,384]{1,0:T(2,128)S(1)}, f32[2,384]{1,0:T(2,128)}, u32[]{:S(2)}) copy-start(f32[2,384]{1,0:T(2,128)} %param.29) | copy-start | bytes 9220
  2.9 4.3 %collective-permute-start = (bf16[12,64,32]{1,2,0:T(8,128)(2,1)S(1)}, bf16[12,64,32]{1,2,0:T(8,128)(2,1)S(1)}, u32[]{:S(2)}, u32[]{:S(2)}) collective-permute-start(bf16[12,64,32]{1,2,0:T(8,128)(2,1)S(1)} %broadcast_select_fusion.7), channel_id=1, source_target_pairs={{0,1},{1,0},{2,3},{3,2},{4,5},{5,4},{6,7},{7,6},{8,9},{9,8},{10,11... | collective-permute-start | bytes 147464 | tf_op jit(solution)/shard_map/ppermute | solution.py:431
  13.7 3.8 %copy-start.1 = (bf16[24,64,384]{2,1,0:T(8,128)(2,1)S(1)}, bf16[24,64,384]{2,1,0:T(8,128)(2,1)}, u32[]{:S(2)}) copy-start(bf16[24,64,384]{2,1,0:T(8,128)(2,1)} %atm_ref.3) | copy-start | bytes 3538948
  13.7 20.5 %all-to-all-start = ((bf16[8,3,64,384]{3,2,1,0:T(8,128)(2,1)}), bf16[8,3,64,384]{3,2,1,0:T(8,128)(2,1)S(1)}, u32[]{:S(2)}, u32[]{:S(2)}) async-start(bf16[8,3,64,384]{3,2,1,0:T(8,128)(2,1)} %bitcast.33), calls=%async_computation | async-start | bytes 2359296 | tf_op jit(solution)/shard_map/all_to_all | solution.py:436
  18.4 1.7 collective-permute-start.1
  20.7 11.5 %collective-permute-start.2 = (bf16[12,16,256]{2,1,0:T(8,128)(2,1)S(1)}, bf16[12,16,256]{2,1,0:T(8,128)(2,1)S(1)}, u32[]{:S(2)}, u32[]{:S(2)}) collective-permute-start(bf16[12,16,256]{2,1,0:T(8,128)(2,1)S(1)} %get-tuple-element.34), channel_id=1, source_target_pairs={{0,2},{2,4},{4,6},{6,8},{8,10},{10,12},{12,14},{1,3},{3,5},{5,7},{... | collective-permute-start | bytes 294920 | tf_op jit(solution)/shard_map/ppermute | solution.py:374
  24.3 9.8 %collective-permute-start.3 = (bf16[12,16,256]{2,1,0:T(8,128)(2,1)S(1)}, bf16[12,16,256]{2,1,0:T(8,128)(2,1)S(1)}, u32[]{:S(2)}, u32[]{:S(2)}) collective-permute-start(bf16[12,16,256]{2,1,0:T(8,128)(2,1)S(1)} %get-tuple-element.35), channel_id=1, source_target_pairs={{2,0},{4,2},{6,4},{8,6},{10,8},{12,10},{14,12},{3,1},{5,3},{7,5},{... | collective-permute-start | bytes 294920 | tf_op jit(solution)/shard_map/ppermute | solution.py:374
  34.2 27.3 %copy-start.7 = (bf16[12,160,256]{2,1,0:T(8,128)(2,1)}, bf16[12,160,256]{2,1,0:T(8,128)(2,1)S(1)}, u32[]{:S(2)}) copy-start(bf16[12,160,256]{2,1,0:T(8,128)(2,1)S(1)} %pad_maximum_fusion.centre_ref) | copy-start | bytes 2949124
  34.2 4.1 %copy-start.4 = (bf16[8,3,64,384]{3,2,1,0:T(8,128)(2,1)}, bf16[8,3,64,384]{3,2,1,0:T(8,128)(2,1)S(1)}, u32[]{:S(2)}) copy-start(bf16[8,3,64,384]{3,2,1,0:T(8,128)(2,1)S(1)} %all-to-all-done.own_hbm) | copy-start | bytes 3538948
  34.2 4.1 %collective-permute-start.4 = (bf16[8,3,64,384]{3,2,1,0:T(8,128)(2,1)S(1)}, bf16[8,3,64,384]{3,2,1,0:T(8,128)(2,1)}, u32[]{:S(2)}, u32[]{:S(2)}) collective-permute-start(bf16[8,3,64,384]{3,2,1,0:T(8,128)(2,1)S(1)} %all-to-all-done.own_hbm), channel_id=1, source_target_pairs={{0,1},{1,0},{2,3},{3,2},{4,5},{5,4},{6,7},{7,6},{8,9},{9,8},{10,11... | collective-permute-start | bytes 3538952 | tf_op jit(solution)/shard_map/ppermute | solution.py:451
  42.9 45.0 %all-to-all-start.1 = ((bf16[128,3,4,384]{3,2,1,0:T(4,128)(2,1)}), bf16[128,3,4,384]{3,2,1,0:T(4,128)(2,1)S(1)}, u32[]{:S(2)}, u32[]{:S(2)}) async-start(bf16[128,3,4,384]{3,2,1,0:T(4,128)(2,1)} %shard_map.213), calls=%async_computation.1 | async-start | bytes 2359296 | tf_op jit(solution)/shard_map/all_to_all | solution.py:454
  57.3 8.5 %copy-start.15 = (f32[384]{0:T(512)S(1)}, f32[384]{0:T(512)}, u32[]{:S(2)}) copy-start(f32[384]{0:T(512)} %param.28) | copy-start | bytes 4612
  57.3 9.0 %copy-start.16 = (f32[384]{0:T(512)S(1)}, f32[384]{0:T(512)}, u32[]{:S(2)}) copy-start(f32[384]{0:T(512)} %param.25) | copy-start | bytes 4612
  57.3 44.2 %collective-permute-start.5 = (bf16[12,160,256]{2,1,0:T(8,128)(2,1)S(1)}, bf16[12,160,256]{2,1,0:T(8,128)(2,1)}, u32[]{:S(2)}, u32[]{:S(2)}) collective-permute-start(bf16[12,160,256]{2,1,0:T(8,128)(2,1)S(1)} %pad_maximum_fusion.centre_ref), channel_id=1, source_target_pairs={{0,1},{2,3},{4,5},{6,7},{8,9},{10,11},{12,13},{14,15},{1,16},{3,18... | collective-permute-start | bytes 2949128 | tf_op jit(solution)/shard_map/ppermute | solution.py:374
  61.5 44.0 %collective-permute-start.6 = (bf16[12,160,256]{2,1,0:T(8,128)(2,1)S(1)}, bf16[12,160,256]{2,1,0:T(8,128)(2,1)}, u32[]{:S(2)}, u32[]{:S(2)}) collective-permute-start(bf16[12,160,256]{2,1,0:T(8,128)(2,1)S(1)} %pad_maximum_fusion.centre_ref), channel_id=1, source_target_pairs={{1,0},{3,2},{5,4},{7,6},{9,8},{11,10},{13,12},{15,14},{16,1},{18,3... | collective-permute-start | bytes 2949128 | tf_op jit(solution)/shard_map/ppermute | solution.py:374
  105.5 12.2 %copy-start.11 = (bf16[2,7,7,256]{3,0,2,1:T(2,128)(2,1)S(1)}, bf16[2,7,7,256]{3,0,2,1:T(2,128)(2,1)}, u32[]{:S(2)}) copy-start(bf16[2,7,7,256]{3,0,2,1:T(2,128)(2,1)} %param.36) | copy-start | bytes 150532
  105.5 13.1 %copy-start.17 = (f32[2,256]{1,0:T(2,128)S(1)}, f32[2,256]{1,0:T(2,128)}, u32[]{:S(2)}) copy-start(f32[2,256]{1,0:T(2,128)} %param.37) | copy-start | bytes 6148
  105.5 13.7 %copy-start.9 = (bf16[2,1024,256]{2,1,0:T(8,128)(2,1)S(1)}, bf16[2,1024,256]{2,1,0:T(8,128)(2,1)}, u32[]{:S(2)}) copy-start(bf16[2,1024,256]{2,1,0:T(8,128)(2,1)} %param.39) | copy-start | bytes 3145732
  105.5 42.1 %all-to-all-start.2 = ((bf16[128,3,4,384]{3,2,1,0:T(4,128)(2,1)}), bf16[128,3,4,384]{3,2,1,0:T(4,128)(2,1)S(1)}, u32[]{:S(2)}, u32[]{:S(2)}) async-start(bf16[128,3,4,384]{3,2,1,0:T(4,128)(2,1)} %bitcast.31), calls=%async_computation.2 | async-start | bytes 2359296 | tf_op jit(solution)/shard_map/all_to_all | solution.py:481
  147.6 6.3 %copy-start.3 = (bf16[128,3,4,384]{3,2,1,0:T(4,128)(2,1)}, bf16[128,3,4,384]{3,2,1,0:T(4,128)(2,1)S(1)}, u32[]{:S(2)}) copy-start(bf16[128,3,4,384]{3,2,1,0:T(4,128)(2,1)S(1)} %all-to-all-done.2.own_hbm) | copy-start | bytes 3538948
  147.6 6.3 %collective-permute-start.7 = (bf16[128,3,4,384]{3,2,1,0:T(4,128)(2,1)S(1)}, bf16[128,3,4,384]{3,2,1,0:T(4,128)(2,1)S(1)}, u32[]{:S(2)}, u32[]{:S(2)}) collective-permute-start(bf16[128,3,4,384]{3,2,1,0:T(4,128)(2,1)S(1)} %all-to-all-done.2.own_hbm), channel_id=1, source_target_pairs={{0,1},{1,0},{2,3},{3,2},{4,5},{5,4},{6,7},{7,6},{8,9},{9,8},{10,11... | collective-permute-start | bytes 3538952 | tf_op jit(solution)/shard_map/ppermute | solution.py:517
  159.5 3.8 %copy-start.12 = (s32[12,128]{1,0:T(8,128)S(1)}, s32[12,128]{1,0:T(8,128)}, u32[]{:S(2)}) copy-start(s32[12,128]{1,0:T(8,128)} %param.23) | copy-start | bytes 18436
  159.5 21.6 %all-to-all-start.3 = ((bf16[8,3,64,384]{3,2,1,0:T(8,128)(2,1)}), bf16[8,3,64,384]{3,2,1,0:T(8,128)(2,1)S(1)}, u32[]{:S(2)}, u32[]{:S(2)}) async-start(bf16[8,3,64,384]{3,2,1,0:T(8,128)(2,1)} %shard_map.216), calls=%async_computation.3 | async-start | bytes 2359296 | tf_op jit(solution)/shard_map/all_to_all | solution.py:520
  (6 other events, 10.5 us)

commit v2 on v1

v2 whole, which is shorter than its diff:
```python
import math

import jax
import jax.numpy as jnp
import ml_dtypes
import numpy as np
from jax import lax
from jax.experimental import pallas as pl
from jax.experimental.pallas import tpu as pltpu
from jax.sharding import Mesh
from jax.sharding import PartitionSpec as P

MODES = 512
STENCIL_TAPS = 7
OCEAN_DILATION = 2
LAT = ("y", "z_hi")
LON = ("z_lo", "x")
ALL = (*LAT, *LON, "comp")
OWNERS = ("z_hi", "z_lo", "x", "y")


epsilon = 1e-05


def owner_order():
    count = lax.axis_size(LAT) * lax.axis_size(LON)
    return np.arange(count).reshape(lax.axis_size("y"), -1).T.reshape(-1)


def wave_tables(owners, lon_count, circle, owned):
    rows = (owners[:, None] * owned + np.arange(owned)).reshape(-1)
    block = circle // (2 * lon_count)
    where = np.arange(lon_count * block)
    forward, inverse = [], []
    row_sets = [rows // owned * 2 * owned + q * owned + rows % owned for q in range(2)]
    place_sets = [(where // block * 2 + q) * block + where % block for q in range(2)]

    def waves(row, place):
        phase = (row[:, None] // 2) * place[None, :] % circle
        angle = phase.astype(np.float32) * np.float32(2.0 * math.pi / circle)
        return np.where((row % 2 == 0)[:, None], np.cos(angle), -np.sin(angle)).astype(np.float32)

    for own in range(2):
        order = (own, 1 - own)
        f = np.concatenate([waves(row_sets[own], place_sets[q]) for q in order], 1)
        forward.append(f / np.float32(math.sqrt(circle)))
        g = []
        for q in order:
            factor = np.where(row_sets[q] // 2 == 0, 1.0, 2.0).astype(np.float32)
            g.append((waves(row_sets[q], place_sets[own]) * factor[:, None]).T)
        inverse.append(np.concatenate(g, 1) / np.float32(math.sqrt(circle)))
    return (
        np.stack(forward).astype(ml_dtypes.bfloat16),
        np.stack(inverse).astype(ml_dtypes.bfloat16),
    )


def waves_kernel(
    table_hbm, own_hbm, other_hbm, out_hbm, table_ref, own_ref, other_ref, held, sems
):
    lats, width = own_ref.shape[0], own_ref.shape[3]
    half = table_ref.shape[1] // 2
    table = pltpu.make_async_copy(table_hbm, table_ref, sems.at[0])
    table.start()
    owns, others, sends = [], [], []
    for i in range(lats):
        owns.append(pltpu.make_async_copy(own_hbm.at[:, i], own_ref.at[i], sems.at[1 + i]))
        owns[-1].start()
        at = sems.at[1 + lats + i]
        others.append(pltpu.make_async_copy(other_hbm.at[:, i], other_ref.at[i], at))
        others[-1].start()
    table.wait()
    for i in range(lats):
        owns[i].wait()
        total = jnp.dot(
            table_ref[:, :half],
            own_ref[i].reshape(half, width),
            preferred_element_type=jnp.float32,
        )
        others[i].wait()
        total += jnp.dot(
            table_ref[:, half:],
            other_ref[i].reshape(half, width),
            preferred_element_type=jnp.float32,
        )
        held[i] = total.astype(jnp.bfloat16).reshape(held.shape[1:])
        at = sems.at[1 + 2 * lats + i]
        sends.append(pltpu.make_async_copy(held.at[i], out_hbm.at[:, i], at))
        sends[-1].start()
    for send in sends:
        send.wait()


def waves(shape, table, own, other):
    lats = shape[1]
    return call(
        waves_kernel,
        shape,
        table,
        own,
        other,
        scratch=[
            pltpu.VMEM(table.shape, jnp.bfloat16),
            pltpu.VMEM((lats, own.shape[0], *own.shape[2:]), jnp.bfloat16),
            pltpu.VMEM((lats, own.shape[0], *own.shape[2:]), jnp.bfloat16),
            pltpu.VMEM((lats, shape[0], *shape[2:]), jnp.bfloat16),
            pltpu.SemaphoreType.DMA((1 + 3 * lats,)),
        ],
        behind=3,
        away=True,
    )


def filter_kernel(
    gain_ref,
    spectrum_hbm,
    weights_hbm,
    out_hbm,
    spectrum_ref,
    weighted_ref,
    mix_ref,
    turned_ref,
    rows_ref,
    held,
    sems,
):
    count = weighted_ref.shape[0]
    lats, owned, width = spectrum_ref.shape
    block = 64
    side = block * owned
    parts = lats // block
    targets = [weighted_ref.at[m] for m in range(count)]
    targets += [mix_ref.at[:, h * width : (h + 1) * width] for h in range(2)]
    targets += [turned_ref.at[m] for m in range(count)]
    arrivals = []
    for b in range(parts):
        part = pl.ds(b * block, block)
        at = sems.at[len(targets) + b]
        arrivals.append(pltpu.make_async_copy(spectrum_hbm.at[part], spectrum_ref.at[part], at))
        arrivals[-1].start()
    fetches, at = [], 0
    for n, target in enumerate(targets):
        size = target.shape[0]
        fetches.append(
            pltpu.make_async_copy(weights_hbm.at[pl.ds(at, size)], target, sems.at[n])
        )
        fetches[-1].start()
        at += size
    r = lax.broadcasted_iota(jnp.int32, (side, side), 0)
    s = lax.broadcasted_iota(jnp.int32, (side, side), 1)
    pick = jnp.where((r % block) * owned + r // block == s, 1.0, 0.0).astype(jnp.bfloat16)
    back = jnp.where((s % block) * owned + s // block == r, 1.0, 0.0).astype(jnp.bfloat16)

    def columns(p):
        return slice(p % 2 * width, (p % 2 + 1) * width)

    for b in range(parts):
        span = slice(b * block, (b + 1) * block)
        arrivals[b].wait()
        piece = spectrum_ref[span].reshape(side, width)
        moved = jnp.dot(pick, piece, preferred_element_type=jnp.float32).astype(jnp.bfloat16)
        for p in range(owned):
            rows_ref[p // 2, span, columns(p)] = moved[p * block : (p + 1) * block]
    gain = jnp.transpose(jnp.broadcast_to(gain_ref[...], (8, lats)))[:, :1]
    for fetch in fetches:
        fetch.wait()
    for m in range(count):
        coeffs = jnp.dot(weighted_ref[m], rows_ref[m], preferred_element_type=jnp.float32)
        mixed = jnp.dot(
            coeffs.astype(jnp.bfloat16), mix_ref[...], preferred_element_type=jnp.float32
        )
        filtered = (mixed * gain).astype(jnp.bfloat16)
        rows_ref[m] = jnp.dot(
            turned_ref[m], filtered, preferred_element_type=jnp.float32
        ).astype(jnp.bfloat16)
    sends = []
    for b in range(parts):
        span = slice(b * block, (b + 1) * block)
        piece = jnp.concatenate(
            [rows_ref[p // 2, span, columns(p)] for p in range(owned)], axis=0
        )
        moved = jnp.dot(back, piece, preferred_element_type=jnp.float32).astype(jnp.bfloat16)
        held[span] = moved.reshape(block, owned, width)
        at = sems.at[len(targets) + parts + b]
        part = pl.ds(b * block, block)
        sends.append(pltpu.make_async_copy(held.at[part], out_hbm.at[part], at))
        sends[-1].start()
    for send in sends:
        send.wait()


VMEM = 62_900_000


def call(kernel, shape, *args, scratch=(), room=0, scalars=0, behind=0, away=False):
    spaces = [pltpu.SMEM] * scalars + [pltpu.VMEM] * (len(args) - scalars - behind)
    spaces += [pltpu.HBM] * behind
    return pl.pallas_call(
        kernel,
        out_shape=jax.ShapeDtypeStruct(shape, jnp.bfloat16),
        in_specs=[pl.BlockSpec(memory_space=space) for space in spaces],
        out_specs=pl.BlockSpec(memory_space=pltpu.HBM if away else pltpu.VMEM),
        scratch_shapes=list(scratch),
        compiler_params=pltpu.CompilerParams(vmem_limit_bytes=VMEM - room),
    )(*args)


def gelu(x):
    inner = x * (math.sqrt(2.0 / math.pi) + (math.sqrt(2.0 / math.pi) * 0.044715) * (x * x))
    half = 0.5 * x
    return half + half * jnp.tanh(inner)


def normalised(values, gain):
    centred = values - jnp.mean(values, axis=-1, keepdims=True)
    spread = jnp.mean(centred * centred, axis=-1, keepdims=True)
    return (centred * lax.rsqrt(spread + epsilon) * gain).astype(jnp.bfloat16)


def prologue_kernel(atm_ref, flux_ref, out_weight_ref, gain_ref, out_hbm, held, sems):
    rows, lon_dev, width = atm_ref.shape
    each = rows // sems.shape[0]
    sends = []
    for k in range(sems.shape[0]):
        part = pl.ds(k * each, each)
        flux = flux_ref[pl.ds(k * each * lon_dev, each * lon_dev)]
        forced = atm_ref[part].reshape(each * lon_dev, width).astype(jnp.float32) + jnp.dot(
            flux, out_weight_ref[...], preferred_element_type=jnp.float32
        )
        held[part] = normalised(forced, gain_ref[...]).reshape(each, lon_dev, width)
        sends.append(pltpu.make_async_copy(held.at[part], out_hbm.at[part], sems.at[k]))
        sends[-1].start()
    for send in sends:
        send.wait()


def epilogue_kernel(
    atm_ref, flux_ref, spectral_ref, out_weight_ref, gain_ref, up_ref, down_ref, out_ref
):
    rows, lon_dev, width = atm_ref.shape
    each = rows // 2
    side = each * lon_dev
    for k in range(2):
        part = pl.ds(k * each, each)
        forced = atm_ref[part].reshape(side, width).astype(jnp.float32) + jnp.dot(
            flux_ref[pl.ds(k * side, side)],
            out_weight_ref[...],
            preferred_element_type=jnp.float32,
        )
        mixed = forced + spectral_ref[part].reshape(side, width).astype(jnp.float32)
        normed = normalised(mixed, gain_ref[...])
        hidden = gelu(jnp.dot(normed, up_ref[...], preferred_element_type=jnp.float32))
        total = mixed + jnp.dot(
            hidden.astype(jnp.bfloat16), down_ref[...], preferred_element_type=jnp.float32
        )
        out_ref[part] = total.astype(jnp.bfloat16).reshape(each, lon_dev, width)


def epilogue(atm, flux, spectral, *weights, rows=8):
    lat_dev, lon_dev, width = atm.shape
    field = pl.BlockSpec((rows, lon_dev, width), lambda i: (i, 0, 0))
    specs = [field, pl.BlockSpec((rows * lon_dev, flux.shape[1]), lambda i: (i, 0)), field]
    specs += [pl.BlockSpec(w.shape, lambda i: (0, 0)) for w in weights]
    return pl.pallas_call(
        epilogue_kernel,
        grid=(lat_dev // rows,),
        out_shape=jax.ShapeDtypeStruct(atm.shape, jnp.bfloat16),
        in_specs=specs,
        out_specs=field,
        compiler_params=pltpu.CompilerParams(vmem_limit_bytes=VMEM - 38000000),
    )(atm, flux, spectral, *weights)


HALO = 16
LEAD = 8
LANES = 128
REACH = STENCIL_TAPS // 2 * OCEAN_DILATION


def ocean_rows(field, kern, gain, up, down, sums, out_ref, group, low, high):
    blocks = field.shape[0]
    rows, cols, width = out_ref.shape
    stride = cols // 8
    each = stride // OCEAN_DILATION

    def step(g, carry):
        top = g * group
        for r in range(group):
            for lane in range(blocks):
                part = slice(lane * LANES, (lane + 1) * LANES)
                for parity in range(OCEAN_DILATION):
                    acc = [None] * each
                    for a in range(STENCIL_TAPS):
                        row = top + r + a * OCEAN_DILATION
                        first = LEAD - REACH + parity
                        loads = [
                            field[lane, row, pl.ds(first + OCEAN_DILATION * q, 8, stride=stride), :]
                            for q in range(each + STENCIL_TAPS - 1)
                        ]
                        for b in range(STENCIL_TAPS):
                            weight = kern[a * STENCIL_TAPS + b, :, part]
                            for q in range(each):
                                term = loads[q + b] * weight
                                acc[q] = term if acc[q] is None else acc[q] + term
                    for q in range(each):
                        at = pl.ds(parity + OCEAN_DILATION * q, 8, stride=stride)
                        sums[lane, r, at, :] = acc[q]
        side = group * cols
        stencil = jnp.concatenate(
            [sums[lane].reshape(side, LANES) for lane in range(blocks)], axis=1
        )
        normed = normalised(stencil, gain[...])
        hidden = gelu(jnp.dot(normed, up[...], preferred_element_type=jnp.float32))
        total = jnp.dot(
            hidden.astype(jnp.bfloat16), down[...], preferred_element_type=jnp.float32
        )
        for r in range(group):
            centre = jnp.concatenate(
                [field[lane, top + r + REACH, LEAD : LEAD + cols, :] for lane in range(blocks)],
                axis=1,
            )
            value = centre + total[r * cols : (r + 1) * cols]
            col = lax.broadcasted_iota(jnp.int32, value.shape, 0)
            value = jnp.where((col >= low) & (col < high), value, 0.0)
            out_ref[top + r] = value.astype(jnp.bfloat16)
        return carry

    lax.fori_loop(0, rows // group, step, 0)


def ocean_kernel(
    inside_ref,
    centre_ref,
    north_ref,
    south_ref,
    kern_ref,
    gain_ref,
    up_ref,
    down_ref,
    out_ref,
    field,
    sums,
):
    at = 0
    for ref in (north_ref, centre_ref, south_ref):
        for lane in range(field.shape[0]):
            field[lane, at : at + ref.shape[0]] = ref[
                :, :, lane * LANES : (lane + 1) * LANES
            ].astype(jnp.float32)
        at += ref.shape[0]
    group = sums.shape[1]
    low, high = inside_ref[0], inside_ref[1]
    ocean_rows(field, kern_ref, gain_ref, up_ref, down_ref, sums, out_ref, group, low, high)


def ocean_block(first_col, circle, centre, north, south, kern, gain, up, down):
    rows, cols, width = centre.shape
    blocks, out_cols = width // LANES, cols - 2 * LEAD
    return call(
        ocean_kernel,
        (rows, out_cols, width),
        jnp.stack([-first_col, circle - first_col]).astype(jnp.int32),
        centre,
        north,
        south,
        kern,
        gain,
        up,
        down,
        scratch=[
            pltpu.VMEM((blocks, rows + 2 * REACH, cols, LANES), jnp.float32),
            pltpu.VMEM((blocks, 4, out_cols, LANES), jnp.float32),
        ],
        scalars=1,
        room=38_000_000,
    )


def shifted(block, dy, dx):
    tall = lax.axis_size(LAT) * lax.axis_size("comp")
    broad = lax.axis_size(LON)

    def place(y, x):
        return (y // 2 * broad + x) * 2 + y % 2

    pairs = [
        (place(y, x), place(y + dy, x + dx))
        for y in range(tall)
        for x in range(broad)
        if 0 <= y + dy < tall and 0 <= x + dx < broad
    ]
    return lax.ppermute(block, ALL, pairs)


def local(
    atm_state,
    ocean_state,
    wet_mask,
    legendre,
    quad_weight,
    spec_real,
    spec_imag,
    degree_gain,
    atm_gain,
    atm_up,
    atm_down,
    atm_to_surface,
    surface_to_atm,
    ocean_to_surface,
    surface_to_ocean,
    ocean_kernel,
    ocean_gain,
    ocean_up,
    ocean_down,
):
    lat_count = lax.axis_size(LAT)
    lon_count = lax.axis_size(LON)
    lat_dev, lon_dev, width = atm_state.shape
    sea_rows, sea_cols, sea_width = ocean_state.shape
    lat_total = lat_dev * lat_count
    circle = lon_dev * lon_count * 2
    owned = 2 * legendre.shape[0]
    owners = lat_count * lon_count
    order = owner_order()
    lats = lat_dev // lon_count
    me = lax.axis_index("comp")
    swap = [(0, 1), (1, 0)]
    forward, inverse = wave_tables(order, lon_count, circle, owned)
    forward = lax.dynamic_index_in_dim(jnp.asarray(forward), me, 0, keepdims=False)
    inverse = lax.dynamic_index_in_dim(jnp.asarray(inverse), me, 0, keepdims=False)
    wet = wet_mask.astype(jnp.float32)[:, :, None]
    ocean_flux = (
        jnp.dot(ocean_state, ocean_to_surface, preferred_element_type=jnp.float32) * wet
    ).astype(jnp.bfloat16)
    atm_flux = jnp.dot(atm_state, atm_to_surface, preferred_element_type=jnp.float32).astype(
        jnp.bfloat16
    )

    def halves(mine, dim):
        low, high = jnp.split(mine, 2, axis=dim)
        return (jnp.where(me == 0, low, high), jnp.where(me == 0, high, low))

    def together(kept, got, dim):
        low = jnp.where(me == 0, kept, got)
        high = jnp.where(me == 0, got, kept)
        return jnp.concatenate([low, high], axis=dim)

    kept_ocean, sent_ocean = halves(ocean_flux, 1)
    kept_atm, sent_atm = halves(atm_flux, 0)
    got_ocean = lax.ppermute(sent_ocean, "comp", swap)
    flux_here = together(kept_ocean, got_ocean, 0).reshape(lat_dev * lon_dev, -1)
    normed = call(
        prologue_kernel,
        atm_state.shape,
        atm_state,
        flux_here,
        surface_to_atm,
        atm_gain[:1],
        scratch=[pltpu.VMEM(atm_state.shape, jnp.bfloat16), pltpu.SemaphoreType.DMA((3,))],
        away=True,
        room=24000000,
    )
    rings = lax.all_to_all(
        normed.reshape(lon_count, lats, lon_dev, width), LON, 0, 0, tiled=True
    )
    flux_sea = together(kept_atm, lax.ppermute(sent_atm, "comp", swap), 1)
    ocean_in = (
        ocean_state.astype(jnp.float32)
        + wet * jnp.dot(flux_sea, surface_to_ocean, preferred_element_type=jnp.float32)
    ).astype(jnp.bfloat16)
    west = shifted(ocean_in[:, -HALO:], 0, 1)
    east = shifted(ocean_in[:, :HALO], 0, -1)
    broad = jnp.concatenate([west, ocean_in, east], axis=1)
    rings, broad = lax.optimization_barrier((rings, broad))
    seen = (order[:, None] * lats + np.arange(lats)).reshape(-1)
    moved = jnp.asarray(np.eye(lat_total)[:, seen].astype(ml_dtypes.bfloat16))
    table = jnp.einsum(
        "mlt,ts->mls", legendre, moved, preferred_element_type=jnp.float32
    ).astype(jnp.bfloat16)
    weight = quad_weight.reshape(lax.axis_size("y"), -1, lats).swapaxes(0, 1).reshape(-1)
    weighted = (table.astype(jnp.float32) * (weight / lat_total)).astype(jnp.bfloat16)
    turned = jnp.swapaxes(table, 1, 2)
    spectrum = waves(
        (owners, lats, owned, width), forward, rings, lax.ppermute(rings, "comp", swap)
    )
    spectrum, broad = lax.optimization_barrier((spectrum, broad))
    gathered = lax.all_to_all(spectrum, OWNERS, 0, 0, tiled=True)
    north = shifted(broad[-REACH:], 1, 0)
    south = shifted(broad[:REACH], -1, 0)
    weights = jnp.concatenate(
        [*weighted, spec_real, -spec_imag, spec_imag, spec_real, *turned], axis=0
    )
    filtered = call(
        filter_kernel,
        (lat_total, owned, width),
        degree_gain[None],
        gathered.reshape(lat_total, owned, width),
        weights,
        scratch=[
            pltpu.VMEM((lat_total, owned, width), jnp.bfloat16),
            pltpu.VMEM(weighted.shape, jnp.bfloat16),
            pltpu.VMEM((2 * width, 2 * width), jnp.bfloat16),
            pltpu.VMEM(turned.shape, jnp.bfloat16),
            pltpu.VMEM((owned // 2, lat_total, 2 * width), jnp.bfloat16),
            pltpu.VMEM((lat_total, owned, width), jnp.bfloat16),
            pltpu.SemaphoreType.DMA((6 + lat_total // 64 * 2,)),
        ],
        behind=2,
        away=True,
        room=100000,
    )
    filtered, broad, north, south = lax.optimization_barrier((filtered, broad, north, south))
    returned = lax.all_to_all(
        filtered.reshape(owners, lats, owned, width), OWNERS, 0, 0, tiled=True
    )
    first_col = lax.axis_index(LON) * sea_cols
    kernels = jnp.broadcast_to(
        ocean_kernel.astype(jnp.float32).reshape(2, STENCIL_TAPS**2, 1, sea_width),
        (2, STENCIL_TAPS**2, 8, sea_width),
    )
    blocks = [
        (kernels[k], ocean_gain[k : k + 1], ocean_up[k], ocean_down[k]) for k in range(2)
    ]
    first = ocean_block(first_col - LEAD, circle, broad, north, south, *blocks[0])
    returned, first = lax.optimization_barrier((returned, first))
    spatial = waves(
        (lon_count, lats, lon_dev, width), inverse, returned, lax.ppermute(returned, "comp", swap)
    )
    north = shifted(first[-REACH:], 1, 0)
    south = shifted(first[:REACH], -1, 0)
    spatial, first, north, south = lax.optimization_barrier((spatial, first, north, south))
    spectral = lax.all_to_all(spatial, LON, 0, 0, tiled=True).reshape(lat_dev, lon_dev, width)
    current = ocean_block(first_col, circle, first, north, south, *blocks[1])
    ocean_out = jnp.where(wet_mask[:, :, None] == 1, current, ocean_state)
    spectral, ocean_out = lax.optimization_barrier((spectral, ocean_out))
    atm_out = epilogue(
        atm_state, flux_here, spectral, surface_to_atm, atm_gain[1:], atm_up, atm_down
    )
    return (atm_out, ocean_out)


def solution(mesh):
    lat_count, lon_count = mesh.shape["lat"], mesh.shape["lon"]
    torus = Mesh(
        mesh.devices.reshape(4, lat_count // 4, lon_count // 4, 4, mesh.shape["comp"]), ALL
    )
    atm, sea = P(LAT, (*LON, "comp"), None), P((*LAT, "comp"), LON, None)
    placed = (atm, sea, P((*LAT, "comp"), LON), P(ALL, None, None)) + (P(),) * 15
    return jax.shard_map(
        local, mesh=torus, in_specs=placed, out_specs=(atm, sea), check_vma=False
    )
```

time: 192 us -> 189 us (0.984)
  Pallas kernels: 70.5 us -> 48.5 us
  local copies, waits for them, and re-layouts: 16.5 us -> 34 us
  starting transfers between devices: 54.7 us -> 61.3 us
  waiting for transfers between devices: 39.4 us -> 36 us
  other arithmetic: 5.98 us -> 3.45 us
    pallas_call x5 -> x6, Pallas kernels: 56.4 us -> 41 us  [call(): pl.pallas_call(kernel, out_shape=jax.ShapeDtypeStruct(shape, jnp.bfloat16...]
    unnamed x37 -> x58, local copies, waits for them, and re-layouts: 5.32 us -> 14.2 us
    pallas_call x2 -> x1, Pallas kernels: 14.2 us -> 7.55 us  [epilogue(): pl.pallas_call(epilogue_kernel, grid=(lat_dev // rows,), out_shape=jax.Sh...]
    another operation x0 -> x3, local copies, waits for them, and re-layouts: none -> 4.56 us  [local(): weights = jnp.concatenate([*weighted, spec_real, -spec_imag, spec_imag, s...]
    ppermute x4 -> x6, starting transfers between devices: 11.2 us -> 15.7 us  [shifted(): return lax.ppermute(block, ALL, pairs)]
    ppermute x4 -> x6, waiting for transfers between devices: 17.7 us -> 14.3 us  [shifted(): return lax.ppermute(block, ALL, pairs)]
    slice x2 -> x4, local copies, waits for them, and re-layouts: 0.86 us -> 3.42 us  [the longest x1 2.14 us: local(): south = shifted(first[:REACH], -1, 0)]
    div x0 -> x3, local copies, waits for them, and re-layouts: none -> 1.93 us  [local(): weight / lat_total]
  transfers between devices with their start and end apart: 12 -> 14, of which waited for: 10 -> 8; matrix products, arithmetic and copies ran while one was open for 10% -> 17% of each run, Pallas kernels for 25% -> 18%
where the time goes in v2:
time: 189 us; the launch traced here: 188 us
  starting transfers between devices  61.3 us (32%)
  Pallas kernels  48.5 us (26%)
  waiting for transfers between devices  36 us (19%)
  local copies, waits for them, and re-layouts  34 us (18%)
  other arithmetic  3.45 us (2%)
  matrix products  3.33 us (2%)
    pallas_call x6, Pallas kernels, call(): pl.pallas_call(kernel, out_shape=jax.ShapeDtypeStruct(shape, jnp.bfloat16...  41 us
    ppermute x6, starting transfers between devices, shifted(): return lax.ppermute(block, ALL, pairs)  15.7 us
    all_to_all x1, starting transfers between devices, local(): gathered = lax.all_to_all(spectrum, OWNERS, 0, 0, tiled=True)  14.5 us
    ppermute x6, waiting for transfers between devices, shifted(): return lax.ppermute(block, ALL, pairs)  14.3 us
    unnamed x58, local copies, waits for them, and re-layouts  14.2 us
    all_to_all x1, waiting for transfers between devices, local(): lax.all_to_all(filtered.reshape(owners, lats, owned, width), OWNERS, 0, 0...  13.5 us
    all_to_all x1, starting transfers between devices, local(): lax.all_to_all(filtered.reshape(owners, lats, owned, width), OWNERS, 0, 0...  12.1 us
    pallas_call x1, Pallas kernels, epilogue(): pl.pallas_call(epilogue_kernel, grid=(lat_dev // rows,), out_shape=jax.Sh...  7.55 us
  transfers between devices with their start and end apart: 14, of which 8 were waited for; matrix products, arithmetic and copies ran while one was open for 17% of the time, Pallas kernels for 18%

profile of v2, /device:TPU:1, one launch (start us, length us, event | category | flops | bytes accessed | tf_op | source)
XLA Modules:
  0.0 187.9 jit_solution(15702040210651525641)
XLA Ops:
  3.1 3.3 %collective-permute-start = (bf16[12,64,32]{1,2,0:T(8,128)(2,1)S(1)}, bf16[12,64,32]{1,2,0:T(8,128)(2,1)S(1)}, u32[]{:S(2)}, u32[]{:S(2)}) collective-permute-start(bf16[12,64,32]{1,2,0:T(8,128)(2,1)S(1)} %broadcast_select_fusion.7), channel_id=1, source_target_pairs={{0,1},{1,0},{2,3},{3,2},{4,5},{5,4},{6,7},{7,6},{8,9},{9,8},{10,11... | collective-permute-start | bytes 147464 | tf_op jit(solution)/shard_map/ppermute | solution.py:450
  9.6 4.4 %all-to-all-start = ((bf16[8,3,64,384]{3,2,1,0:T(8,128)(2,1)}), bf16[8,3,64,384]{3,2,1,0:T(8,128)(2,1)}, u32[]{:S(2)}, u32[]{:S(2)}) async-start(bf16[8,3,64,384]{3,2,1,0:T(8,128)(2,1)} %bitcast.4), calls=%async_computation | async-start | bytes 2359296 | tf_op jit(solution)/shard_map/all_to_all | solution.py:463
  16.8 3.5 %collective-permute-start.2 = (bf16[12,16,256]{2,1,0:T(8,128)(2,1)S(1)}, bf16[12,16,256]{2,1,0:T(8,128)(2,1)S(1)}, u32[]{:S(2)}, u32[]{:S(2)}) collective-permute-start(bf16[12,16,256]{2,1,0:T(8,128)(2,1)S(1)} %get-tuple-element.44), channel_id=1, source_target_pairs={{0,2},{2,4},{4,6},{6,8},{8,10},{10,12},{12,14},{1,3},{3,5},{5,7},{... | collective-permute-start | bytes 294920 | tf_op jit(solution)/shard_map/ppermute | solution.py:392
  21.6 7.3 %collective-permute-done.2 = bf16[12,16,256]{2,1,0:T(8,128)(2,1)S(1)} collective-permute-done((bf16[12,16,256]{2,1,0:T(8,128)(2,1)S(1)}, bf16[12,16,256]{2,1,0:T(8,128)(2,1)S(1)}, u32[]{:S(2)}, u32[]{:S(2)}) %collective-permute-start.2) | collective-permute-done | bytes 98336 | tf_op jit(solution)/shard_map/ppermute | solution.py:392
  32.1 2.3 %dynamic-slice_bitcast_fusion.table_hbm = bf16[512,1024]{1,0:T(8,128)(2,1)} fusion(bf16[2,512,1024]{2,1,0:T(8,128)(2,1)} %constant.40.clone, s32[]{:T(128)S(6)} %select_n.50), kind=kLoop, calls=%fused_computation.6 | loop fusion | bytes 2097156 | tf_op jit(solution)/shard_map/jit(dynamic_index_in_dim)/squeeze | solution.py:429
  34.9 4.5 %shard_map.222 = bf16[128,3,4,384]{3,2,1,0:T(4,128)(2,1)} custom-call(bf16[512,1024]{1,0:T(8,128)(2,1)} %dynamic-slice_bitcast_fusion.table_hbm, bf16[8,3,64,384]{3,2,1,0:T(8,128)(2,1)} %all-to-all-done.own_hbm, bf16[8,3,64,384]{3,2,1,0:T(8,128)(2,1)} %collective-permute-done.4.other_hbm), custom_call_target="tpu_custom_call" | custom-call | tf_op jit(solution)/shard_map/pallas_call | solution.py:198
  39.4 14.5 %all-to-all-start.1 = ((bf16[128,3,4,384]{3,2,1,0:T(4,128)(2,1)}), bf16[128,3,4,384]{3,2,1,0:T(4,128)(2,1)}, u32[]{:S(2)}, u32[]{:S(2)}) async-start(bf16[128,3,4,384]{3,2,1,0:T(4,128)(2,1)} %shard_map.222), calls=%async_computation.1 | async-start | bytes 2359296 | tf_op jit(solution)/shard_map/all_to_all | solution.py:487
  69.7 4.2 %collective-permute-start.5 = (bf16[6,160,256]{2,1,0:T(8,128)(2,1)}, bf16[6,160,256]{2,1,0:T(8,128)(2,1)}, u32[]{:S(2)}, u32[]{:S(2)}) collective-permute-start(bf16[6,160,256]{2,1,0:T(8,128)(2,1)} %get-tuple-element.41), channel_id=1, source_target_pairs={{0,1},{2,3},{4,5},{6,7},{8,9},{10,11},{12,13},{14,15},{1,16},{3,18... | collective-permute-start | bytes 1474568 | tf_op jit(solution)/shard_map/ppermute | solution.py:392
  73.9 2.1 %collective-permute-start.6 = (bf16[6,160,256]{2,1,0:T(8,128)(2,1)}, bf16[6,160,256]{2,1,0:T(8,128)(2,1)}, u32[]{:S(2)}, u32[]{:S(2)}) collective-permute-start(bf16[6,160,256]{2,1,0:T(8,128)(2,1)} %get-tuple-element.40), channel_id=1, source_target_pairs={{1,0},{3,2},{5,4},{7,6},{9,8},{11,10},{13,12},{15,14},{16,1},{18,3... | collective-permute-start | bytes 1474568 | tf_op jit(solution)/shard_map/ppermute | solution.py:392
  78.8 6.5 %all-to-all-done.1 = bf16[128,3,4,384]{3,2,1,0:T(4,128)(2,1)} async-done(((bf16[128,3,4,384]{3,2,1,0:T(4,128)(2,1)}), bf16[128,3,4,384]{3,2,1,0:T(4,128)(2,1)}, u32[]{:S(2)}, u32[]{:S(2)}) %all-to-all-start.1) | async-done | bytes 1179680 | tf_op jit(solution)/shard_map/all_to_all | solution.py:487
  85.3 6.7 %shard_map.223 = bf16[384,4,384]{2,1,0:T(4,128)(2,1)} custom-call(f32[1,384]{1,0:T(1,128)} %broadcast_in_dim.25.gain_ref, bf16[384,4,384]{2,1,0:T(4,128)(2,1)} %bitcast.7.spectrum_hbm, bf16[3072,384]{1,0:T(8,128)(2,1)} %fusion.2.weights_hbm), custom_call_target="tpu_custom_call" | custom-call | tf_op jit(solution)/shard_map/pallas_call | solution.py:198
  92.1 12.1 %all-to-all-start.2 = ((bf16[128,3,4,384]{3,2,1,0:T(4,128)(2,1)}), bf16[128,3,4,384]{3,2,1,0:T(4,128)(2,1)}, u32[]{:S(2)}, u32[]{:S(2)}) async-start(bf16[128,3,4,384]{3,2,1,0:T(4,128)(2,1)} %bitcast.55), calls=%async_computation.2 | async-start | bytes 2359296 | tf_op jit(solution)/shard_map/all_to_all | solution.py:513
  104.7 2.1 %slice_bitcast_fusion = (bf16[1024,256]{1,0:T(8,128)(2,1)}, bf16[1024,256]{1,0:T(8,128)(2,1)S(1)}) fusion(bf16[2,1024,256]{2,1,0:T(8,128)(2,1)} %param.40), kind=kLoop, calls=%fused_computation.11 | loop fusion | bytes 2097152 | tf_op jit(solution)/shard_map/squeeze | solution.py:522
  107.7 11.3 %shard_map.224.centre_ref = bf16[12,144,256]{2,1,0:T(8,128)(2,1)S(1)} custom-call(s32[2]{0:T(128)S(1)} %pad_add_fusion.inside_ref, bf16[12,160,256]{2,1,0:T(8,128)(2,1)S(1)} %pad_maximum_fusion.centre_ref, bf16[6,160,256]{2,1,0:T(8,128)(2,1)} %collective-permute-done.5.north_ref, bf16[6,160,256]{2,1,0:T(8,128)(2,1)} %collective-permute-done.6.south_ref, ...), custom_call_target="tpu_custom_call" | custom-call | tf_op jit(solution)/shard_map/pallas_call | solution.py:198
  119.9 13.5 %all-to-all-done.2.own_hbm = bf16[128,3,4,384]{3,2,1,0:T(4,128)(2,1)} async-done(((bf16[128,3,4,384]{3,2,1,0:T(4,128)(2,1)}), bf16[128,3,4,384]{3,2,1,0:T(4,128)(2,1)}, u32[]{:S(2)}, u32[]{:S(2)}) %all-to-all-start.2) | async-done | bytes 1179680 | tf_op jit(solution)/shard_map/all_to_all | solution.py:513
  133.5 5.4 %collective-permute-start.7 = (bf16[128,3,4,384]{3,2,1,0:T(4,128)(2,1)}, bf16[128,3,4,384]{3,2,1,0:T(4,128)(2,1)}, u32[]{:S(2)}, u32[]{:S(2)}) collective-permute-start(bf16[128,3,4,384]{3,2,1,0:T(4,128)(2,1)} %all-to-all-done.2.own_hbm), channel_id=1, source_target_pairs={{0,1},{1,0},{2,3},{3,2},{4,5},{5,4},{6,7},{7,6},{8,9},{9,8},{10,11... | collective-permute-start | bytes 3538952 | tf_op jit(solution)/shard_map/ppermute | solution.py:527
  138.8 2.1 %fusion.12 = (bf16[6,144,256]{2,1,0:T(8,128)(2,1)}, bf16[6,144,256]{2,1,0:T(8,128)(2,1)}) fusion(bf16[12,144,256]{2,1,0:T(8,128)(2,1)} %copy-done.2), kind=kLoop, calls=%fused_computation.50 | loop fusion | bytes 1769472 | tf_op jit(solution)/shard_map/slice | solution.py:530
  142.9 2.7 %collective-permute-start.9 = (bf16[6,144,256]{2,1,0:T(8,128)(2,1)}, bf16[6,144,256]{2,1,0:T(8,128)(2,1)}, u32[]{:S(2)}, u32[]{:S(2)}) collective-permute-start(bf16[6,144,256]{2,1,0:T(8,128)(2,1)} %get-tuple-element.42), channel_id=1, source_target_pairs={{1,0},{3,2},{5,4},{7,6},{9,8},{11,10},{13,12},{15,14},{16,1},{18,3... | collective-permute-start | bytes 1327112 | tf_op jit(solution)/shard_map/ppermute | solution.py:392
  145.5 2.3 %dynamic-slice_bitcast_fusion.1.table_hbm = bf16[512,1024]{1,0:T(8,128)(2,1)} fusion(bf16[2,512,1024]{2,1,0:T(8,128)(2,1)} %constant.41.clone, s32[]{:T(128)S(6)} %select_n.50), kind=kLoop, calls=%fused_computation.7 | loop fusion | bytes 2097156 | tf_op jit(solution)/shard_map/jit(dynamic_index_in_dim)/squeeze | solution.py:430
  147.8 4.6 %shard_map.225 = bf16[8,3,64,384]{3,2,1,0:T(8,128)(2,1)} custom-call(bf16[512,1024]{1,0:T(8,128)(2,1)} %dynamic-slice_bitcast_fusion.1.table_hbm, bf16[128,3,4,384]{3,2,1,0:T(4,128)(2,1)} %all-to-all-done.2.own_hbm, bf16[128,3,4,384]{3,2,1,0:T(4,128)(2,1)} %collective-permute-done.7.other_hbm), custom_call_target="tpu_custom_call" | custom-call | tf_op jit(solution)/shard_map/pallas_call | solution.py:198
  153.2 5.2 %collective-permute-done.9.south_ref = bf16[6,144,256]{2,1,0:T(8,128)(2,1)} collective-permute-done((bf16[6,144,256]{2,1,0:T(8,128)(2,1)}, bf16[6,144,256]{2,1,0:T(8,128)(2,1)}, u32[]{:S(2)}, u32[]{:S(2)}) %collective-permute-start.9) | collective-permute-done | bytes 442400 | tf_op jit(solution)/shard_map/ppermute | solution.py:392
  158.5 4.2 %all-to-all-start.3 = ((bf16[8,3,64,384]{3,2,1,0:T(8,128)(2,1)}), bf16[8,3,64,384]{3,2,1,0:T(8,128)(2,1)}, u32[]{:S(2)}, u32[]{:S(2)}) async-start(bf16[8,3,64,384]{3,2,1,0:T(8,128)(2,1)} %shard_map.225), calls=%async_computation.3 | async-start | bytes 2359296 | tf_op jit(solution)/shard_map/all_to_all | solution.py:532
  166.0 12.1 %shard_map.226 = bf16[12,128,256]{2,1,0:T(8,128)(2,1)S(1)} custom-call(s32[2]{0:T(128)S(1)} %pad_add_fusion.1.inside_ref, bf16[12,144,256]{2,1,0:T(8,128)(2,1)S(1)} %copy-done.3, bf16[6,144,256]{2,1,0:T(8,128)(2,1)S(1)} %copy-done.9, bf16[6,144,256]{2,1,0:T(8,128)(2,1)} %collective-permute-done.9.south_ref, f32[49,8,256]{2,1,0:T(8,128)S(1)} %broadcast_in_dim.30.kern_ref, ...), custom_call_target="tpu_custom_call" | custom-call | tf_op jit(solution)/shard_map/pallas_call | solution.py:198
  180.3 7.6 %shard_map.227 = bf16[24,64,384]{2,1,0:T(8,128)(2,1)} custom-call(bf16[24,64,384]{2,1,0:T(8,128)(2,1)S(1)} %copy-done.1, bf16[1536,32]{1,0:T(8,128)(2,1)S(1)} %bitcast.52, bf16[24,64,384]{2,1,0:T(8,128)(2,1)} %bitcast.21.spectral_ref, bf16[32,384]{1,0:T(8,128)(2,1)S(1)} %copy-done.10, f32[1,384]{1,0:T(1,128)S(1)} %get-tuple-element.52.gain_ref, ...), custom_call_target="tpu_custom_call" | custom-call | tf_op jit(solution)/shard_map/pallas_call | solution.py:264
  (111 shorter events, 42.1 us)
Async XLA Ops:
  0.6 55.2 %copy-start = (bf16[2,384,384]{2,1,0:T(8,128)(2,1)S(1)}, bf16[2,384,384]{2,1,0:T(8,128)(2,1)}, u32[]{:S(2)}) copy-start(bf16[2,384,384]{2,1,0:T(8,128)(2,1)} %param.25) | copy-start | bytes 1769476
  3.1 4.3 %collective-permute-start = (bf16[12,64,32]{1,2,0:T(8,128)(2,1)S(1)}, bf16[12,64,32]{1,2,0:T(8,128)(2,1)S(1)}, u32[]{:S(2)}, u32[]{:S(2)}) collective-permute-start(bf16[12,64,32]{1,2,0:T(8,128)(2,1)S(1)} %broadcast_select_fusion.7), channel_id=1, source_target_pairs={{0,1},{1,0},{2,3},{3,2},{4,5},{5,4},{6,7},{7,6},{8,9},{9,8},{10,11... | collective-permute-start | bytes 147464 | tf_op jit(solution)/shard_map/ppermute | solution.py:450
  9.6 21.2 %all-to-all-start = ((bf16[8,3,64,384]{3,2,1,0:T(8,128)(2,1)}), bf16[8,3,64,384]{3,2,1,0:T(8,128)(2,1)}, u32[]{:S(2)}, u32[]{:S(2)}) async-start(bf16[8,3,64,384]{3,2,1,0:T(8,128)(2,1)} %bitcast.4), calls=%async_computation | async-start | bytes 2359296 | tf_op jit(solution)/shard_map/all_to_all | solution.py:463
  14.8 1.4 collective-permute-start.1
  16.8 12.1 %collective-permute-start.2 = (bf16[12,16,256]{2,1,0:T(8,128)(2,1)S(1)}, bf16[12,16,256]{2,1,0:T(8,128)(2,1)S(1)}, u32[]{:S(2)}, u32[]{:S(2)}) collective-permute-start(bf16[12,16,256]{2,1,0:T(8,128)(2,1)S(1)} %get-tuple-element.44), channel_id=1, source_target_pairs={{0,2},{2,4},{4,6},{6,8},{8,10},{10,12},{12,14},{1,3},{3,5},{5,7},{... | collective-permute-start | bytes 294920 | tf_op jit(solution)/shard_map/ppermute | solution.py:392
  20.3 10.4 %collective-permute-start.3 = (bf16[12,16,256]{2,1,0:T(8,128)(2,1)S(1)}, bf16[12,16,256]{2,1,0:T(8,128)(2,1)S(1)}, u32[]{:S(2)}, u32[]{:S(2)}) collective-permute-start(bf16[12,16,256]{2,1,0:T(8,128)(2,1)S(1)} %get-tuple-element.45), channel_id=1, source_target_pairs={{2,0},{4,2},{6,4},{8,6},{10,8},{12,10},{14,12},{3,1},{5,3},{7,5},{... | collective-permute-start | bytes 294920 | tf_op jit(solution)/shard_map/ppermute | solution.py:392
  30.8 4.1 %collective-permute-start.4 = (bf16[8,3,64,384]{3,2,1,0:T(8,128)(2,1)}, bf16[8,3,64,384]{3,2,1,0:T(8,128)(2,1)}, u32[]{:S(2)}, u32[]{:S(2)}) collective-permute-start(bf16[8,3,64,384]{3,2,1,0:T(8,128)(2,1)} %all-to-all-done.own_hbm), channel_id=1, source_target_pairs={{0,1},{1,0},{2,3},{3,2},{4,5},{5,4},{6,7},{7,6},{8,9},{9,8},{10,11... | collective-permute-start | bytes 3538952 | tf_op jit(solution)/shard_map/ppermute | solution.py:484
  39.4 14.5 %copy-start.24 = (f32[384]{0:T(512)S(1)}, f32[384]{0:T(512)}, u32[]{:S(2)}) copy-start(f32[384]{0:T(512)} %param.26) | copy-start | bytes 4612
  39.4 16.4 %copy-start.18 = (bf16[384,384,1]{0,1,2:T(8,128)(2,1)S(1)}, bf16[384,384,1]{0,1,2:T(8,128)(2,1)}, u32[]{:S(2)}) copy-start(bf16[384,384,1]{0,1,2:T(8,128)(2,1)} %constant.47) | copy-start | bytes 884740
  39.4 45.9 %all-to-all-start.1 = ((bf16[128,3,4,384]{3,2,1,0:T(4,128)(2,1)}), bf16[128,3,4,384]{3,2,1,0:T(4,128)(2,1)}, u32[]{:S(2)}, u32[]{:S(2)}) async-start(bf16[128,3,4,384]{3,2,1,0:T(4,128)(2,1)} %shard_map.222), calls=%async_computation.1 | async-start | bytes 2359296 | tf_op jit(solution)/shard_map/all_to_all | solution.py:487
  65.3 10.7 %copy-start.16 = (bf16[384,384]{1,0:T(8,128)(2,1)S(1)}, bf16[384,384]{1,0:T(8,128)(2,1)}, u32[]{:S(2)}) copy-start(bf16[384,384]{1,0:T(8,128)(2,1)} %param.27) | copy-start | bytes 884740
  67.1 10.2 %copy-start.14 = (bf16[384,2,384]{2,0,1:T(8,128)(2,1)S(1)}, bf16[384,2,384]{2,0,1:T(8,128)(2,1)}, u32[]{:S(2)}) copy-start(bf16[384,2,384]{2,0,1:T(8,128)(2,1)} %copy-done.13) | copy-start | bytes 1769476
  69.7 22.4 %collective-permute-start.5 = (bf16[6,160,256]{2,1,0:T(8,128)(2,1)}, bf16[6,160,256]{2,1,0:T(8,128)(2,1)}, u32[]{:S(2)}, u32[]{:S(2)}) collective-permute-start(bf16[6,160,256]{2,1,0:T(8,128)(2,1)} %get-tuple-element.41), channel_id=1, source_target_pairs={{0,1},{2,3},{4,5},{6,7},{8,9},{10,11},{12,13},{14,15},{1,16},{3,18... | collective-permute-start | bytes 1474568 | tf_op jit(solution)/shard_map/ppermute | solution.py:392
  73.9 18.2 %collective-permute-start.6 = (bf16[6,160,256]{2,1,0:T(8,128)(2,1)}, bf16[6,160,256]{2,1,0:T(8,128)(2,1)}, u32[]{:S(2)}, u32[]{:S(2)}) collective-permute-start(bf16[6,160,256]{2,1,0:T(8,128)(2,1)} %get-tuple-element.40), channel_id=1, source_target_pairs={{1,0},{3,2},{5,4},{7,6},{9,8},{11,10},{13,12},{15,14},{16,1},{18,3... | collective-permute-start | bytes 1474568 | tf_op jit(solution)/shard_map/ppermute | solution.py:392
  92.1 12.2 %copy-start.19 = (bf16[2,7,7,256]{3,0,2,1:T(2,128)(2,1)S(1)}, bf16[2,7,7,256]{3,0,2,1:T(2,128)(2,1)}, u32[]{:S(2)}) copy-start(bf16[2,7,7,256]{3,0,2,1:T(2,128)(2,1)} %param.37) | copy-start | bytes 150532
  92.1 12.6 %copy-start.25 = (f32[2,256]{1,0:T(2,128)S(1)}, f32[2,256]{1,0:T(2,128)}, u32[]{:S(2)}) copy-start(f32[2,256]{1,0:T(2,128)} %param.38) | copy-start | bytes 6148
  92.1 41.4 %all-to-all-start.2 = ((bf16[128,3,4,384]{3,2,1,0:T(4,128)(2,1)}), bf16[128,3,4,384]{3,2,1,0:T(4,128)(2,1)}, u32[]{:S(2)}, u32[]{:S(2)}) async-start(bf16[128,3,4,384]{3,2,1,0:T(4,128)(2,1)} %bitcast.55), calls=%async_computation.2 | async-start | bytes 2359296 | tf_op jit(solution)/shard_map/all_to_all | solution.py:513
  133.5 14.4 %collective-permute-start.7 = (bf16[128,3,4,384]{3,2,1,0:T(4,128)(2,1)}, bf16[128,3,4,384]{3,2,1,0:T(4,128)(2,1)}, u32[]{:S(2)}, u32[]{:S(2)}) collective-permute-start(bf16[128,3,4,384]{3,2,1,0:T(4,128)(2,1)} %all-to-all-done.2.own_hbm), channel_id=1, source_target_pairs={{0,1},{1,0},{2,3},{3,2},{4,5},{5,4},{6,7},{7,6},{8,9},{9,8},{10,11... | collective-permute-start | bytes 3538952 | tf_op jit(solution)/shard_map/ppermute | solution.py:527
  141.0 11.4 %collective-permute-start.8 = (bf16[6,144,256]{2,1,0:T(8,128)(2,1)}, bf16[6,144,256]{2,1,0:T(8,128)(2,1)S(1)}, u32[]{:S(2)}, u32[]{:S(2)}) collective-permute-start(bf16[6,144,256]{2,1,0:T(8,128)(2,1)} %get-tuple-element.43), channel_id=1, source_target_pairs={{0,1},{2,3},{4,5},{6,7},{8,9},{10,11},{12,13},{14,15},{1,16},{3,18... | collective-permute-start | bytes 1327112 | tf_op jit(solution)/shard_map/ppermute | solution.py:392
  142.9 15.6 %collective-permute-start.9 = (bf16[6,144,256]{2,1,0:T(8,128)(2,1)}, bf16[6,144,256]{2,1,0:T(8,128)(2,1)}, u32[]{:S(2)}, u32[]{:S(2)}) collective-permute-start(bf16[6,144,256]{2,1,0:T(8,128)(2,1)} %get-tuple-element.42), channel_id=1, source_target_pairs={{1,0},{3,2},{5,4},{7,6},{9,8},{11,10},{13,12},{15,14},{16,1},{18,3... | collective-permute-start | bytes 1327112 | tf_op jit(solution)/shard_map/ppermute | solution.py:392
  152.4 10.4 %copy-start.20 = (s32[12,128]{1,0:T(8,128)S(1)}, s32[12,128]{1,0:T(8,128)}, u32[]{:S(2)}) copy-start(s32[12,128]{1,0:T(8,128)} %param.24) | copy-start | bytes 18436
  152.4 10.5 %copy-start.3 = (bf16[12,144,256]{2,1,0:T(8,128)(2,1)S(1)}, bf16[12,144,256]{2,1,0:T(8,128)(2,1)}, u32[]{:S(2)}) copy-start(bf16[12,144,256]{2,1,0:T(8,128)(2,1)} %copy-done.2) | copy-start | bytes 2654212
  158.5 20.8 %all-to-all-start.3 = ((bf16[8,3,64,384]{3,2,1,0:T(8,128)(2,1)}), bf16[8,3,64,384]{3,2,1,0:T(8,128)(2,1)}, u32[]{:S(2)}, u32[]{:S(2)}) async-start(bf16[8,3,64,384]{3,2,1,0:T(8,128)(2,1)} %shard_map.225), calls=%async_computation.3 | async-start | bytes 2359296 | tf_op jit(solution)/shard_map/all_to_all | solution.py:532
  166.0 12.1 %copy-start.12 = (bf16[12,128,256]{2,1,0:T(8,128)(2,1)S(1)}, bf16[12,128,256]{2,1,0:T(8,128)(2,1)}, u32[]{:S(2)}) copy-start(bf16[12,128,256]{2,1,0:T(8,128)(2,1)} %param.23) | copy-start | bytes 2359300
  (16 other events, 63.3 us)

commit v3 on v2

--- a/solution.py
+++ b/solution.py
@@ -1,3 +1,4 @@
+import functools
 import math
 
 import jax
@@ -235,40 +236,90 @@
 
 
 def epilogue_kernel(
-    atm_ref, flux_ref, spectral_ref, out_weight_ref, gain_ref, up_ref, down_ref, out_ref
+    gain_ref,
+    out_weight_ref,
+    flux_ref,
+    atm_hbm,
+    spectral_hbm,
+    up_hbm,
+    down_hbm,
+    out_hbm,
+    atm,
+    spectral,
+    up,
+    down,
+    held,
+    sems,
 ):
-    rows, lon_dev, width = atm_ref.shape
-    each = rows // 2
+    rows, lon_dev, width = atm.shape
+    parts = 3
+    each = rows // parts
     side = each * lon_dev
-    for k in range(2):
-        part = pl.ds(k * each, each)
-        forced = atm_ref[part].reshape(side, width).astype(jnp.float32) + jnp.dot(
+    spans = [pl.ds(k * each, each) for k in range(parts)]
+    fields = [
+        [
+            pltpu.make_async_copy(atm_hbm.at[span], atm.at[span], sems.at[k]),
+            pltpu.make_async_copy(spectral_hbm.at[span], spectral.at[span], sems.at[parts + k]),
+        ]
+        for k, span in enumerate(spans)
+    ]
+    weights = [
+        pltpu.make_async_copy(up_hbm, up, sems.at[3 * parts]),
+        pltpu.make_async_copy(down_hbm, down, sems.at[3 * parts + 1]),
+    ]
+    for copy in fields[0] + weights + [c for pair in fields[1:] for c in pair]:
+        copy.start()
+    sends = []
+    for k, span in enumerate(spans):
+        for copy in fields[k]:
+            copy.wait()
+        forced = atm[span].reshape(side, width).astype(jnp.float32) + jnp.dot(
             flux_ref[pl.ds(k * side, side)],
             out_weight_ref[...],
             preferred_element_type=jnp.float32,
         )
-        mixed = forced + spectral_ref[part].reshape(side, width).astype(jnp.float32)
+        mixed = forced + spectral[span].reshape(side, width).astype(jnp.float32)
         normed = normalised(mixed, gain_ref[...])
-        hidden = gelu(jnp.dot(normed, up_ref[...], preferred_element_type=jnp.float32))
+        if k == 0:
+            weights[0].wait()
+        hidden = gelu(jnp.dot(normed, up[...], preferred_element_type=jnp.float32))
+        if k == 0:
+            weights[1].wait()
         total = mixed + jnp.dot(
-            hidden.astype(jnp.bfloat16), down_ref[...], preferred_element_type=jnp.float32
-        )
-        out_ref[part] = total.astype(jnp.bfloat16).reshape(each, lon_dev, width)
-
-
-def epilogue(atm, flux, spectral, *weights, rows=8):
-    lat_dev, lon_dev, width = atm.shape
-    field = pl.BlockSpec((rows, lon_dev, width), lambda i: (i, 0, 0))
-    specs = [field, pl.BlockSpec((rows * lon_dev, flux.shape[1]), lambda i: (i, 0)), field]
-    specs += [pl.BlockSpec(w.shape, lambda i: (0, 0)) for w in weights]
-    return pl.pallas_call(
+            hidden.astype(jnp.bfloat16), down[...], preferred_element_type=jnp.float32
+        )
+        held[span] = total.astype(jnp.bfloat16).reshape(each, lon_dev, width)
+        sends.append(
+            pltpu.make_async_copy(held.at[span], out_hbm.at[span], sems.at[2 * parts + k])
+        )
+        sends[-1].start()
+    for send in sends:
+        send.wait()
+
+
+def epilogue(atm, flux, spectral, out_weight, gain, up, down):
+    return call(
         epilogue_kernel,
-        grid=(lat_dev // rows,),
-        out_shape=jax.ShapeDtypeStruct(atm.shape, jnp.bfloat16),
-        in_specs=specs,
-        out_specs=field,
-        compiler_params=pltpu.CompilerParams(vmem_limit_bytes=VMEM - 38000000),
-    )(atm, flux, spectral, *weights)
+        atm.shape,
+        gain,
+        out_weight,
+        flux,
+        atm,
+        spectral,
+        up,
+        down,
+        scratch=[
+            pltpu.VMEM(atm.shape, jnp.bfloat16),
+            pltpu.VMEM(atm.shape, jnp.bfloat16),
+            pltpu.VMEM(up.shape, jnp.bfloat16),
+            pltpu.VMEM(down.shape, jnp.bfloat16),
+            pltpu.VMEM(atm.shape, jnp.bfloat16),
+            pltpu.SemaphoreType.DMA((11,)),
+        ],
+        behind=4,
+        away=True,
+        room=100_000,
+    )
 
 
 HALO = 16
@@ -277,14 +328,45 @@
 REACH = STENCIL_TAPS // 2 * OCEAN_DILATION
 
 
-def ocean_rows(field, kern, gain, up, down, sums, out_ref, group, low, high):
+def ocean_kernel(
+    inside_ref,
+    gain_ref,
+    north_hbm,
+    upper_hbm,
+    lower_hbm,
+    south_hbm,
+    kern_hbm,
+    up_hbm,
+    down_hbm,
+    *rest,
+    block,
+    group,
+):
+    *outs, staged, field, kern, up, down, sums, held, sems = rest
+    half = staged.shape[1]
     blocks = field.shape[0]
-    rows, cols, width = out_ref.shape
+    rows, cols, width = held.shape
     stride = cols // 8
     each = stride // OCEAN_DILATION
-
-    def step(g, carry):
-        top = g * group
+    arrivals = [pltpu.make_async_copy(kern_hbm.at[block], kern, sems.at[0])]
+    for n, piece in enumerate((north_hbm, upper_hbm, lower_hbm, south_hbm)):
+        arrivals.append(pltpu.make_async_copy(piece, staged.at[n], sems.at[1 + n]))
+    weights = [
+        pltpu.make_async_copy(up_hbm.at[block], up, sems.at[5]),
+        pltpu.make_async_copy(down_hbm.at[block], down, sems.at[6]),
+    ]
+    for copy in arrivals + weights:
+        copy.start()
+    for n in range(4):
+        arrivals[1 + n].wait()
+        for lane in range(blocks):
+            field[lane, n * half : (n + 1) * half] = staged[
+                n, :, :, lane * LANES : (lane + 1) * LANES
+            ].astype(jnp.float32)
+    arrivals[0].wait()
+    low, high = inside_ref[0], inside_ref[1]
+
+    def stencil(top):
         for r in range(group):
             for lane in range(blocks):
                 part = slice(lane * LANES, (lane + 1) * LANES)
@@ -305,11 +387,13 @@
                     for q in range(each):
                         at = pl.ds(parity + OCEAN_DILATION * q, 8, stride=stride)
                         sums[lane, r, at, :] = acc[q]
+
+    def layers(top):
         side = group * cols
-        stencil = jnp.concatenate(
+        joined = jnp.concatenate(
             [sums[lane].reshape(side, LANES) for lane in range(blocks)], axis=1
         )
-        normed = normalised(stencil, gain[...])
+        normed = normalised(joined, gain_ref[...])
         hidden = gelu(jnp.dot(normed, up[...], preferred_element_type=jnp.float32))
         total = jnp.dot(
             hidden.astype(jnp.bfloat16), down[...], preferred_element_type=jnp.float32
@@ -322,57 +406,63 @@
             value = centre + total[r * cols : (r + 1) * cols]
             col = lax.broadcasted_iota(jnp.int32, value.shape, 0)
             value = jnp.where((col >= low) & (col < high), value, 0.0)
-            out_ref[top + r] = value.astype(jnp.bfloat16)
+            held[top + r] = value.astype(jnp.bfloat16)
+
+    def step(g, carry):
+        stencil(g * group)
+
+        @pl.when(g == 0)
+        def _():
+            for copy in weights:
+                copy.wait()
+
+        layers(g * group)
         return carry
 
     lax.fori_loop(0, rows // group, step, 0)
-
-
-def ocean_kernel(
-    inside_ref,
-    centre_ref,
-    north_ref,
-    south_ref,
-    kern_ref,
-    gain_ref,
-    up_ref,
-    down_ref,
-    out_ref,
-    field,
-    sums,
-):
-    at = 0
-    for ref in (north_ref, centre_ref, south_ref):
-        for lane in range(field.shape[0]):
-            field[lane, at : at + ref.shape[0]] = ref[
-                :, :, lane * LANES : (lane + 1) * LANES
-            ].astype(jnp.float32)
-        at += ref.shape[0]
-    group = sums.shape[1]
-    low, high = inside_ref[0], inside_ref[1]
-    ocean_rows(field, kern_ref, gain_ref, up_ref, down_ref, sums, out_ref, group, low, high)
-
-
-def ocean_block(first_col, circle, centre, north, south, kern, gain, up, down):
-    rows, cols, width = centre.shape
-    blocks, out_cols = width // LANES, cols - 2 * LEAD
-    return call(
-        ocean_kernel,
-        (rows, out_cols, width),
+    sends = []
+    each_out = rows // len(outs)
+    for n, out in enumerate(outs):
+        part = pl.ds(n * each_out, each_out)
+        sends.append(pltpu.make_async_copy(held.at[part], out, sems.at[7 + n]))
+        sends[-1].start()
+    for send in sends:
+        send.wait()
+
+
+def ocean_block(first_col, circle, pieces, kern, gain, up, down, block, parts):
+    half, cols, width = pieces[0].shape
+    blocks, out_cols, rows = width // LANES, cols - 2 * LEAD, 2 * half
+    group = 4
+    out = jax.ShapeDtypeStruct((rows // parts, out_cols, width), jnp.bfloat16)
+    hbm = pl.BlockSpec(memory_space=pltpu.HBM)
+    return pl.pallas_call(
+        functools.partial(ocean_kernel, block=block, group=group),
+        out_shape=[out] * parts,
+        in_specs=[
+            pl.BlockSpec(memory_space=pltpu.SMEM),
+            pl.BlockSpec(memory_space=pltpu.VMEM),
+            *[hbm] * 7,
+        ],
+        out_specs=[hbm] * parts,
+        scratch_shapes=[
+            pltpu.VMEM((4, half, cols, width), jnp.bfloat16),
+            pltpu.VMEM((blocks, 4 * half, cols, LANES), jnp.float32),
+            pltpu.VMEM(kern.shape[1:], jnp.float32),
+            pltpu.VMEM(up.shape[1:], jnp.bfloat16),
+            pltpu.VMEM(down.shape[1:], jnp.bfloat16),
+            pltpu.VMEM((blocks, group, out_cols, LANES), jnp.float32),
+            pltpu.VMEM((rows, out_cols, width), jnp.bfloat16),
+            pltpu.SemaphoreType.DMA((7 + parts,)),
+        ],
+        compiler_params=pltpu.CompilerParams(vmem_limit_bytes=VMEM - 100_000),
+    )(
         jnp.stack([-first_col, circle - first_col]).astype(jnp.int32),
-        centre,
-        north,
-        south,
+        gain[block : block + 1],
+        *pieces,
         kern,
-        gain,
         up,
         down,
-        scratch=[
-            pltpu.VMEM((blocks, rows + 2 * REACH, cols, LANES), jnp.float32),
-            pltpu.VMEM((blocks, 4, out_cols, LANES), jnp.float32),
-        ],
-        scalars=1,
-        room=38_000_000,
     )
 
 
@@ -470,8 +560,11 @@
     ).astype(jnp.bfloat16)
     west = shifted(ocean_in[:, -HALO:], 0, 1)
     east = shifted(ocean_in[:, :HALO], 0, -1)
-    broad = jnp.concatenate([west, ocean_in, east], axis=1)
-    rings, broad = lax.optimization_barrier((rings, broad))
+    upper, lower = [
+        jnp.concatenate([west[part], ocean_in[part], east[part]], axis=1)
+        for part in (slice(0, REACH), slice(REACH, None))
+    ]
+    rings, upper, lower = lax.optimization_barrier((rings, upper, lower))
     seen = (order[:, None] * lats + np.arange(lats)).reshape(-1)
     moved = jnp.asarray(np.eye(lat_total)[:, seen].astype(ml_dtypes.bfloat16))
     table = jnp.einsum(
@@ -483,10 +576,9 @@
     spectrum = waves(
         (owners, lats, owned, width), forward, rings, lax.ppermute(rings, "comp", swap)
     )
-    spectrum, broad = lax.optimization_barrier((spectrum, broad))
+    spectrum, upper, lower = lax.optimization_barrier((spectrum, upper, lower))
     gathered = lax.all_to_all(spectrum, OWNERS, 0, 0, tiled=True)
-    north = shifted(broad[-REACH:], 1, 0)
-    south = shifted(broad[:REACH], -1, 0)
+    north, south = shifted(lower, 1, 0), shifted(upper, -1, 0)
     weights = jnp.concatenate(
         [*weighted, spec_real, -spec_imag, spec_imag, spec_real, *turned], axis=0
     )
@@ -509,7 +601,7 @@
         away=True,
         room=100000,
     )
-    filtered, broad, north, south = lax.optimization_barrier((filtered, broad, north, south))
+    filtered, *pieces = lax.optimization_barrier((filtered, north, upper, lower, south))
     returned = lax.all_to_all(
         filtered.reshape(owners, lats, owned, width), OWNERS, 0, 0, tiled=True
     )
@@ -518,19 +610,16 @@
         ocean_kernel.astype(jnp.float32).reshape(2, STENCIL_TAPS**2, 1, sea_width),
         (2, STENCIL_TAPS**2, 8, sea_width),
     )
-    blocks = [
-        (kernels[k], ocean_gain[k : k + 1], ocean_up[k], ocean_down[k]) for k in range(2)
-    ]
-    first = ocean_block(first_col - LEAD, circle, broad, north, south, *blocks[0])
-    returned, first = lax.optimization_barrier((returned, first))
+    ocean = (kernels, ocean_gain, ocean_up, ocean_down)
+    upper, lower = ocean_block(first_col - LEAD, circle, pieces, *ocean, 0, 2)
+    north, south = shifted(lower, 1, 0), shifted(upper, -1, 0)
+    returned, *pieces = lax.optimization_barrier((returned, north, upper, lower, south))
     spatial = waves(
         (lon_count, lats, lon_dev, width), inverse, returned, lax.ppermute(returned, "comp", swap)
     )
-    north = shifted(first[-REACH:], 1, 0)
-    south = shifted(first[:REACH], -1, 0)
-    spatial, first, north, south = lax.optimization_barrier((spatial, first, north, south))
+    spatial, *pieces = lax.optimization_barrier((spatial, *pieces))
     spectral = lax.all_to_all(spatial, LON, 0, 0, tiled=True).reshape(lat_dev, lon_dev, width)
-    current = ocean_block(first_col, circle, first, north, south, *blocks[1])
+    (current,) = ocean_block(first_col, circle, pieces, *ocean, 1, 1)
     ocean_out = jnp.where(wet_mask[:, :, None] == 1, current, ocean_state)
     spectral, ocean_out = lax.optimization_barrier((spectral, ocean_out))
     atm_out = epilogue(

time: 189 us -> 190 us (level)
  Pallas kernels: 48.5 us -> 58.4 us
  local copies, waits for them, and re-layouts: 34 us -> 24.9 us
  starting transfers between devices: 61.3 us -> 57.3 us
  other arithmetic: 3.45 us -> 6.67 us
    pallas_call x1 -> x2, Pallas kernels: 7.55 us -> 33 us  [ocean_block(): pl.pallas_call(functools.partial(ocean_kernel, block=block, group=group),...]
    pallas_call x6 -> x5, Pallas kernels: 41 us -> 25.4 us  [call(): pl.pallas_call(kernel, out_shape=jax.ShapeDtypeStruct(shape, jnp.bfloat16...]
    all_to_all x1, waiting for transfers between devices: 13.5 us -> 0.01 us  [local(): lax.all_to_all(filtered.reshape(owners, lats, owned, width), OWNERS, 0, 0...]
    ppermute x6, waiting for transfers between devices: 14.3 us -> 23.2 us  [shifted(): return lax.ppermute(block, ALL, pairs)]
    ppermute x1, starting transfers between devices: 5.36 us -> 0.31 us  [local(): lax.ppermute(returned, 'comp', swap)]
    ppermute x6, starting transfers between devices: 15.7 us -> 20.4 us  [shifted(): return lax.ppermute(block, ALL, pairs)]
    all_to_all x1, waiting for transfers between devices: 6.48 us -> 10.4 us  [local(): gathered = lax.all_to_all(spectrum, OWNERS, 0, 0, tiled=True)]
    unnamed x58 -> x48, local copies, waits for them, and re-layouts: 14.2 us -> 10.6 us
  transfers between devices with their start and end apart: 14 -> 14, of which waited for: 8 -> 8; matrix products, arithmetic and copies ran while one was open for 17% -> 15% of each run, Pallas kernels for 18% -> 21%
where the time goes in v3:
time: 190 us; the launch traced here: 188 us
  Pallas kernels  58.4 us (31%)
  starting transfers between devices  57.3 us (30%)
  waiting for transfers between devices  35.7 us (19%)
  local copies, waits for them, and re-layouts  24.9 us (13%)
  other arithmetic  6.67 us (4%)
  matrix products  3.32 us (2%)
    pallas_call x2, Pallas kernels, ocean_block(): pl.pallas_call(functools.partial(ocean_kernel, block=block, group=group),...  33 us
    pallas_call x5, Pallas kernels, call(): pl.pallas_call(kernel, out_shape=jax.ShapeDtypeStruct(shape, jnp.bfloat16...  25.4 us
    ppermute x6, waiting for transfers between devices, shifted(): return lax.ppermute(block, ALL, pairs)  23.2 us
    ppermute x6, starting transfers between devices, shifted(): return lax.ppermute(block, ALL, pairs)  20.4 us
    all_to_all x1, starting transfers between devices, local(): gathered = lax.all_to_all(spectrum, OWNERS, 0, 0, tiled=True)  14 us
    unnamed x48, local copies, waits for them, and re-layouts  10.6 us
    all_to_all x1, waiting for transfers between devices, local(): gathered = lax.all_to_all(spectrum, OWNERS, 0, 0, tiled=True)  10.4 us
    all_to_all x1, starting transfers between devices, local(): lax.all_to_all(filtered.reshape(owners, lats, owned, width), OWNERS, 0, 0...  9.91 us
  transfers between devices with their start and end apart: 14, of which 8 were waited for; matrix products, arithmetic and copies ran while one was open for 15% of the time, Pallas kernels for 21%

profile of v3, /device:TPU:1, one launch (start us, length us, event | category | flops | bytes accessed | tf_op | source)
XLA Modules:
  0.0 187.6 jit_solution(5587369900242283598)
XLA Ops:
  3.1 3.3 %collective-permute-start = (bf16[12,64,32]{1,2,0:T(8,128)(2,1)S(1)}, bf16[12,64,32]{1,2,0:T(8,128)(2,1)S(1)}, u32[]{:S(2)}, u32[]{:S(2)}) collective-permute-start(bf16[12,64,32]{1,2,0:T(8,128)(2,1)S(1)} %broadcast_select_fusion.7), channel_id=1, source_target_pairs={{0,1},{1,0},{2,3},{3,2},{4,5},{5,4},{6,7},{7,6},{8,9},{9,8},{10,11... | collective-permute-start | bytes 147464 | tf_op jit(solution)/shard_map/ppermute | solution.py:540
  9.9 4.4 %all-to-all-start = ((bf16[8,3,64,384]{3,2,1,0:T(8,128)(2,1)}), bf16[8,3,64,384]{3,2,1,0:T(8,128)(2,1)}, u32[]{:S(2)}, u32[]{:S(2)}) async-start(bf16[8,3,64,384]{3,2,1,0:T(8,128)(2,1)} %bitcast.4), calls=%async_computation | async-start | bytes 2359296 | tf_op jit(solution)/shard_map/all_to_all | solution.py:553
  17.2 3.2 %collective-permute-start.2 = (bf16[12,16,256]{2,1,0:T(8,128)(2,1)S(1)}, bf16[12,16,256]{2,1,0:T(8,128)(2,1)S(1)}, u32[]{:S(2)}, u32[]{:S(2)}) collective-permute-start(bf16[12,16,256]{2,1,0:T(8,128)(2,1)S(1)} %get-tuple-element.54), channel_id=1, source_target_pairs={{0,2},{2,4},{4,6},{6,8},{8,10},{10,12},{12,14},{1,3},{3,5},{5,7},{... | collective-permute-start | bytes 294920 | tf_op jit(solution)/shard_map/ppermute | solution.py:482
  21.8 7.8 %collective-permute-done.2 = bf16[12,16,256]{2,1,0:T(8,128)(2,1)S(1)} collective-permute-done((bf16[12,16,256]{2,1,0:T(8,128)(2,1)S(1)}, bf16[12,16,256]{2,1,0:T(8,128)(2,1)S(1)}, u32[]{:S(2)}, u32[]{:S(2)}) %collective-permute-start.2) | collective-permute-done | bytes 98336 | tf_op jit(solution)/shard_map/ppermute | solution.py:482
  33.3 2.3 %dynamic-slice_bitcast_fusion.table_hbm = bf16[512,1024]{1,0:T(8,128)(2,1)} fusion(bf16[2,512,1024]{2,1,0:T(8,128)(2,1)} %constant.40.clone, s32[]{:T(128)S(6)} %select_n.50), kind=kLoop, calls=%fused_computation.6 | loop fusion | bytes 2097156 | tf_op jit(solution)/shard_map/jit(dynamic_index_in_dim)/squeeze | solution.py:519
  37.0 4.6 %shard_map.222 = bf16[128,3,4,384]{3,2,1,0:T(4,128)(2,1)} custom-call(bf16[512,1024]{1,0:T(8,128)(2,1)} %dynamic-slice_bitcast_fusion.table_hbm, bf16[8,3,64,384]{3,2,1,0:T(8,128)(2,1)} %all-to-all-done.own_hbm, bf16[8,3,64,384]{3,2,1,0:T(8,128)(2,1)} %copy-done.8), custom_call_target="tpu_custom_call" | custom-call | tf_op jit(solution)/shard_map/pallas_call | solution.py:199
  41.6 14.0 %all-to-all-start.1 = ((bf16[128,3,4,384]{3,2,1,0:T(4,128)(2,1)}), bf16[128,3,4,384]{3,2,1,0:T(4,128)(2,1)S(1)}, u32[]{:S(2)}, u32[]{:S(2)}) async-start(bf16[128,3,4,384]{3,2,1,0:T(4,128)(2,1)} %shard_map.222), calls=%async_computation.1 | async-start | bytes 2359296 | tf_op jit(solution)/shard_map/all_to_all | solution.py:580
  59.6 1.9 %copy.31 = bf16[384,384]{1,0:T(8,128)(2,1)} copy(bf16[384,384]{0,1:T(8,128)(2,1)} %get-tuple-element.56) | data formatting | bytes 589824 | tf_op jit(solution)/shard_map/unstack | solution.py:583
  68.1 4.3 %collective-permute-start.5 = (bf16[6,160,256]{2,1,0:T(8,128)(2,1)}, bf16[6,160,256]{2,1,0:T(8,128)(2,1)}, u32[]{:S(2)}, u32[]{:S(2)}) collective-permute-start(bf16[6,160,256]{2,1,0:T(8,128)(2,1)} %get-tuple-element.36.lower_hbm), channel_id=1, source_target_pairs={{0,1},{2,3},{4,5},{6,7},{8,9},{10,11},{12,13},{14,15},{1,16},{3,18... | collective-permute-start | bytes 1474568 | tf_op jit(solution)/shard_map/ppermute | solution.py:482
  72.4 2.1 %collective-permute-start.6 = (bf16[6,160,256]{2,1,0:T(8,128)(2,1)}, bf16[6,160,256]{2,1,0:T(8,128)(2,1)}, u32[]{:S(2)}, u32[]{:S(2)}) collective-permute-start(bf16[6,160,256]{2,1,0:T(8,128)(2,1)} %get-tuple-element.35.upper_hbm), channel_id=1, source_target_pairs={{1,0},{3,2},{5,4},{7,6},{9,8},{11,10},{13,12},{15,14},{16,1},{18,3... | collective-permute-start | bytes 1474568 | tf_op jit(solution)/shard_map/ppermute | solution.py:482
  77.3 10.4 %all-to-all-done.1 = bf16[128,3,4,384]{3,2,1,0:T(4,128)(2,1)S(1)} async-done(((bf16[128,3,4,384]{3,2,1,0:T(4,128)(2,1)}), bf16[128,3,4,384]{3,2,1,0:T(4,128)(2,1)S(1)}, u32[]{:S(2)}, u32[]{:S(2)}) %all-to-all-start.1) | async-done | bytes 1179680 | tf_op jit(solution)/shard_map/all_to_all | solution.py:580
  88.7 6.7 %shard_map.223 = bf16[384,4,384]{2,1,0:T(4,128)(2,1)} custom-call(f32[1,384]{1,0:T(1,128)} %broadcast_in_dim.24.gain_ref, bf16[384,4,384]{2,1,0:T(4,128)(2,1)} %bitcast.51, bf16[3072,384]{1,0:T(8,128)(2,1)} %fusion.2.weights_hbm), custom_call_target="tpu_custom_call" | custom-call | tf_op jit(solution)/shard_map/pallas_call | solution.py:199
  95.5 9.9 %all-to-all-start.2 = ((bf16[128,3,4,384]{3,2,1,0:T(4,128)(2,1)}), bf16[128,3,4,384]{3,2,1,0:T(4,128)(2,1)S(1)}, u32[]{:S(2)}, u32[]{:S(2)}) async-start(bf16[128,3,4,384]{3,2,1,0:T(4,128)(2,1)} %bitcast.50), calls=%async_computation.2 | async-start | bytes 2359296 | tf_op jit(solution)/shard_map/all_to_all | solution.py:605
  107.7 15.2 %shard_map.224 = (bf16[6,144,256]{2,1,0:T(8,128)(2,1)}, bf16[6,144,256]{2,1,0:T(8,128)(2,1)}) custom-call(s32[2]{0:T(128)} %pad_add_fusion.inside_ref, f32[1,256]{1,0:T(1,128)} %get-tuple-element.69.gain_ref, bf16[6,160,256]{2,1,0:T(8,128)(2,1)} %collective-permute-done.5.north_hbm, bf16[6,160,256]{2,1,0:T(8,128)(2,1)} %get-tuple-element.35.upper_hbm, ...), custom_call_target="tpu_custom_call" | custom-call | tf_op jit(solution)/shard_map/pallas_call | solution.py:439
  122.9 7.6 %collective-permute-start.7 = (bf16[6,144,256]{2,1,0:T(8,128)(2,1)}, bf16[6,144,256]{2,1,0:T(8,128)(2,1)S(1)}, u32[]{:S(2)}, u32[]{:S(2)}) collective-permute-start(bf16[6,144,256]{2,1,0:T(8,128)(2,1)} %get-tuple-element.48.lower_hbm), channel_id=1, source_target_pairs={{0,1},{2,3},{4,5},{6,7},{8,9},{10,11},{12,13},{14,15},{1,16},{3,18... | collective-permute-start | bytes 1327112 | tf_op jit(solution)/shard_map/ppermute | solution.py:482
  130.4 1.9 %collective-permute-start.8 = (bf16[6,144,256]{2,1,0:T(8,128)(2,1)}, bf16[6,144,256]{2,1,0:T(8,128)(2,1)S(1)}, u32[]{:S(2)}, u32[]{:S(2)}) collective-permute-start(bf16[6,144,256]{2,1,0:T(8,128)(2,1)} %get-tuple-element.47.upper_hbm), channel_id=1, source_target_pairs={{1,0},{3,2},{5,4},{7,6},{9,8},{11,10},{13,12},{15,14},{16,1},{18,3... | collective-permute-start | bytes 1327112 | tf_op jit(solution)/shard_map/ppermute | solution.py:482
  132.4 5.7 %collective-permute-done.7.north_hbm = bf16[6,144,256]{2,1,0:T(8,128)(2,1)S(1)} collective-permute-done((bf16[6,144,256]{2,1,0:T(8,128)(2,1)}, bf16[6,144,256]{2,1,0:T(8,128)(2,1)S(1)}, u32[]{:S(2)}, u32[]{:S(2)}) %collective-permute-start.7) | collective-permute-done | bytes 442400 | tf_op jit(solution)/shard_map/ppermute | solution.py:482
  138.0 7.9 %collective-permute-done.8.south_hbm = bf16[6,144,256]{2,1,0:T(8,128)(2,1)S(1)} collective-permute-done((bf16[6,144,256]{2,1,0:T(8,128)(2,1)}, bf16[6,144,256]{2,1,0:T(8,128)(2,1)S(1)}, u32[]{:S(2)}, u32[]{:S(2)}) %collective-permute-start.8) | collective-permute-done | bytes 442400 | tf_op jit(solution)/shard_map/ppermute | solution.py:482
  146.2 2.5 %dynamic-slice_bitcast_fusion.1.table_hbm = bf16[512,1024]{1,0:T(8,128)(2,1)} fusion(bf16[2,512,1024]{2,1,0:T(8,128)(2,1)} %constant.41.clone, s32[]{:T(128)S(6)} %select_n.50), kind=kLoop, calls=%fused_computation.7 | loop fusion | bytes 2097156 | tf_op jit(solution)/shard_map/jit(dynamic_index_in_dim)/squeeze | solution.py:520
  149.2 4.6 %shard_map.225 = bf16[8,3,64,384]{3,2,1,0:T(8,128)(2,1)} custom-call(bf16[512,1024]{1,0:T(8,128)(2,1)} %dynamic-slice_bitcast_fusion.1.table_hbm, bf16[128,3,4,384]{3,2,1,0:T(4,128)(2,1)} %copy-done.5, bf16[128,3,4,384]{3,2,1,0:T(4,128)(2,1)} %collective-permute-done.9.other_hbm), custom_call_target="tpu_custom_call" | custom-call | tf_op jit(solution)/shard_map/pallas_call | solution.py:199
  153.8 4.0 %all-to-all-start.3 = ((bf16[8,3,64,384]{3,2,1,0:T(8,128)(2,1)}), bf16[8,3,64,384]{3,2,1,0:T(8,128)(2,1)S(1)}, u32[]{:S(2)}, u32[]{:S(2)}) async-start(bf16[8,3,64,384]{3,2,1,0:T(8,128)(2,1)} %shard_map.225), calls=%async_computation.3 | async-start | bytes 2359296 | tf_op jit(solution)/shard_map/all_to_all | solution.py:621
  158.5 17.8 %shard_map.226 = bf16[12,128,256]{2,1,0:T(8,128)(2,1)} custom-call(s32[2]{0:T(128)} %pad_add_fusion.1.inside_ref, f32[1,256]{1,0:T(1,128)} %get-tuple-element.68.gain_ref, bf16[6,144,256]{2,1,0:T(8,128)(2,1)} %copy-done.11, bf16[6,144,256]{2,1,0:T(8,128)(2,1)} %get-tuple-element.47.upper_hbm, bf16[6,144,256]{2,1,0:T(8,128)(2,1)} %get-tuple-element.48.lower_hbm, ...), custom_call_target="tpu_custom_call" | custom-call | tf_op jit(solution)/shard_map/pallas_call | solution.py:439
  176.3 2.3 %broadcast_select_fusion = bf16[12,128,256]{2,1,0:T(8,128)(2,1)} fusion(bf16[12,128,256]{2,1,0:T(8,128)(2,1)} %shard_map.226, bf16[12,128,256]{2,1,0:T(8,128)(2,1)S(1)} %copy-done.4, pred[12,128]{1,0:T(8,128)(4,1)S(1)} %broadcast_compare_fusion), kind=kLoop, calls=%fused_computation.8 | loop fusion | flops 393216 | bytes 2360832 | tf_op jit(solution)/shard_map/jit(_where)/select_n | solution.py:623
  179.6 7.8 %shard_map.227 = bf16[24,64,384]{2,1,0:T(8,128)(2,1)} custom-call(f32[1,384]{1,0:T(1,128)} %get-tuple-element.67.gain_ref, bf16[32,384]{1,0:T(8,128)(2,1)} %out_weight_ref.3, bf16[1536,32]{1,0:T(8,128)(2,1)} %bitcast.47, bf16[24,64,384]{2,1,0:T(8,128)(2,1)} %atm_hbm.1, bf16[24,64,384]{2,1,0:T(8,128)(2,1)} %bitcast.52, bf16[384,768]{1,0:T(8,128)(2,1)} %up_hbm.5, ...), custom_call_target="tpu_custom_call" | custom-call | tf_op jit(solution)/shard_map/pallas_call | solution.py:199
  (97 shorter events, 34.1 us)
Async XLA Ops:
  0.6 55.5 %copy-start = (bf16[2,384,384]{2,1,0:T(8,128)(2,1)S(1)}, bf16[2,384,384]{2,1,0:T(8,128)(2,1)}, u32[]{:S(2)}) copy-start(bf16[2,384,384]{2,1,0:T(8,128)(2,1)} %param.25) | copy-start | bytes 1769476
  3.1 4.6 %collective-permute-start = (bf16[12,64,32]{1,2,0:T(8,128)(2,1)S(1)}, bf16[12,64,32]{1,2,0:T(8,128)(2,1)S(1)}, u32[]{:S(2)}, u32[]{:S(2)}) collective-permute-start(bf16[12,64,32]{1,2,0:T(8,128)(2,1)S(1)} %broadcast_select_fusion.7), channel_id=1, source_target_pairs={{0,1},{1,0},{2,3},{3,2},{4,5},{5,4},{6,7},{7,6},{8,9},{9,8},{10,11... | collective-permute-start | bytes 147464 | tf_op jit(solution)/shard_map/ppermute | solution.py:540
  9.9 22.6 %all-to-all-start = ((bf16[8,3,64,384]{3,2,1,0:T(8,128)(2,1)}), bf16[8,3,64,384]{3,2,1,0:T(8,128)(2,1)}, u32[]{:S(2)}, u32[]{:S(2)}) async-start(bf16[8,3,64,384]{3,2,1,0:T(8,128)(2,1)} %bitcast.4), calls=%async_computation | async-start | bytes 2359296 | tf_op jit(solution)/shard_map/all_to_all | solution.py:553
  15.2 1.4 collective-permute-start.1
  17.2 12.4 %collective-permute-start.2 = (bf16[12,16,256]{2,1,0:T(8,128)(2,1)S(1)}, bf16[12,16,256]{2,1,0:T(8,128)(2,1)S(1)}, u32[]{:S(2)}, u32[]{:S(2)}) collective-permute-start(bf16[12,16,256]{2,1,0:T(8,128)(2,1)S(1)} %get-tuple-element.54), channel_id=1, source_target_pairs={{0,2},{2,4},{4,6},{6,8},{8,10},{10,12},{12,14},{1,3},{3,5},{5,7},{... | collective-permute-start | bytes 294920 | tf_op jit(solution)/shard_map/ppermute | solution.py:482
  20.5 11.0 %collective-permute-start.3 = (bf16[12,16,256]{2,1,0:T(8,128)(2,1)S(1)}, bf16[12,16,256]{2,1,0:T(8,128)(2,1)S(1)}, u32[]{:S(2)}, u32[]{:S(2)}) collective-permute-start(bf16[12,16,256]{2,1,0:T(8,128)(2,1)S(1)} %get-tuple-element.55), channel_id=1, source_target_pairs={{2,0},{4,2},{6,4},{8,6},{10,8},{12,10},{14,12},{3,1},{5,3},{7,5},{... | collective-permute-start | bytes 294920 | tf_op jit(solution)/shard_map/ppermute | solution.py:482
  32.5 3.5 %collective-permute-start.4 = (bf16[8,3,64,384]{3,2,1,0:T(8,128)(2,1)}, bf16[8,3,64,384]{3,2,1,0:T(8,128)(2,1)S(1)}, u32[]{:S(2)}, u32[]{:S(2)}) collective-permute-start(bf16[8,3,64,384]{3,2,1,0:T(8,128)(2,1)} %all-to-all-done.own_hbm), channel_id=1, source_target_pairs={{0,1},{1,0},{2,3},{3,2},{4,5},{5,4},{6,7},{7,6},{8,9},{9,8},{10,11... | collective-permute-start | bytes 3538952 | tf_op jit(solution)/shard_map/ppermute | solution.py:577
  41.6 14.0 %copy-start.19 = (f32[384]{0:T(512)S(1)}, f32[384]{0:T(512)}, u32[]{:S(2)}) copy-start(f32[384]{0:T(512)} %param.26) | copy-start | bytes 4612
  41.6 14.5 %copy-start.13 = (bf16[384,384,1]{0,1,2:T(8,128)(2,1)S(1)}, bf16[384,384,1]{0,1,2:T(8,128)(2,1)}, u32[]{:S(2)}) copy-start(bf16[384,384,1]{0,1,2:T(8,128)(2,1)} %constant.47) | copy-start | bytes 884740
  41.6 46.1 %all-to-all-start.1 = ((bf16[128,3,4,384]{3,2,1,0:T(4,128)(2,1)}), bf16[128,3,4,384]{3,2,1,0:T(4,128)(2,1)S(1)}, u32[]{:S(2)}, u32[]{:S(2)}) async-start(bf16[128,3,4,384]{3,2,1,0:T(4,128)(2,1)} %shard_map.222), calls=%async_computation.1 | async-start | bytes 2359296 | tf_op jit(solution)/shard_map/all_to_all | solution.py:580
  56.8 9.8 %copy-start.9 = (bf16[384,384]{1,0:T(8,128)(2,1)S(1)}, bf16[384,384]{1,0:T(8,128)(2,1)}, u32[]{:S(2)}) copy-start(bf16[384,384]{1,0:T(8,128)(2,1)} %param.28) | copy-start | bytes 884740
  59.6 15.7 %copy-start.18 = (f32[384]{0:T(512)S(1)}, f32[384]{0:T(512)}, u32[]{:S(2)}) copy-start(f32[384]{0:T(512)} %param.29) | copy-start | bytes 4612
  61.5 13.1 %copy-start.10 = (bf16[384,384]{1,0:T(8,128)(2,1)S(1)}, bf16[384,384]{1,0:T(8,128)(2,1)}, u32[]{:S(2)}) copy-start(bf16[384,384]{1,0:T(8,128)(2,1)} %param.27) | copy-start | bytes 884740
  68.1 27.4 %collective-permute-start.5 = (bf16[6,160,256]{2,1,0:T(8,128)(2,1)}, bf16[6,160,256]{2,1,0:T(8,128)(2,1)}, u32[]{:S(2)}, u32[]{:S(2)}) collective-permute-start(bf16[6,160,256]{2,1,0:T(8,128)(2,1)} %get-tuple-element.36.lower_hbm), channel_id=1, source_target_pairs={{0,1},{2,3},{4,5},{6,7},{8,9},{10,11},{12,13},{14,15},{1,16},{3,18... | collective-permute-start | bytes 1474568 | tf_op jit(solution)/shard_map/ppermute | solution.py:482
  72.4 23.1 %collective-permute-start.6 = (bf16[6,160,256]{2,1,0:T(8,128)(2,1)}, bf16[6,160,256]{2,1,0:T(8,128)(2,1)}, u32[]{:S(2)}, u32[]{:S(2)}) collective-permute-start(bf16[6,160,256]{2,1,0:T(8,128)(2,1)} %get-tuple-element.35.upper_hbm), channel_id=1, source_target_pairs={{1,0},{3,2},{5,4},{7,6},{9,8},{11,10},{13,12},{15,14},{16,1},{18,3... | collective-permute-start | bytes 1474568 | tf_op jit(solution)/shard_map/ppermute | solution.py:482
  95.5 10.0 %copy-start.14 = (bf16[2,7,7,256]{3,0,2,1:T(2,128)(2,1)S(1)}, bf16[2,7,7,256]{3,0,2,1:T(2,128)(2,1)}, u32[]{:S(2)}) copy-start(bf16[2,7,7,256]{3,0,2,1:T(2,128)(2,1)} %param.37) | copy-start | bytes 150532
  95.5 10.7 %copy-start.20 = (f32[2,256]{1,0:T(2,128)S(1)}, f32[2,256]{1,0:T(2,128)}, u32[]{:S(2)}) copy-start(f32[2,256]{1,0:T(2,128)} %param.38) | copy-start | bytes 6148
  95.5 50.4 %all-to-all-start.2 = ((bf16[128,3,4,384]{3,2,1,0:T(4,128)(2,1)}), bf16[128,3,4,384]{3,2,1,0:T(4,128)(2,1)S(1)}, u32[]{:S(2)}, u32[]{:S(2)}) async-start(bf16[128,3,4,384]{3,2,1,0:T(4,128)(2,1)} %bitcast.50), calls=%async_computation.2 | async-start | bytes 2359296 | tf_op jit(solution)/shard_map/all_to_all | solution.py:605
  122.9 15.2 %collective-permute-start.7 = (bf16[6,144,256]{2,1,0:T(8,128)(2,1)}, bf16[6,144,256]{2,1,0:T(8,128)(2,1)S(1)}, u32[]{:S(2)}, u32[]{:S(2)}) collective-permute-start(bf16[6,144,256]{2,1,0:T(8,128)(2,1)} %get-tuple-element.48.lower_hbm), channel_id=1, source_target_pairs={{0,1},{2,3},{4,5},{6,7},{8,9},{10,11},{12,13},{14,15},{1,16},{3,18... | collective-permute-start | bytes 1327112 | tf_op jit(solution)/shard_map/ppermute | solution.py:482
  130.4 15.5 %collective-permute-start.8 = (bf16[6,144,256]{2,1,0:T(8,128)(2,1)}, bf16[6,144,256]{2,1,0:T(8,128)(2,1)S(1)}, u32[]{:S(2)}, u32[]{:S(2)}) collective-permute-start(bf16[6,144,256]{2,1,0:T(8,128)(2,1)} %get-tuple-element.47.upper_hbm), channel_id=1, source_target_pairs={{1,0},{3,2},{5,4},{7,6},{9,8},{11,10},{13,12},{15,14},{16,1},{18,3... | collective-permute-start | bytes 1327112 | tf_op jit(solution)/shard_map/ppermute | solution.py:482
  138.0 15.8 %copy-start.11 = (bf16[6,144,256]{2,1,0:T(8,128)(2,1)}, bf16[6,144,256]{2,1,0:T(8,128)(2,1)S(1)}, u32[]{:S(2)}) copy-start(bf16[6,144,256]{2,1,0:T(8,128)(2,1)S(1)} %collective-permute-done.7.north_hbm) | copy-start | bytes 1327108
  145.9 7.9 %copy-start.12 = (bf16[6,144,256]{2,1,0:T(8,128)(2,1)}, bf16[6,144,256]{2,1,0:T(8,128)(2,1)S(1)}, u32[]{:S(2)}) copy-start(bf16[6,144,256]{2,1,0:T(8,128)(2,1)S(1)} %collective-permute-done.8.south_hbm) | copy-start | bytes 1327108
  145.9 3.3 %collective-permute-start.9 = (bf16[128,3,4,384]{3,2,1,0:T(4,128)(2,1)S(1)}, bf16[128,3,4,384]{3,2,1,0:T(4,128)(2,1)}, u32[]{:S(2)}, u32[]{:S(2)}) collective-permute-start(bf16[128,3,4,384]{3,2,1,0:T(4,128)(2,1)S(1)} %all-to-all-done.2.own_hbm), channel_id=1, source_target_pairs={{0,1},{1,0},{2,3},{3,2},{4,5},{5,4},{6,7},{7,6},{8,9},{9,8},{10,11... | collective-permute-start | bytes 3538952 | tf_op jit(solution)/shard_map/ppermute | solution.py:618
  153.8 24.7 %all-to-all-start.3 = ((bf16[8,3,64,384]{3,2,1,0:T(8,128)(2,1)}), bf16[8,3,64,384]{3,2,1,0:T(8,128)(2,1)S(1)}, u32[]{:S(2)}, u32[]{:S(2)}) async-start(bf16[8,3,64,384]{3,2,1,0:T(8,128)(2,1)} %shard_map.225), calls=%async_computation.3 | async-start | bytes 2359296 | tf_op jit(solution)/shard_map/all_to_all | solution.py:621
  (11 other events, 47.4 us)

commit v4 on v2

--- a/solution.py
+++ b/solution.py
@@ -1,3 +1,4 @@
+import functools
 import math
 
 import jax
@@ -111,10 +112,39 @@
     )
 
 
+def prepare_kernel(
+    legendre_ref, moved_ref, weight_ref, real_ref, imag_ref, weighted_ref, turned_ref, mix_ref
+):
+    width = real_ref.shape[0]
+    for m in range(legendre_ref.shape[0]):
+        table = jnp.dot(legendre_ref[m], moved_ref[...], preferred_element_type=jnp.float32)
+        weighted_ref[m] = (table * weight_ref[...]).astype(jnp.bfloat16)
+        turned_ref[m] = jnp.transpose(table).astype(jnp.bfloat16)
+    mix_ref[:width, :width] = real_ref[...]
+    mix_ref[:width, width:] = imag_ref[...]
+    mix_ref[width:, :width] = -imag_ref[...]
+    mix_ref[width:, width:] = real_ref[...]
+
+
+def prepare(legendre, moved, weight, real, imag):
+    count, degrees, lats = legendre.shape
+    shapes = ((count, degrees, lats), (count, lats, degrees), (2 * real.shape[0],) * 2)
+    here = pl.BlockSpec(memory_space=pltpu.VMEM)
+    return pl.pallas_call(
+        prepare_kernel,
+        out_shape=[jax.ShapeDtypeStruct(shape, jnp.bfloat16) for shape in shapes],
+        in_specs=[here] * 5,
+        out_specs=[here] * 3,
+        compiler_params=pltpu.CompilerParams(vmem_limit_bytes=VMEM - 38_000_000),
+    )(legendre, moved, weight, real, imag)
+
+
 def filter_kernel(
     gain_ref,
     spectrum_hbm,
-    weights_hbm,
+    weighted_hbm,
+    mix_hbm,
+    turned_hbm,
     out_hbm,
     spectrum_ref,
     weighted_ref,
@@ -129,23 +159,19 @@
     block = 64
     side = block * owned
     parts = lats // block
-    targets = [weighted_ref.at[m] for m in range(count)]
-    targets += [mix_ref.at[:, h * width : (h + 1) * width] for h in range(2)]
-    targets += [turned_ref.at[m] for m in range(count)]
+    pairs = ((weighted_hbm, weighted_ref), (mix_hbm, mix_ref), (turned_hbm, turned_ref))
     arrivals = []
     for b in range(parts):
         part = pl.ds(b * block, block)
-        at = sems.at[len(targets) + b]
+        at = sems.at[len(pairs) + b]
         arrivals.append(pltpu.make_async_copy(spectrum_hbm.at[part], spectrum_ref.at[part], at))
         arrivals[-1].start()
-    fetches, at = [], 0
-    for n, target in enumerate(targets):
-        size = target.shape[0]
-        fetches.append(
-            pltpu.make_async_copy(weights_hbm.at[pl.ds(at, size)], target, sems.at[n])
-        )
-        fetches[-1].start()
-        at += size
+    fetches = [
+        pltpu.make_async_copy(source, target, sems.at[n])
+        for n, (source, target) in enumerate(pairs)
+    ]
+    for fetch in fetches:
+        fetch.start()
     r = lax.broadcasted_iota(jnp.int32, (side, side), 0)
     s = lax.broadcasted_iota(jnp.int32, (side, side), 1)
     pick = jnp.where((r % block) * owned + r // block == s, 1.0, 0.0).astype(jnp.bfloat16)
@@ -181,7 +207,7 @@
         )
         moved = jnp.dot(back, piece, preferred_element_type=jnp.float32).astype(jnp.bfloat16)
         held[span] = moved.reshape(block, owned, width)
-        at = sems.at[len(targets) + parts + b]
+        at = sems.at[len(pairs) + parts + b]
         part = pl.ds(b * block, block)
         sends.append(pltpu.make_async_copy(held.at[part], out_hbm.at[part], at))
         sends[-1].start()
@@ -330,19 +356,20 @@
 
 def ocean_kernel(
     inside_ref,
-    centre_ref,
     north_ref,
+    upper_ref,
+    lower_ref,
     south_ref,
     kern_ref,
     gain_ref,
     up_ref,
     down_ref,
-    out_ref,
-    field,
-    sums,
+    *rest,
+    block,
 ):
+    *outs, field, sums, held = rest
     at = 0
-    for ref in (north_ref, centre_ref, south_ref):
+    for ref in (north_ref, upper_ref, lower_ref, south_ref):
         for lane in range(field.shape[0]):
             field[lane, at : at + ref.shape[0]] = ref[
                 :, :, lane * LANES : (lane + 1) * LANES
@@ -350,29 +377,36 @@
         at += ref.shape[0]
     group = sums.shape[1]
     low, high = inside_ref[0], inside_ref[1]
-    ocean_rows(field, kern_ref, gain_ref, up_ref, down_ref, sums, out_ref, group, low, high)
-
-
-def ocean_block(first_col, circle, centre, north, south, kern, gain, up, down):
-    rows, cols, width = centre.shape
-    blocks, out_cols = width // LANES, cols - 2 * LEAD
-    return call(
-        ocean_kernel,
-        (rows, out_cols, width),
+    weights = (kern_ref.at[block], gain_ref, up_ref.at[block], down_ref.at[block])
+    ocean_rows(field, *weights, sums, held, group, low, high)
+    each = held.shape[0] // len(outs)
+    for n, out in enumerate(outs):
+        out[...] = held[n * each : (n + 1) * each]
+
+
+def ocean_block(first_col, circle, pieces, kern, gain, up, down, block, parts):
+    half, cols, width = pieces[0].shape
+    blocks, out_cols, rows = width // LANES, cols - 2 * LEAD, 2 * half
+    out = jax.ShapeDtypeStruct((rows // parts, out_cols, width), jnp.bfloat16)
+    here = pl.BlockSpec(memory_space=pltpu.VMEM)
+    return pl.pallas_call(
+        functools.partial(ocean_kernel, block=block),
+        out_shape=[out] * parts,
+        in_specs=[pl.BlockSpec(memory_space=pltpu.SMEM), *[here] * 8],
+        out_specs=[here] * parts,
+        scratch_shapes=[
+            pltpu.VMEM((blocks, rows + 2 * REACH, cols, LANES), jnp.float32),
+            pltpu.VMEM((blocks, 4, out_cols, LANES), jnp.float32),
+            pltpu.VMEM((rows, out_cols, width), jnp.bfloat16),
+        ],
+        compiler_params=pltpu.CompilerParams(vmem_limit_bytes=VMEM - 38_000_000),
+    )(
         jnp.stack([-first_col, circle - first_col]).astype(jnp.int32),
-        centre,
-        north,
-        south,
+        *pieces,
         kern,
-        gain,
+        gain[block : block + 1],
         up,
         down,
-        scratch=[
-            pltpu.VMEM((blocks, rows + 2 * REACH, cols, LANES), jnp.float32),
-            pltpu.VMEM((blocks, 4, out_cols, LANES), jnp.float32),
-        ],
-        scalars=1,
-        room=38_000_000,
     )
 
 
@@ -470,32 +504,41 @@
     ).astype(jnp.bfloat16)
     west = shifted(ocean_in[:, -HALO:], 0, 1)
     east = shifted(ocean_in[:, :HALO], 0, -1)
-    broad = jnp.concatenate([west, ocean_in, east], axis=1)
-    rings, broad = lax.optimization_barrier((rings, broad))
+    upper, lower = [
+        jnp.concatenate([west[part], ocean_in[part], east[part]], axis=1)
+        for part in (slice(0, REACH), slice(REACH, None))
+    ]
     seen = (order[:, None] * lats + np.arange(lats)).reshape(-1)
     moved = jnp.asarray(np.eye(lat_total)[:, seen].astype(ml_dtypes.bfloat16))
-    table = jnp.einsum(
-        "mlt,ts->mls", legendre, moved, preferred_element_type=jnp.float32
-    ).astype(jnp.bfloat16)
-    weight = quad_weight.reshape(lax.axis_size("y"), -1, lats).swapaxes(0, 1).reshape(-1)
-    weighted = (table.astype(jnp.float32) * (weight / lat_total)).astype(jnp.bfloat16)
-    turned = jnp.swapaxes(table, 1, 2)
+    weight = quad_weight.reshape(lax.axis_size("y"), -1, lats).swapaxes(0, 1).reshape(1, -1)
+    weighted, turned, mix = prepare(legendre, moved, weight / lat_total, spec_real, spec_imag)
+    gain_row = degree_gain[None]
+    rings, upper, lower, weighted, turned, mix, gain_row = lax.optimization_barrier(
+        (rings, upper, lower, weighted, turned, mix, gain_row)
+    )
+    north, south = shifted(lower, 1, 0), shifted(upper, -1, 0)
     spectrum = waves(
         (owners, lats, owned, width), forward, rings, lax.ppermute(rings, "comp", swap)
     )
-    spectrum, broad = lax.optimization_barrier((spectrum, broad))
+    spectrum, *pieces = lax.optimization_barrier((spectrum, north, upper, lower, south))
     gathered = lax.all_to_all(spectrum, OWNERS, 0, 0, tiled=True)
-    north = shifted(broad[-REACH:], 1, 0)
-    south = shifted(broad[:REACH], -1, 0)
-    weights = jnp.concatenate(
-        [*weighted, spec_real, -spec_imag, spec_imag, spec_real, *turned], axis=0
-    )
+    first_col = lax.axis_index(LON) * sea_cols
+    kernels = jnp.broadcast_to(
+        ocean_kernel.astype(jnp.float32).reshape(2, STENCIL_TAPS**2, 1, sea_width),
+        (2, STENCIL_TAPS**2, 8, sea_width),
+    )
+    ocean = (kernels, ocean_gain, ocean_up, ocean_down)
+    upper, lower = ocean_block(first_col - LEAD, circle, pieces, *ocean, 0, 2)
+    gathered, upper, lower = lax.optimization_barrier((gathered, upper, lower))
+    north, south = shifted(lower, 1, 0), shifted(upper, -1, 0)
     filtered = call(
         filter_kernel,
         (lat_total, owned, width),
-        degree_gain[None],
+        gain_row,
         gathered.reshape(lat_total, owned, width),
-        weights,
+        weighted,
+        mix,
+        turned,
         scratch=[
             pltpu.VMEM((lat_total, owned, width), jnp.bfloat16),
             pltpu.VMEM(weighted.shape, jnp.bfloat16),
@@ -503,36 +546,23 @@
             pltpu.VMEM(turned.shape, jnp.bfloat16),
             pltpu.VMEM((owned // 2, lat_total, 2 * width), jnp.bfloat16),
             pltpu.VMEM((lat_total, owned, width), jnp.bfloat16),
-            pltpu.SemaphoreType.DMA((6 + lat_total // 64 * 2,)),
+            pltpu.SemaphoreType.DMA((3 + lat_total // 64 * 2,)),
         ],
-        behind=2,
+        behind=4,
         away=True,
-        room=100000,
-    )
-    filtered, broad, north, south = lax.optimization_barrier((filtered, broad, north, south))
+        room=100_000,
+    )
+    filtered, *pieces = lax.optimization_barrier((filtered, north, upper, lower, south))
     returned = lax.all_to_all(
         filtered.reshape(owners, lats, owned, width), OWNERS, 0, 0, tiled=True
     )
-    first_col = lax.axis_index(LON) * sea_cols
-    kernels = jnp.broadcast_to(
-        ocean_kernel.astype(jnp.float32).reshape(2, STENCIL_TAPS**2, 1, sea_width),
-        (2, STENCIL_TAPS**2, 8, sea_width),
-    )
-    blocks = [
-        (kernels[k], ocean_gain[k : k + 1], ocean_up[k], ocean_down[k]) for k in range(2)
-    ]
-    first = ocean_block(first_col - LEAD, circle, broad, north, south, *blocks[0])
-    returned, first = lax.optimization_barrier((returned, first))
+    (current,) = ocean_block(first_col, circle, pieces, *ocean, 1, 1)
+    ocean_out = jnp.where(wet_mask[:, :, None] == 1, current, ocean_state)
+    returned, ocean_out = lax.optimization_barrier((returned, ocean_out))
     spatial = waves(
         (lon_count, lats, lon_dev, width), inverse, returned, lax.ppermute(returned, "comp", swap)
     )
-    north = shifted(first[-REACH:], 1, 0)
-    south = shifted(first[:REACH], -1, 0)
-    spatial, first, north, south = lax.optimization_barrier((spatial, first, north, south))
     spectral = lax.all_to_all(spatial, LON, 0, 0, tiled=True).reshape(lat_dev, lon_dev, width)
-    current = ocean_block(first_col, circle, first, north, south, *blocks[1])
-    ocean_out = jnp.where(wet_mask[:, :, None] == 1, current, ocean_state)
-    spectral, ocean_out = lax.optimization_barrier((spectral, ocean_out))
     atm_out = epilogue(
         atm_state, flux_here, spectral, surface_to_atm, atm_gain[1:], atm_up, atm_down
     )

time: 189 us -> 197 us (1.042)
  blocking collectives: 0 us -> 20.1 us
  local copies, waits for them, and re-layouts: 34 us -> 20.5 us
  waiting for transfers between devices: 36 us -> 48.7 us
  starting transfers between devices: 61.3 us -> 50.1 us
    pallas_call x0 -> x3, Pallas kernels: none -> 25 us  [the longest x2 24.3 us: ocean_block(): pl.pallas_call(functools.partial(ocean_kernel, block=block), out_shape=[o...]
    pallas_call x6 -> x4, Pallas kernels: 41 us -> 17.6 us  [call(): pl.pallas_call(kernel, out_shape=jax.ShapeDtypeStruct(shape, jnp.bfloat16...]
    all_to_all x0 -> x1, blocking collectives: none -> 20.1 us  [local(): lax.all_to_all(spatial, LON, 0, 0, tiled=True)]
    all_to_all x1, waiting for transfers between devices: 6.48 us -> 14.5 us  [local(): gathered = lax.all_to_all(spectrum, OWNERS, 0, 0, tiled=True)]
    ppermute x6, waiting for transfers between devices: 14.3 us -> 19.8 us  [shifted(): return lax.ppermute(block, ALL, pairs)]
    ppermute x1, starting transfers between devices: 5.36 us -> 0.01 us  [local(): lax.ppermute(returned, 'comp', swap)]
    another operation x3 -> x0, local copies, waits for them, and re-layouts: 4.56 us -> none  [local(): weights = jnp.concatenate([*weighted, spec_real, -spec_imag, spec_imag, s...]
    all_to_all x1 -> x0, starting transfers between devices: 4.25 us -> none  [local(): lax.all_to_all(spatial, LON, 0, 0, tiled=True)]
  transfers between devices with their start and end apart: 14 -> 13, of which waited for: 8 -> 8; matrix products, arithmetic and copies ran while one was open for 17% -> 5% of each run, Pallas kernels for 18% -> 18%
where the time goes in v4:
time: 197 us; the launch traced here: 196 us
  starting transfers between devices  50.1 us (25%)
  Pallas kernels  49.1 us (25%)
  waiting for transfers between devices  48.7 us (25%)
  local copies, waits for them, and re-layouts  20.5 us (10%)
  blocking collectives  20.1 us (10%)
  other arithmetic  3.05 us (2%)
  matrix products  2.93 us (1%)
    pallas_call x2, Pallas kernels, ocean_block(): pl.pallas_call(functools.partial(ocean_kernel, block=block), out_shape=[o...  24.3 us
    all_to_all x1, blocking collectives, local(): lax.all_to_all(spatial, LON, 0, 0, tiled=True)  20.1 us
    ppermute x6, waiting for transfers between devices, shifted(): return lax.ppermute(block, ALL, pairs)  19.8 us
    pallas_call x4, Pallas kernels, call(): pl.pallas_call(kernel, out_shape=jax.ShapeDtypeStruct(shape, jnp.bfloat16...  17.6 us
    ppermute x6, starting transfers between devices, shifted(): return lax.ppermute(block, ALL, pairs)  15.8 us
    all_to_all x1, waiting for transfers between devices, local(): gathered = lax.all_to_all(spectrum, OWNERS, 0, 0, tiled=True)  14.5 us
    all_to_all x1, starting transfers between devices, local(): gathered = lax.all_to_all(spectrum, OWNERS, 0, 0, tiled=True)  13.8 us
    unnamed x72, local copies, waits for them, and re-layouts  13.7 us
  transfers between devices with their start and end apart: 13, of which 8 were waited for; matrix products, arithmetic and copies ran while one was open for 5% of the time, Pallas kernels for 18%

profile of v4, /device:TPU:1, one launch (start us, length us, event | category | flops | bytes accessed | tf_op | source)
XLA Modules:
  0.0 195.7 jit_solution(6043336561022046038)
XLA Ops:
  3.0 3.3 %collective-permute-start = (bf16[12,64,32]{1,2,0:T(8,128)(2,1)S(1)}, bf16[12,64,32]{1,2,0:T(8,128)(2,1)S(1)}, u32[]{:S(2)}, u32[]{:S(2)}) collective-permute-start(bf16[12,64,32]{1,2,0:T(8,128)(2,1)S(1)} %broadcast_select_fusion.7), channel_id=1, source_target_pairs={{0,1},{1,0},{2,3},{3,2},{4,5},{5,4},{6,7},{7,6},{8,9},{9,8},{10,11... | collective-permute-start | bytes 147464 | tf_op jit(solution)/shard_map/ppermute | solution.py:484
  7.7 1.8 shard_map.221
  9.5 4.3 %all-to-all-start = ((bf16[8,3,64,384]{3,2,1,0:T(8,128)(2,1)}), bf16[8,3,64,384]{3,2,1,0:T(8,128)(2,1)}, u32[]{:S(2)}, u32[]{:S(2)}) async-start(bf16[8,3,64,384]{3,2,1,0:T(8,128)(2,1)} %bitcast.3), calls=%async_computation | async-start | bytes 2359296 | tf_op jit(solution)/shard_map/all_to_all | solution.py:497
  19.6 3.5 %collective-permute-start.2 = (bf16[12,16,256]{2,1,0:T(8,128)(2,1)S(1)}, bf16[12,16,256]{2,1,0:T(8,128)(2,1)S(1)}, u32[]{:S(2)}, u32[]{:S(2)}) collective-permute-start(bf16[12,16,256]{2,1,0:T(8,128)(2,1)S(1)} %get-tuple-element.58), channel_id=1, source_target_pairs={{0,2},{2,4},{4,6},{6,8},{8,10},{10,12},{12,14},{1,3},{3,5},{5,7},{... | collective-permute-start | bytes 294920 | tf_op jit(solution)/shard_map/ppermute | solution.py:426
  24.5 4.3 %collective-permute-done.2 = bf16[12,16,256]{2,1,0:T(8,128)(2,1)S(1)} collective-permute-done((bf16[12,16,256]{2,1,0:T(8,128)(2,1)S(1)}, bf16[12,16,256]{2,1,0:T(8,128)(2,1)S(1)}, u32[]{:S(2)}, u32[]{:S(2)}) %collective-permute-start.2) | collective-permute-done | bytes 98336 | tf_op jit(solution)/shard_map/ppermute | solution.py:426
  31.9 4.3 %collective-permute-start.5 = (bf16[6,160,256]{2,1,0:T(8,128)(2,1)S(1)}, bf16[6,160,256]{2,1,0:T(8,128)(2,1)S(1)}, u32[]{:S(2)}, u32[]{:S(2)}) collective-permute-start(bf16[6,160,256]{2,1,0:T(8,128)(2,1)S(1)} %get-tuple-element.39.lower_ref), channel_id=1, source_target_pairs={{0,1},{2,3},{4,5},{6,7},{8,9},{10,11},{12,13},{14,15},{1,16},{3,18... | collective-permute-start | bytes 1474568 | tf_op jit(solution)/shard_map/ppermute | solution.py:426
  36.2 1.9 collective-permute-start.6
  38.2 2.3 %dynamic-slice_bitcast_fusion.table_hbm = bf16[512,1024]{1,0:T(8,128)(2,1)} fusion(bf16[2,512,1024]{2,1,0:T(8,128)(2,1)} %constant.40.clone, s32[]{:T(128)S(6)} %select_n.50), kind=kLoop, calls=%fused_computation.4 | loop fusion | bytes 2097156 | tf_op jit(solution)/shard_map/jit(dynamic_index_in_dim)/squeeze | solution.py:463
  40.5 4.5 %shard_map.223 = bf16[128,3,4,384]{3,2,1,0:T(4,128)(2,1)} custom-call(bf16[512,1024]{1,0:T(8,128)(2,1)} %dynamic-slice_bitcast_fusion.table_hbm, bf16[8,3,64,384]{3,2,1,0:T(8,128)(2,1)} %all-to-all-done.own_hbm, bf16[8,3,64,384]{3,2,1,0:T(8,128)(2,1)} %collective-permute-done.4.other_hbm), custom_call_target="tpu_custom_call" | custom-call | tf_op jit(solution)/shard_map/pallas_call | solution.py:224
  45.1 7.6 %collective-permute-done.6.south_ref = bf16[6,160,256]{2,1,0:T(8,128)(2,1)} collective-permute-done((bf16[6,160,256]{2,1,0:T(8,128)(2,1)S(1)}, bf16[6,160,256]{2,1,0:T(8,128)(2,1)}, u32[]{:S(2)}, u32[]{:S(2)}) %collective-permute-start.6) | collective-permute-done | bytes 491552 | tf_op jit(solution)/shard_map/ppermute | solution.py:426
  52.7 13.8 %all-to-all-start.1 = ((bf16[128,3,4,384]{3,2,1,0:T(4,128)(2,1)}), bf16[128,3,4,384]{3,2,1,0:T(4,128)(2,1)}, u32[]{:S(2)}, u32[]{:S(2)}) async-start(bf16[128,3,4,384]{3,2,1,0:T(4,128)(2,1)} %shard_map.223), calls=%async_computation.1 | async-start | bytes 2359296 | tf_op jit(solution)/shard_map/all_to_all | solution.py:524
  72.0 11.2 %shard_map.224 = (bf16[6,144,256]{2,1,0:T(8,128)(2,1)S(1)}, bf16[6,144,256]{2,1,0:T(8,128)(2,1)S(1)}) custom-call(s32[2]{0:T(128)S(1)} %pad_add_fusion.inside_ref, bf16[6,160,256]{2,1,0:T(8,128)(2,1)S(1)} %copy-done.16, bf16[6,160,256]{2,1,0:T(8,128)(2,1)S(1)} %copy-done.6, bf16[6,160,256]{2,1,0:T(8,128)(2,1)S(1)} %copy-done.8, ...), custom_call_target="tpu_custom_call" | custom-call | tf_op jit(solution)/shard_map/pallas_call | solution.py:392
  84.8 14.5 %all-to-all-done.1 = bf16[128,3,4,384]{3,2,1,0:T(4,128)(2,1)} async-done(((bf16[128,3,4,384]{3,2,1,0:T(4,128)(2,1)}), bf16[128,3,4,384]{3,2,1,0:T(4,128)(2,1)}, u32[]{:S(2)}, u32[]{:S(2)}) %all-to-all-start.1) | async-done | bytes 1179680 | tf_op jit(solution)/shard_map/all_to_all | solution.py:524
  99.3 2.9 %collective-permute-start.7 = (bf16[6,144,256]{2,1,0:T(8,128)(2,1)}, bf16[6,144,256]{2,1,0:T(8,128)(2,1)S(1)}, u32[]{:S(2)}, u32[]{:S(2)}) collective-permute-start(bf16[6,144,256]{2,1,0:T(8,128)(2,1)} %copy-done.19), channel_id=1, source_target_pairs={{0,1},{2,3},{4,5},{6,7},{8,9},{10,11},{12,13},{14,15},{1,16},{3,18... | collective-permute-start | bytes 1327112 | tf_op jit(solution)/shard_map/ppermute | solution.py:426
  102.2 1.9 collective-permute-start.8
  104.1 6.7 %shard_map.225 = bf16[384,4,384]{2,1,0:T(4,128)(2,1)} custom-call(f32[1,384]{1,0:T(1,128)} %broadcast_in_dim.23.gain_ref, bf16[384,4,384]{2,1,0:T(4,128)(2,1)} %bitcast.11.spectrum_hbm, bf16[2,384,384]{2,1,0:T(8,128)(2,1)} %copy-done.13, bf16[768,768]{1,0:T(8,128)(2,1)} %copy-done.9, bf16[2,384,384]{2,1,0:T(8,128)(2,1)} %copy-done.14), custom_call_target="tpu_custom_call" | custom-call | tf_op jit(solution)/shard_map/pallas_call | solution.py:224
  111.6 6.2 %collective-permute-done.8.south_ref = bf16[6,144,256]{2,1,0:T(8,128)(2,1)} collective-permute-done((bf16[6,144,256]{2,1,0:T(8,128)(2,1)}, bf16[6,144,256]{2,1,0:T(8,128)(2,1)}, u32[]{:S(2)}, u32[]{:S(2)}) %collective-permute-start.8) | collective-permute-done | bytes 442400 | tf_op jit(solution)/shard_map/ppermute | solution.py:426
  117.8 11.3 %all-to-all-start.2 = ((bf16[128,3,4,384]{3,2,1,0:T(4,128)(2,1)}), bf16[128,3,4,384]{3,2,1,0:T(4,128)(2,1)}, u32[]{:S(2)}, u32[]{:S(2)}) async-start(bf16[128,3,4,384]{3,2,1,0:T(4,128)(2,1)} %bitcast.31), calls=%async_computation.2 | async-start | bytes 2359296 | tf_op jit(solution)/shard_map/all_to_all | solution.py:556
  133.4 13.1 %shard_map.226 = bf16[12,128,256]{2,1,0:T(8,128)(2,1)S(1)} custom-call(s32[2]{0:T(128)S(1)} %pad_add_fusion.1.inside_ref, bf16[6,144,256]{2,1,0:T(8,128)(2,1)S(1)} %copy-done.22, bf16[6,144,256]{2,1,0:T(8,128)(2,1)S(1)} %copy-done.18, bf16[6,144,256]{2,1,0:T(8,128)(2,1)S(1)} %copy-done.20, bf16[6,144,256]{2,1,0:T(8,128)(2,1)} %collective-permute-done.8.south_ref, ...), custom_call_target="tpu_custom_call" | custom-call | tf_op jit(solution)/shard_map/pallas_call | solution.py:392
  147.7 12.7 %all-to-all-done.2.own_hbm = bf16[128,3,4,384]{3,2,1,0:T(4,128)(2,1)} async-done(((bf16[128,3,4,384]{3,2,1,0:T(4,128)(2,1)}), bf16[128,3,4,384]{3,2,1,0:T(4,128)(2,1)}, u32[]{:S(2)}, u32[]{:S(2)}) %all-to-all-start.2) | async-done | bytes 1179680 | tf_op jit(solution)/shard_map/all_to_all | solution.py:556
  160.4 2.3 %dynamic-slice_bitcast_fusion.1.table_hbm = bf16[512,1024]{1,0:T(8,128)(2,1)} fusion(bf16[2,512,1024]{2,1,0:T(8,128)(2,1)} %constant.41.clone, s32[]{:T(128)S(6)} %select_n.50), kind=kLoop, calls=%fused_computation.5 | loop fusion | bytes 2097156 | tf_op jit(solution)/shard_map/jit(dynamic_index_in_dim)/squeeze | solution.py:464
  164.5 4.5 %shard_map.227 = bf16[8,3,64,384]{3,2,1,0:T(8,128)(2,1)} custom-call(bf16[512,1024]{1,0:T(8,128)(2,1)} %dynamic-slice_bitcast_fusion.1.table_hbm, bf16[128,3,4,384]{3,2,1,0:T(4,128)(2,1)} %all-to-all-done.2.own_hbm, bf16[128,3,4,384]{3,2,1,0:T(4,128)(2,1)} %copy-done.29), custom_call_target="tpu_custom_call" | custom-call | tf_op jit(solution)/shard_map/pallas_call | solution.py:224
  169.1 20.1 %all_to_all.20 = bf16[8,3,64,384]{3,2,1,0:T(8,128)(2,1)S(1)} all-to-all(bf16[8,3,64,384]{3,2,1,0:T(8,128)(2,1)} %shard_map.227), channel_id=1, replica_groups=mesh['y'=4,'z_hi'=4,'z_lo'=2,'x'=4,'comp'=2] {'z_lo','x'}, dimensions={0} | all-to-all | bytes 2359296 | tf_op jit(solution)/shard_map/all_to_all | solution.py:565
  189.1 6.6 %shard_map.228 = bf16[24,64,384]{2,1,0:T(8,128)(2,1)} custom-call(bf16[24,64,384]{2,1,0:T(8,128)(2,1)S(1)} %copy-done.1, bf16[1536,32]{1,0:T(8,128)(2,1)S(1)} %bitcast.30, bf16[24,64,384]{2,1,0:T(8,128)(2,1)S(1)} %bitcast.28, bf16[32,384]{1,0:T(8,128)(2,1)S(1)} %copy-done.26, f32[1,384]{1,0:T(1,128)S(1)} %get-tuple-element.68.gain_ref, ...), custom_call_target="tpu_custom_call" | custom-call | tf_op jit(solution)/shard_map/pallas_call | solution.py:290
  (114 shorter events, 28.9 us)
Async XLA Ops:
  0.6 13.2 %copy-start = (bf16[384,32]{0,1:T(8,128)(2,1)S(1)}, bf16[384,32]{0,1:T(8,128)(2,1)}, u32[]{:S(2)}) copy-start(bf16[384,32]{0,1:T(8,128)(2,1)} %param.33) | copy-start | bytes 73732
  1.4 6.4 %copy-start.26 = (bf16[32,384]{1,0:T(8,128)(2,1)S(1)}, bf16[32,384]{1,0:T(8,128)(2,1)}, u32[]{:S(2)}) copy-start(bf16[32,384]{1,0:T(8,128)(2,1)} %out_weight_ref.3) | copy-start | bytes 73732
  3.0 4.3 %collective-permute-start = (bf16[12,64,32]{1,2,0:T(8,128)(2,1)S(1)}, bf16[12,64,32]{1,2,0:T(8,128)(2,1)S(1)}, u32[]{:S(2)}, u32[]{:S(2)}) collective-permute-start(bf16[12,64,32]{1,2,0:T(8,128)(2,1)S(1)} %broadcast_select_fusion.7), channel_id=1, source_target_pairs={{0,1},{1,0},{2,3},{3,2},{4,5},{5,4},{6,7},{7,6},{8,9},{9,8},{10,11... | collective-permute-start | bytes 147464 | tf_op jit(solution)/shard_map/ppermute | solution.py:484
  9.5 21.1 %all-to-all-start = ((bf16[8,3,64,384]{3,2,1,0:T(8,128)(2,1)}), bf16[8,3,64,384]{3,2,1,0:T(8,128)(2,1)}, u32[]{:S(2)}, u32[]{:S(2)}) async-start(bf16[8,3,64,384]{3,2,1,0:T(8,128)(2,1)} %bitcast.3), calls=%async_computation | async-start | bytes 2359296 | tf_op jit(solution)/shard_map/all_to_all | solution.py:497
  15.4 2.9 %collective-permute-start.1 = (bf16[12,64,32]{1,2,0:T(8,128)(2,1)}, bf16[12,64,32]{1,2,0:T(8,128)(2,1)S(1)}, u32[]{:S(2)}, u32[]{:S(2)}) collective-permute-start(bf16[12,64,32]{1,2,0:T(8,128)(2,1)} %broadcast_select_fusion.3), channel_id=1, source_target_pairs={{0,1},{1,0},{2,3},{3,2},{4,5},{5,4},{6,7},{7,6},{8,9},{9,8},{10,11... | collective-permute-start | bytes 147464 | tf_op jit(solution)/shard_map/ppermute | solution.py:500
  19.6 9.2 %collective-permute-start.2 = (bf16[12,16,256]{2,1,0:T(8,128)(2,1)S(1)}, bf16[12,16,256]{2,1,0:T(8,128)(2,1)S(1)}, u32[]{:S(2)}, u32[]{:S(2)}) collective-permute-start(bf16[12,16,256]{2,1,0:T(8,128)(2,1)S(1)} %get-tuple-element.58), channel_id=1, source_target_pairs={{0,2},{2,4},{4,6},{6,8},{8,10},{10,12},{12,14},{1,3},{3,5},{5,7},{... | collective-permute-start | bytes 294920 | tf_op jit(solution)/shard_map/ppermute | solution.py:426
  23.2 7.4 %collective-permute-start.3 = (bf16[12,16,256]{2,1,0:T(8,128)(2,1)S(1)}, bf16[12,16,256]{2,1,0:T(8,128)(2,1)S(1)}, u32[]{:S(2)}, u32[]{:S(2)}) collective-permute-start(bf16[12,16,256]{2,1,0:T(8,128)(2,1)S(1)} %get-tuple-element.59), channel_id=1, source_target_pairs={{2,0},{4,2},{6,4},{8,6},{10,8},{12,10},{14,12},{3,1},{5,3},{7,5},{... | collective-permute-start | bytes 294920 | tf_op jit(solution)/shard_map/ppermute | solution.py:426
  30.6 14.3 %copy-start.5 = (bf16[6,160,256]{2,1,0:T(8,128)(2,1)}, bf16[6,160,256]{2,1,0:T(8,128)(2,1)S(1)}, u32[]{:S(2)}) copy-start(bf16[6,160,256]{2,1,0:T(8,128)(2,1)S(1)} %get-tuple-element.38.upper_ref) | copy-start | bytes 1474564
  30.7 14.3 %copy-start.7 = (bf16[6,160,256]{2,1,0:T(8,128)(2,1)}, bf16[6,160,256]{2,1,0:T(8,128)(2,1)S(1)}, u32[]{:S(2)}) copy-start(bf16[6,160,256]{2,1,0:T(8,128)(2,1)S(1)} %get-tuple-element.39.lower_ref) | copy-start | bytes 1474564
  30.7 9.8 %collective-permute-start.4 = (bf16[8,3,64,384]{3,2,1,0:T(8,128)(2,1)}, bf16[8,3,64,384]{3,2,1,0:T(8,128)(2,1)}, u32[]{:S(2)}, u32[]{:S(2)}) collective-permute-start(bf16[8,3,64,384]{3,2,1,0:T(8,128)(2,1)} %all-to-all-done.own_hbm), channel_id=1, source_target_pairs={{0,1},{1,0},{2,3},{3,2},{4,5},{5,4},{6,7},{7,6},{8,9},{9,8},{10,11... | collective-permute-start | bytes 3538952 | tf_op jit(solution)/shard_map/ppermute | solution.py:521
  31.9 13.1 %collective-permute-start.5 = (bf16[6,160,256]{2,1,0:T(8,128)(2,1)S(1)}, bf16[6,160,256]{2,1,0:T(8,128)(2,1)S(1)}, u32[]{:S(2)}, u32[]{:S(2)}) collective-permute-start(bf16[6,160,256]{2,1,0:T(8,128)(2,1)S(1)} %get-tuple-element.39.lower_ref), channel_id=1, source_target_pairs={{0,1},{2,3},{4,5},{6,7},{8,9},{10,11},{12,13},{14,15},{1,16},{3,18... | collective-permute-start | bytes 1474568 | tf_op jit(solution)/shard_map/ppermute | solution.py:426
  36.2 16.4 %collective-permute-start.6 = (bf16[6,160,256]{2,1,0:T(8,128)(2,1)S(1)}, bf16[6,160,256]{2,1,0:T(8,128)(2,1)}, u32[]{:S(2)}, u32[]{:S(2)}) collective-permute-start(bf16[6,160,256]{2,1,0:T(8,128)(2,1)S(1)} %get-tuple-element.38.upper_ref), channel_id=1, source_target_pairs={{1,0},{3,2},{5,4},{7,6},{9,8},{11,10},{13,12},{15,14},{16,1},{18,3... | collective-permute-start | bytes 1474568 | tf_op jit(solution)/shard_map/ppermute | solution.py:426
  45.0 21.5 %copy-start.30 = (bf16[2,7,7,256]{3,0,2,1:T(2,128)(2,1)S(1)}, bf16[2,7,7,256]{3,0,2,1:T(2,128)(2,1)}, u32[]{:S(2)}) copy-start(bf16[2,7,7,256]{3,0,2,1:T(2,128)(2,1)} %param.37) | copy-start | bytes 150532
  45.0 21.6 %copy-start.35 = (f32[2,256]{1,0:T(2,128)S(1)}, f32[2,256]{1,0:T(2,128)}, u32[]{:S(2)}) copy-start(f32[2,256]{1,0:T(2,128)} %param.38) | copy-start | bytes 6148
  45.0 7.6 %copy-start.15 = (bf16[6,160,256]{2,1,0:T(8,128)(2,1)}, bf16[6,160,256]{2,1,0:T(8,128)(2,1)S(1)}, u32[]{:S(2)}) copy-start(bf16[6,160,256]{2,1,0:T(8,128)(2,1)S(1)} %collective-permute-done.5.north_ref) | copy-start | bytes 1474564
  52.7 46.6 %all-to-all-start.1 = ((bf16[128,3,4,384]{3,2,1,0:T(4,128)(2,1)}), bf16[128,3,4,384]{3,2,1,0:T(4,128)(2,1)}, u32[]{:S(2)}, u32[]{:S(2)}) async-start(bf16[128,3,4,384]{3,2,1,0:T(4,128)(2,1)} %shard_map.223), calls=%async_computation.1 | async-start | bytes 2359296 | tf_op jit(solution)/shard_map/all_to_all | solution.py:524
  99.3 11.6 %collective-permute-start.7 = (bf16[6,144,256]{2,1,0:T(8,128)(2,1)}, bf16[6,144,256]{2,1,0:T(8,128)(2,1)S(1)}, u32[]{:S(2)}, u32[]{:S(2)}) collective-permute-start(bf16[6,144,256]{2,1,0:T(8,128)(2,1)} %copy-done.19), channel_id=1, source_target_pairs={{0,1},{2,3},{4,5},{6,7},{8,9},{10,11},{12,13},{14,15},{1,16},{3,18... | collective-permute-start | bytes 1327112 | tf_op jit(solution)/shard_map/ppermute | solution.py:426
  102.2 15.6 %collective-permute-start.8 = (bf16[6,144,256]{2,1,0:T(8,128)(2,1)}, bf16[6,144,256]{2,1,0:T(8,128)(2,1)}, u32[]{:S(2)}, u32[]{:S(2)}) collective-permute-start(bf16[6,144,256]{2,1,0:T(8,128)(2,1)} %copy-done.17), channel_id=1, source_target_pairs={{1,0},{3,2},{5,4},{7,6},{9,8},{11,10},{13,12},{15,14},{16,1},{18,3... | collective-permute-start | bytes 1327112 | tf_op jit(solution)/shard_map/ppermute | solution.py:426
  117.8 11.4 %copy-start.31 = (s32[12,128]{1,0:T(8,128)S(1)}, s32[12,128]{1,0:T(8,128)}, u32[]{:S(2)}) copy-start(s32[12,128]{1,0:T(8,128)} %param.24) | copy-start | bytes 18436
  117.8 42.6 %all-to-all-start.2 = ((bf16[128,3,4,384]{3,2,1,0:T(4,128)(2,1)}), bf16[128,3,4,384]{3,2,1,0:T(4,128)(2,1)}, u32[]{:S(2)}, u32[]{:S(2)}) async-start(bf16[128,3,4,384]{3,2,1,0:T(4,128)(2,1)} %bitcast.31), calls=%async_computation.2 | async-start | bytes 2359296 | tf_op jit(solution)/shard_map/all_to_all | solution.py:556
  133.4 13.1 %copy-start.28 = (bf16[12,128,256]{2,1,0:T(8,128)(2,1)S(1)}, bf16[12,128,256]{2,1,0:T(8,128)(2,1)}, u32[]{:S(2)}) copy-start(bf16[12,128,256]{2,1,0:T(8,128)(2,1)} %param.23) | copy-start | bytes 2359300
  160.4 3.1 %collective-permute-start.9 = (bf16[128,3,4,384]{3,2,1,0:T(4,128)(2,1)}, bf16[128,3,4,384]{3,2,1,0:T(4,128)(2,1)S(1)}, u32[]{:S(2)}, u32[]{:S(2)}) collective-permute-start(bf16[128,3,4,384]{3,2,1,0:T(4,128)(2,1)} %all-to-all-done.2.own_hbm), channel_id=1, source_target_pairs={{0,1},{1,0},{2,3},{3,2},{4,5},{5,4},{6,7},{7,6},{8,9},{9,8},{10,11... | collective-permute-start | bytes 3538952 | tf_op jit(solution)/shard_map/ppermute | solution.py:563
  169.0 20.1 %copy-start.10 = (bf16[384,768]{1,0:T(8,128)(2,1)S(1)}, bf16[384,768]{1,0:T(8,128)(2,1)}, u32[]{:S(2)}) copy-start(bf16[384,768]{1,0:T(8,128)(2,1)} %up_ref.5) | copy-start | bytes 1769476
  169.0 20.1 %copy-start.11 = (bf16[768,384]{1,0:T(8,128)(2,1)S(1)}, bf16[768,384]{1,0:T(8,128)(2,1)}, u32[]{:S(2)}) copy-start(bf16[768,384]{1,0:T(8,128)(2,1)} %down_ref.5) | copy-start | bytes 1769476
  (25 other events, 50.6 us)

commit v5 on v4

--- a/solution.py
+++ b/solution.py
@@ -516,11 +516,10 @@
     rings, upper, lower, weighted, turned, mix, gain_row = lax.optimization_barrier(
         (rings, upper, lower, weighted, turned, mix, gain_row)
     )
-    north, south = shifted(lower, 1, 0), shifted(upper, -1, 0)
     spectrum = waves(
         (owners, lats, owned, width), forward, rings, lax.ppermute(rings, "comp", swap)
     )
-    spectrum, *pieces = lax.optimization_barrier((spectrum, north, upper, lower, south))
+    spectrum, upper, lower = lax.optimization_barrier((spectrum, upper, lower))
     gathered = lax.all_to_all(spectrum, OWNERS, 0, 0, tiled=True)
     first_col = lax.axis_index(LON) * sea_cols
     kernels = jnp.broadcast_to(
@@ -528,8 +527,6 @@
         (2, STENCIL_TAPS**2, 8, sea_width),
     )
     ocean = (kernels, ocean_gain, ocean_up, ocean_down)
-    upper, lower = ocean_block(first_col - LEAD, circle, pieces, *ocean, 0, 2)
-    gathered, upper, lower = lax.optimization_barrier((gathered, upper, lower))
     north, south = shifted(lower, 1, 0), shifted(upper, -1, 0)
     filtered = call(
         filter_kernel,
@@ -556,13 +553,17 @@
     returned = lax.all_to_all(
         filtered.reshape(owners, lats, owned, width), OWNERS, 0, 0, tiled=True
     )
+    upper, lower = ocean_block(first_col - LEAD, circle, pieces, *ocean, 0, 2)
+    north, south = shifted(lower, 1, 0), shifted(upper, -1, 0)
+    returned, *pieces = lax.optimization_barrier((returned, north, upper, lower, south))
+    spatial = waves(
+        (lon_count, lats, lon_dev, width), inverse, returned, lax.ppermute(returned, "comp", swap)
+    )
+    spatial, *pieces = lax.optimization_barrier((spatial, *pieces))
+    spectral = lax.all_to_all(spatial, LON, 0, 0, tiled=True).reshape(lat_dev, lon_dev, width)
     (current,) = ocean_block(first_col, circle, pieces, *ocean, 1, 1)
     ocean_out = jnp.where(wet_mask[:, :, None] == 1, current, ocean_state)
-    returned, ocean_out = lax.optimization_barrier((returned, ocean_out))
-    spatial = waves(
-        (lon_count, lats, lon_dev, width), inverse, returned, lax.ppermute(returned, "comp", swap)
-    )
-    spectral = lax.all_to_all(spatial, LON, 0, 0, tiled=True).reshape(lat_dev, lon_dev, width)
+    spectral, ocean_out = lax.optimization_barrier((spectral, ocean_out))
     atm_out = epilogue(
         atm_state, flux_here, spectral, surface_to_atm, atm_gain[1:], atm_up, atm_down
     )

time: 197 us -> 191 us (0.970)
  blocking collectives: 20.1 us -> 0 us
  starting transfers between devices: 50.1 us -> 60.7 us
  local copies, waits for them, and re-layouts: 20.5 us -> 28.3 us
  waiting for transfers between devices: 48.7 us -> 44 us
  Pallas kernels: 49.1 us -> 47 us
    all_to_all x1 -> x0, blocking collectives: 20.1 us -> none  [local(): lax.all_to_all(spatial, LON, 0, 0, tiled=True)]
    all_to_all x1, waiting for transfers between devices: 12.7 us -> 0.01 us  [local(): lax.all_to_all(filtered.reshape(owners, lats, owned, width), OWNERS, 0, 0...]
    all_to_all x1, waiting for transfers between devices: 14.5 us -> 25.4 us  [local(): gathered = lax.all_to_all(spectrum, OWNERS, 0, 0, tiled=True)]
    unnamed x72 -> x92, local copies, waits for them, and re-layouts: 13.7 us -> 20.8 us
    all_to_all x0 -> x1, starting transfers between devices: none -> 4.03 us  [local(): lax.all_to_all(spatial, LON, 0, 0, tiled=True)]
    ppermute x6, starting transfers between devices: 15.8 us -> 19.9 us  [shifted(): return lax.ppermute(block, ALL, pairs)]
    ppermute x6, waiting for transfers between devices: 19.8 us -> 16.6 us  [shifted(): return lax.ppermute(block, ALL, pairs)]
    all_to_all x1, starting transfers between devices: 13.8 us -> 16.6 us  [local(): gathered = lax.all_to_all(spectrum, OWNERS, 0, 0, tiled=True)]
  transfers between devices with their start and end apart: 13 -> 14, of which waited for: 8 -> 8; matrix products, arithmetic and copies ran while one was open for 5% -> 6% of each run, Pallas kernels for 18% -> 16%
where the time goes in v5:
time: 191 us; the launch traced here: 188 us
  starting transfers between devices  60.7 us (32%)
  Pallas kernels  47 us (25%)
  waiting for transfers between devices  44 us (23%)
  local copies, waits for them, and re-layouts  28.3 us (15%)
  other arithmetic  4.05 us (2%)
  matrix products  2.92 us (2%)
    all_to_all x1, waiting for transfers between devices, local(): gathered = lax.all_to_all(spectrum, OWNERS, 0, 0, tiled=True)  25.4 us
    pallas_call x2, Pallas kernels, ocean_block(): pl.pallas_call(functools.partial(ocean_kernel, block=block), out_shape=[o...  22.2 us
    unnamed x92, local copies, waits for them, and re-layouts  20.8 us
    ppermute x6, starting transfers between devices, shifted(): return lax.ppermute(block, ALL, pairs)  19.9 us
    pallas_call x4, Pallas kernels, call(): pl.pallas_call(kernel, out_shape=jax.ShapeDtypeStruct(shape, jnp.bfloat16...  17.6 us
    all_to_all x1, starting transfers between devices, local(): gathered = lax.all_to_all(spectrum, OWNERS, 0, 0, tiled=True)  16.6 us
    ppermute x6, waiting for transfers between devices, shifted(): return lax.ppermute(block, ALL, pairs)  16.6 us
    all_to_all x1, starting transfers between devices, local(): lax.all_to_all(filtered.reshape(owners, lats, owned, width), OWNERS, 0, 0...  11.1 us
  transfers between devices with their start and end apart: 14, of which 8 were waited for; matrix products, arithmetic and copies ran while one was open for 6% of the time, Pallas kernels for 16%

profile of v5, /device:TPU:1, one launch (start us, length us, event | category | flops | bytes accessed | tf_op | source)
XLA Modules:
  0.0 188.3 jit_solution(14036799904791481233)
XLA Ops:
  3.0 3.3 %collective-permute-start = (bf16[12,64,32]{1,2,0:T(8,128)(2,1)S(1)}, bf16[12,64,32]{1,2,0:T(8,128)(2,1)S(1)}, u32[]{:S(2)}, u32[]{:S(2)}) collective-permute-start(bf16[12,64,32]{1,2,0:T(8,128)(2,1)S(1)} %broadcast_select_fusion.7), channel_id=1, source_target_pairs={{0,1},{1,0},{2,3},{3,2},{4,5},{5,4},{6,7},{7,6},{8,9},{9,8},{10,11... | collective-permute-start | bytes 147464 | tf_op jit(solution)/shard_map/ppermute | solution.py:484
  7.7 1.8 shard_map.221
  9.5 4.3 %all-to-all-start = ((bf16[8,3,64,384]{3,2,1,0:T(8,128)(2,1)}), bf16[8,3,64,384]{3,2,1,0:T(8,128)(2,1)}, u32[]{:S(2)}, u32[]{:S(2)}) async-start(bf16[8,3,64,384]{3,2,1,0:T(8,128)(2,1)} %bitcast.3), calls=%async_computation | async-start | bytes 2359296 | tf_op jit(solution)/shard_map/all_to_all | solution.py:497
  21.4 3.5 %collective-permute-start.2 = (bf16[12,16,256]{2,1,0:T(8,128)(2,1)S(1)}, bf16[12,16,256]{2,1,0:T(8,128)(2,1)S(1)}, u32[]{:S(2)}, u32[]{:S(2)}) collective-permute-start(bf16[12,16,256]{2,1,0:T(8,128)(2,1)S(1)} %get-tuple-element.68), channel_id=1, source_target_pairs={{0,2},{2,4},{4,6},{6,8},{8,10},{10,12},{12,14},{1,3},{3,5},{5,7},{... | collective-permute-start | bytes 294920 | tf_op jit(solution)/shard_map/ppermute | solution.py:426
  26.3 2.5 %collective-permute-done.2 = bf16[12,16,256]{2,1,0:T(8,128)(2,1)S(1)} collective-permute-done((bf16[12,16,256]{2,1,0:T(8,128)(2,1)S(1)}, bf16[12,16,256]{2,1,0:T(8,128)(2,1)S(1)}, u32[]{:S(2)}, u32[]{:S(2)}) %collective-permute-start.2) | collective-permute-done | bytes 98336 | tf_op jit(solution)/shard_map/ppermute | solution.py:426
  28.8 2.1 %collective-permute-done.3 = bf16[12,16,256]{2,1,0:T(8,128)(2,1)S(1)} collective-permute-done((bf16[12,16,256]{2,1,0:T(8,128)(2,1)S(1)}, bf16[12,16,256]{2,1,0:T(8,128)(2,1)S(1)}, u32[]{:S(2)}, u32[]{:S(2)}) %collective-permute-start.3) | collective-permute-done | bytes 98336 | tf_op jit(solution)/shard_map/ppermute | solution.py:426
  32.3 2.3 %dynamic-slice_bitcast_fusion.table_hbm = bf16[512,1024]{1,0:T(8,128)(2,1)} fusion(bf16[2,512,1024]{2,1,0:T(8,128)(2,1)} %constant.40.clone, s32[]{:T(128)S(6)} %select_n.50), kind=kLoop, calls=%fused_computation.4 | loop fusion | bytes 2097156 | tf_op jit(solution)/shard_map/jit(dynamic_index_in_dim)/squeeze | solution.py:463
  36.0 4.6 %shard_map.223 = bf16[128,3,4,384]{3,2,1,0:T(4,128)(2,1)} custom-call(bf16[512,1024]{1,0:T(8,128)(2,1)} %dynamic-slice_bitcast_fusion.table_hbm, bf16[8,3,64,384]{3,2,1,0:T(8,128)(2,1)} %all-to-all-done.own_hbm, bf16[8,3,64,384]{3,2,1,0:T(8,128)(2,1)} %copy-done.37), custom_call_target="tpu_custom_call" | custom-call | tf_op jit(solution)/shard_map/pallas_call | solution.py:224
  40.5 16.6 %all-to-all-start.1 = ((bf16[128,3,4,384]{3,2,1,0:T(4,128)(2,1)}), bf16[128,3,4,384]{3,2,1,0:T(4,128)(2,1)}, u32[]{:S(2)}, u32[]{:S(2)}) async-start(bf16[128,3,4,384]{3,2,1,0:T(4,128)(2,1)} %shard_map.223), calls=%async_computation.1 | async-start | bytes 2359296 | tf_op jit(solution)/shard_map/all_to_all | solution.py:523
  57.2 4.2 %collective-permute-start.5 = (bf16[6,160,256]{2,1,0:T(8,128)(2,1)S(1)}, bf16[6,160,256]{2,1,0:T(8,128)(2,1)S(1)}, u32[]{:S(2)}, u32[]{:S(2)}) collective-permute-start(bf16[6,160,256]{2,1,0:T(8,128)(2,1)S(1)} %get-tuple-element.50.lower_ref), channel_id=1, source_target_pairs={{0,1},{2,3},{4,5},{6,7},{8,9},{10,11},{12,13},{14,15},{1,16},{3,18... | collective-permute-start | bytes 1474568 | tf_op jit(solution)/shard_map/ppermute | solution.py:426
  61.4 2.1 %collective-permute-start.6 = (bf16[6,160,256]{2,1,0:T(8,128)(2,1)S(1)}, bf16[6,160,256]{2,1,0:T(8,128)(2,1)S(1)}, u32[]{:S(2)}, u32[]{:S(2)}) collective-permute-start(bf16[6,160,256]{2,1,0:T(8,128)(2,1)S(1)} %get-tuple-element.49.upper_ref), channel_id=1, source_target_pairs={{1,0},{3,2},{5,4},{7,6},{9,8},{11,10},{13,12},{15,14},{16,1},{18,3... | collective-permute-start | bytes 1474568 | tf_op jit(solution)/shard_map/ppermute | solution.py:426
  63.5 25.4 %all-to-all-done.1 = bf16[128,3,4,384]{3,2,1,0:T(4,128)(2,1)} async-done(((bf16[128,3,4,384]{3,2,1,0:T(4,128)(2,1)}), bf16[128,3,4,384]{3,2,1,0:T(4,128)(2,1)}, u32[]{:S(2)}, u32[]{:S(2)}) %all-to-all-start.1) | async-done | bytes 1179680 | tf_op jit(solution)/shard_map/all_to_all | solution.py:523
  88.9 6.7 %shard_map.224 = bf16[384,4,384]{2,1,0:T(4,128)(2,1)} custom-call(f32[1,384]{1,0:T(1,128)} %broadcast_in_dim.23.gain_ref, bf16[384,4,384]{2,1,0:T(4,128)(2,1)} %bitcast.8.spectrum_hbm, bf16[2,384,384]{2,1,0:T(8,128)(2,1)} %copy-done.14, bf16[768,768]{1,0:T(8,128)(2,1)} %copy-done.10, bf16[2,384,384]{2,1,0:T(8,128)(2,1)} %copy-done.15), custom_call_target="tpu_custom_call" | custom-call | tf_op jit(solution)/shard_map/pallas_call | solution.py:224
  96.6 11.1 %all-to-all-start.2 = ((bf16[128,3,4,384]{3,2,1,0:T(4,128)(2,1)}), bf16[128,3,4,384]{3,2,1,0:T(4,128)(2,1)}, u32[]{:S(2)}, u32[]{:S(2)}) async-start(bf16[128,3,4,384]{3,2,1,0:T(4,128)(2,1)} %bitcast.31), calls=%async_computation.2 | async-start | bytes 2359296 | tf_op jit(solution)/shard_map/all_to_all | solution.py:553
  113.2 10.7 %shard_map.225 = (bf16[6,144,256]{2,1,0:T(8,128)(2,1)S(1)}, bf16[6,144,256]{2,1,0:T(8,128)(2,1)S(1)}) custom-call(s32[2]{0:T(128)S(1)} %pad_add_fusion.inside_ref, bf16[6,160,256]{2,1,0:T(8,128)(2,1)S(1)} %copy-done.17, bf16[6,160,256]{2,1,0:T(8,128)(2,1)S(1)} %get-tuple-element.49.upper_ref, bf16[6,160,256]{2,1,0:T(8,128)(2,1)S(1)} %copy-done.9, ...), custom_call_target="tpu_custom_call" | custom-call | tf_op jit(solution)/shard_map/pallas_call | solution.py:392
  123.9 6.8 %collective-permute-start.7 = (bf16[6,144,256]{2,1,0:T(8,128)(2,1)S(1)}, bf16[6,144,256]{2,1,0:T(8,128)(2,1)S(1)}, u32[]{:S(2)}, u32[]{:S(2)}) collective-permute-start(bf16[6,144,256]{2,1,0:T(8,128)(2,1)S(1)} %get-tuple-element.62.lower_ref), channel_id=1, source_target_pairs={{0,1},{2,3},{4,5},{6,7},{8,9},{10,11},{12,13},{14,15},{1,16},{3,18... | collective-permute-start | bytes 1327112 | tf_op jit(solution)/shard_map/ppermute | solution.py:426
  131.5 1.9 %collective-permute-start.8 = (bf16[6,144,256]{2,1,0:T(8,128)(2,1)S(1)}, bf16[6,144,256]{2,1,0:T(8,128)(2,1)S(1)}, u32[]{:S(2)}, u32[]{:S(2)}) collective-permute-start(bf16[6,144,256]{2,1,0:T(8,128)(2,1)S(1)} %get-tuple-element.61.upper_ref), channel_id=1, source_target_pairs={{1,0},{3,2},{5,4},{7,6},{9,8},{11,10},{13,12},{15,14},{16,1},{18,3... | collective-permute-start | bytes 1327112 | tf_op jit(solution)/shard_map/ppermute | solution.py:426
  134.2 6.2 %collective-permute-done.7.north_ref = bf16[6,144,256]{2,1,0:T(8,128)(2,1)S(1)} collective-permute-done((bf16[6,144,256]{2,1,0:T(8,128)(2,1)S(1)}, bf16[6,144,256]{2,1,0:T(8,128)(2,1)S(1)}, u32[]{:S(2)}, u32[]{:S(2)}) %collective-permute-start.7) | collective-permute-done | bytes 442400 | tf_op jit(solution)/shard_map/ppermute | solution.py:426
  141.2 5.7 %collective-permute-done.8.south_ref = bf16[6,144,256]{2,1,0:T(8,128)(2,1)S(1)} collective-permute-done((bf16[6,144,256]{2,1,0:T(8,128)(2,1)S(1)}, bf16[6,144,256]{2,1,0:T(8,128)(2,1)S(1)}, u32[]{:S(2)}, u32[]{:S(2)}) %collective-permute-start.8) | collective-permute-done | bytes 442400 | tf_op jit(solution)/shard_map/ppermute | solution.py:426
  147.6 2.3 %dynamic-slice_bitcast_fusion.1.table_hbm = bf16[512,1024]{1,0:T(8,128)(2,1)} fusion(bf16[2,512,1024]{2,1,0:T(8,128)(2,1)} %constant.41.clone, s32[]{:T(128)S(6)} %select_n.50), kind=kLoop, calls=%fused_computation.5 | loop fusion | bytes 2097156 | tf_op jit(solution)/shard_map/jit(dynamic_index_in_dim)/squeeze | solution.py:464
  151.7 4.5 %shard_map.226 = bf16[8,3,64,384]{3,2,1,0:T(8,128)(2,1)} custom-call(bf16[512,1024]{1,0:T(8,128)(2,1)} %dynamic-slice_bitcast_fusion.1.table_hbm, bf16[128,3,4,384]{3,2,1,0:T(4,128)(2,1)} %all-to-all-done.2.own_hbm, bf16[128,3,4,384]{3,2,1,0:T(4,128)(2,1)} %copy-done.38), custom_call_target="tpu_custom_call" | custom-call | tf_op jit(solution)/shard_map/pallas_call | solution.py:224
  156.2 4.0 %all-to-all-start.3 = ((bf16[8,3,64,384]{3,2,1,0:T(8,128)(2,1)}), bf16[8,3,64,384]{3,2,1,0:T(8,128)(2,1)S(1)}, u32[]{:S(2)}, u32[]{:S(2)}) async-start(bf16[8,3,64,384]{3,2,1,0:T(8,128)(2,1)} %shard_map.226), calls=%async_computation.3 | async-start | bytes 2359296 | tf_op jit(solution)/shard_map/all_to_all | solution.py:563
  166.9 11.5 %shard_map.227 = bf16[12,128,256]{2,1,0:T(8,128)(2,1)S(1)} custom-call(s32[2]{0:T(128)S(1)} %pad_add_fusion.1.inside_ref, bf16[6,144,256]{2,1,0:T(8,128)(2,1)S(1)} %copy-done.25, bf16[6,144,256]{2,1,0:T(8,128)(2,1)S(1)} %copy-done.21, bf16[6,144,256]{2,1,0:T(8,128)(2,1)S(1)} %copy-done.23, bf16[6,144,256]{2,1,0:T(8,128)(2,1)S(1)} %copy-done.27, ...), custom_call_target="tpu_custom_call" | custom-call | tf_op jit(solution)/shard_map/pallas_call | solution.py:392
  181.7 6.6 %shard_map.228 = bf16[24,64,384]{2,1,0:T(8,128)(2,1)} custom-call(bf16[24,64,384]{2,1,0:T(8,128)(2,1)S(1)} %copy-done.1, bf16[1536,32]{1,0:T(8,128)(2,1)S(1)} %bitcast.30, bf16[24,64,384]{2,1,0:T(8,128)(2,1)S(1)} %bitcast.28, bf16[32,384]{1,0:T(8,128)(2,1)S(1)} %copy-done.32, f32[1,384]{1,0:T(1,128)S(1)} %get-tuple-element.78.gain_ref, ...), custom_call_target="tpu_custom_call" | custom-call | tf_op jit(solution)/shard_map/pallas_call | solution.py:290
  (135 shorter events, 36.3 us)
Async XLA Ops:
  0.6 13.2 %copy-start = (bf16[384,32]{0,1:T(8,128)(2,1)S(1)}, bf16[384,32]{0,1:T(8,128)(2,1)}, u32[]{:S(2)}) copy-start(bf16[384,32]{0,1:T(8,128)(2,1)} %param.33) | copy-start | bytes 73732
  0.6 5.7 %copy-start.42 = (f32[2,384]{1,0:T(2,128)S(1)}, f32[2,384]{1,0:T(2,128)}, u32[]{:S(2)}) copy-start(f32[2,384]{1,0:T(2,128)} %param.30) | copy-start | bytes 9220
  1.4 6.4 %copy-start.1 = (bf16[24,64,384]{2,1,0:T(8,128)(2,1)S(1)}, bf16[24,64,384]{2,1,0:T(8,128)(2,1)}, u32[]{:S(2)}) copy-start(bf16[24,64,384]{2,1,0:T(8,128)(2,1)} %atm_ref.3) | copy-start | bytes 3538948
  1.4 6.4 %copy-start.31 = (bf16[32,384]{1,0:T(8,128)(2,1)S(1)}, bf16[32,384]{1,0:T(8,128)(2,1)}, u32[]{:S(2)}) copy-start(bf16[32,384]{1,0:T(8,128)(2,1)} %out_weight_ref.3) | copy-start | bytes 73732
  3.0 4.3 %collective-permute-start = (bf16[12,64,32]{1,2,0:T(8,128)(2,1)S(1)}, bf16[12,64,32]{1,2,0:T(8,128)(2,1)S(1)}, u32[]{:S(2)}, u32[]{:S(2)}) collective-permute-start(bf16[12,64,32]{1,2,0:T(8,128)(2,1)S(1)} %broadcast_select_fusion.7), channel_id=1, source_target_pairs={{0,1},{1,0},{2,3},{3,2},{4,5},{5,4},{6,7},{7,6},{8,9},{9,8},{10,11... | collective-permute-start | bytes 147464 | tf_op jit(solution)/shard_map/ppermute | solution.py:484
  9.5 21.5 %all-to-all-start = ((bf16[8,3,64,384]{3,2,1,0:T(8,128)(2,1)}), bf16[8,3,64,384]{3,2,1,0:T(8,128)(2,1)}, u32[]{:S(2)}, u32[]{:S(2)}) async-start(bf16[8,3,64,384]{3,2,1,0:T(8,128)(2,1)} %bitcast.3), calls=%async_computation | async-start | bytes 2359296 | tf_op jit(solution)/shard_map/all_to_all | solution.py:497
  13.9 5.2 %copy-start.13 = (bf16[2,384,384]{2,1,0:T(8,128)(2,1)S(1)}, bf16[2,384,384]{2,1,0:T(8,128)(2,1)}, u32[]{:S(2)}) copy-start(bf16[2,384,384]{2,1,0:T(8,128)(2,1)} %legendre_ref.1) | copy-start | bytes 1769476
  13.9 5.2 %copy-start.28 = (bf16[384,384]{1,0:T(8,128)(2,1)S(1)}, bf16[384,384]{1,0:T(8,128)(2,1)}, u32[]{:S(2)}) copy-start(bf16[384,384]{1,0:T(8,128)(2,1)} %real_ref.1) | copy-start | bytes 884740
  16.1 3.7 %collective-permute-start.1 = (bf16[12,64,32]{1,2,0:T(8,128)(2,1)}, bf16[12,64,32]{1,2,0:T(8,128)(2,1)}, u32[]{:S(2)}, u32[]{:S(2)}) collective-permute-start(bf16[12,64,32]{1,2,0:T(8,128)(2,1)} %broadcast_select_fusion.3), channel_id=1, source_target_pairs={{0,1},{1,0},{2,3},{3,2},{4,5},{5,4},{6,7},{7,6},{8,9},{9,8},{10,11... | collective-permute-start | bytes 147464 | tf_op jit(solution)/shard_map/ppermute | solution.py:500
  21.4 7.4 %collective-permute-start.2 = (bf16[12,16,256]{2,1,0:T(8,128)(2,1)S(1)}, bf16[12,16,256]{2,1,0:T(8,128)(2,1)S(1)}, u32[]{:S(2)}, u32[]{:S(2)}) collective-permute-start(bf16[12,16,256]{2,1,0:T(8,128)(2,1)S(1)} %get-tuple-element.68), channel_id=1, source_target_pairs={{0,2},{2,4},{4,6},{6,8},{8,10},{10,12},{12,14},{1,3},{3,5},{5,7},{... | collective-permute-start | bytes 294920 | tf_op jit(solution)/shard_map/ppermute | solution.py:426
  25.0 6.0 %collective-permute-start.3 = (bf16[12,16,256]{2,1,0:T(8,128)(2,1)S(1)}, bf16[12,16,256]{2,1,0:T(8,128)(2,1)S(1)}, u32[]{:S(2)}, u32[]{:S(2)}) collective-permute-start(bf16[12,16,256]{2,1,0:T(8,128)(2,1)S(1)} %get-tuple-element.69), channel_id=1, source_target_pairs={{2,0},{4,2},{6,4},{8,6},{10,8},{12,10},{14,12},{3,1},{5,3},{7,5},{... | collective-permute-start | bytes 294920 | tf_op jit(solution)/shard_map/ppermute | solution.py:426
  31.1 26.1 %copy-start.8 = (bf16[6,160,256]{2,1,0:T(8,128)(2,1)}, bf16[6,160,256]{2,1,0:T(8,128)(2,1)S(1)}, u32[]{:S(2)}) copy-start(bf16[6,160,256]{2,1,0:T(8,128)(2,1)S(1)} %get-tuple-element.50.lower_ref) | copy-start | bytes 1474564
  31.1 3.9 %collective-permute-start.4 = (bf16[8,3,64,384]{3,2,1,0:T(8,128)(2,1)}, bf16[8,3,64,384]{3,2,1,0:T(8,128)(2,1)S(1)}, u32[]{:S(2)}, u32[]{:S(2)}) collective-permute-start(bf16[8,3,64,384]{3,2,1,0:T(8,128)(2,1)} %all-to-all-done.own_hbm), channel_id=1, source_target_pairs={{0,1},{1,0},{2,3},{3,2},{4,5},{5,4},{6,7},{7,6},{8,9},{9,8},{10,11... | collective-permute-start | bytes 3538952 | tf_op jit(solution)/shard_map/ppermute | solution.py:520
  40.5 48.4 %all-to-all-start.1 = ((bf16[128,3,4,384]{3,2,1,0:T(4,128)(2,1)}), bf16[128,3,4,384]{3,2,1,0:T(4,128)(2,1)}, u32[]{:S(2)}, u32[]{:S(2)}) async-start(bf16[128,3,4,384]{3,2,1,0:T(4,128)(2,1)} %shard_map.223), calls=%async_computation.1 | async-start | bytes 2359296 | tf_op jit(solution)/shard_map/all_to_all | solution.py:523
  57.2 38.4 %collective-permute-start.5 = (bf16[6,160,256]{2,1,0:T(8,128)(2,1)S(1)}, bf16[6,160,256]{2,1,0:T(8,128)(2,1)S(1)}, u32[]{:S(2)}, u32[]{:S(2)}) collective-permute-start(bf16[6,160,256]{2,1,0:T(8,128)(2,1)S(1)} %get-tuple-element.50.lower_ref), channel_id=1, source_target_pairs={{0,1},{2,3},{4,5},{6,7},{8,9},{10,11},{12,13},{14,15},{1,16},{3,18... | collective-permute-start | bytes 1474568 | tf_op jit(solution)/shard_map/ppermute | solution.py:426
  61.4 34.2 %collective-permute-start.6 = (bf16[6,160,256]{2,1,0:T(8,128)(2,1)S(1)}, bf16[6,160,256]{2,1,0:T(8,128)(2,1)S(1)}, u32[]{:S(2)}, u32[]{:S(2)}) collective-permute-start(bf16[6,160,256]{2,1,0:T(8,128)(2,1)S(1)} %get-tuple-element.49.upper_ref), channel_id=1, source_target_pairs={{1,0},{3,2},{5,4},{7,6},{9,8},{11,10},{13,12},{15,14},{16,1},{18,3... | collective-permute-start | bytes 1474568 | tf_op jit(solution)/shard_map/ppermute | solution.py:426
  95.7 12.0 %copy-start.39 = (bf16[2,7,7,256]{3,0,2,1:T(2,128)(2,1)S(1)}, bf16[2,7,7,256]{3,0,2,1:T(2,128)(2,1)}, u32[]{:S(2)}) copy-start(bf16[2,7,7,256]{3,0,2,1:T(2,128)(2,1)} %param.37) | copy-start | bytes 150532
  95.7 12.2 %copy-start.45 = (f32[2,256]{1,0:T(2,128)S(1)}, f32[2,256]{1,0:T(2,128)}, u32[]{:S(2)}) copy-start(f32[2,256]{1,0:T(2,128)} %param.38) | copy-start | bytes 6148
  96.6 51.0 %all-to-all-start.2 = ((bf16[128,3,4,384]{3,2,1,0:T(4,128)(2,1)}), bf16[128,3,4,384]{3,2,1,0:T(4,128)(2,1)}, u32[]{:S(2)}, u32[]{:S(2)}) async-start(bf16[128,3,4,384]{3,2,1,0:T(4,128)(2,1)} %bitcast.31), calls=%async_computation.2 | async-start | bytes 2359296 | tf_op jit(solution)/shard_map/all_to_all | solution.py:553
  123.9 16.5 %collective-permute-start.7 = (bf16[6,144,256]{2,1,0:T(8,128)(2,1)S(1)}, bf16[6,144,256]{2,1,0:T(8,128)(2,1)S(1)}, u32[]{:S(2)}, u32[]{:S(2)}) collective-permute-start(bf16[6,144,256]{2,1,0:T(8,128)(2,1)S(1)} %get-tuple-element.62.lower_ref), channel_id=1, source_target_pairs={{0,1},{2,3},{4,5},{6,7},{8,9},{10,11},{12,13},{14,15},{1,16},{3,18... | collective-permute-start | bytes 1327112 | tf_op jit(solution)/shard_map/ppermute | solution.py:426
  131.5 15.4 %collective-permute-start.8 = (bf16[6,144,256]{2,1,0:T(8,128)(2,1)S(1)}, bf16[6,144,256]{2,1,0:T(8,128)(2,1)S(1)}, u32[]{:S(2)}, u32[]{:S(2)}) collective-permute-start(bf16[6,144,256]{2,1,0:T(8,128)(2,1)S(1)} %get-tuple-element.61.upper_ref), channel_id=1, source_target_pairs={{1,0},{3,2},{5,4},{7,6},{9,8},{11,10},{13,12},{15,14},{16,1},{18,3... | collective-permute-start | bytes 1327112 | tf_op jit(solution)/shard_map/ppermute | solution.py:426
  147.6 3.1 %collective-permute-start.9 = (bf16[128,3,4,384]{3,2,1,0:T(4,128)(2,1)}, bf16[128,3,4,384]{3,2,1,0:T(4,128)(2,1)S(1)}, u32[]{:S(2)}, u32[]{:S(2)}) collective-permute-start(bf16[128,3,4,384]{3,2,1,0:T(4,128)(2,1)} %all-to-all-done.2.own_hbm), channel_id=1, source_target_pairs={{0,1},{1,0},{2,3},{3,2},{4,5},{5,4},{6,7},{7,6},{8,9},{9,8},{10,11... | collective-permute-start | bytes 3538952 | tf_op jit(solution)/shard_map/ppermute | solution.py:560
  156.2 23.3 %all-to-all-start.3 = ((bf16[8,3,64,384]{3,2,1,0:T(8,128)(2,1)}), bf16[8,3,64,384]{3,2,1,0:T(8,128)(2,1)S(1)}, u32[]{:S(2)}, u32[]{:S(2)}) async-start(bf16[8,3,64,384]{3,2,1,0:T(8,128)(2,1)} %shard_map.226), calls=%async_computation.3 | async-start | bytes 2359296 | tf_op jit(solution)/shard_map/all_to_all | solution.py:563
  166.9 11.5 %copy-start.34 = (bf16[12,128,256]{2,1,0:T(8,128)(2,1)S(1)}, bf16[12,128,256]{2,1,0:T(8,128)(2,1)}, u32[]{:S(2)}) copy-start(bf16[12,128,256]{2,1,0:T(8,128)(2,1)} %param.23) | copy-start | bytes 2359300
  (36 other events, 62.0 us)

commit v6 on v2

--- a/solution.py
+++ b/solution.py
@@ -277,7 +277,7 @@
 REACH = STENCIL_TAPS // 2 * OCEAN_DILATION
 
 
-def ocean_rows(field, kern, gain, up, down, sums, out_ref, group, low, high):
+def ocean_rows(field, kern, gain, up, down, sums, out_ref, group, bounds):
     blocks = field.shape[0]
     rows, cols, width = out_ref.shape
     stride = cols // 8
@@ -320,6 +320,8 @@
                 axis=1,
             )
             value = centre + total[r * cols : (r + 1) * cols]
+            row_low, row_high, low, high = bounds
+            high = jnp.where((top + r >= row_low) & (top + r < row_high), high, low)
             col = lax.broadcasted_iota(jnp.int32, value.shape, 0)
             value = jnp.where((col >= low) & (col < high), value, 0.0)
             out_ref[top + r] = value.astype(jnp.bfloat16)
@@ -328,47 +330,37 @@
     lax.fori_loop(0, rows // group, step, 0)
 
 
-def ocean_kernel(
-    inside_ref,
-    centre_ref,
-    north_ref,
-    south_ref,
-    kern_ref,
-    gain_ref,
-    up_ref,
-    down_ref,
-    out_ref,
-    field,
-    sums,
-):
+def ocean_kernel(inside_ref, *refs):
+    *pieces, kern_ref, gain_ref, up_ref, down_ref, out_ref, field, sums = refs
     at = 0
-    for ref in (north_ref, centre_ref, south_ref):
+    for ref in pieces:
         for lane in range(field.shape[0]):
             field[lane, at : at + ref.shape[0]] = ref[
                 :, :, lane * LANES : (lane + 1) * LANES
             ].astype(jnp.float32)
         at += ref.shape[0]
-    group = sums.shape[1]
-    low, high = inside_ref[0], inside_ref[1]
-    ocean_rows(field, kern_ref, gain_ref, up_ref, down_ref, sums, out_ref, group, low, high)
-
-
-def ocean_block(first_col, circle, centre, north, south, kern, gain, up, down):
-    rows, cols, width = centre.shape
-    blocks, out_cols = width // LANES, cols - 2 * LEAD
+    bounds = [inside_ref[n] for n in range(4)]
+    ocean_rows(
+        field, kern_ref, gain_ref, up_ref, down_ref, sums, out_ref, sums.shape[1], bounds
+    )
+
+
+def ocean_block(corner, extent, pieces, kern, gain, up, down):
+    rows = sum(piece.shape[0] for piece in pieces)
+    cols, width = pieces[0].shape[1:]
+    blocks, out_rows, out_cols = width // LANES, rows - 2 * REACH, cols - 2 * LEAD
+    bounds = [side for at, size in zip(corner, extent) for side in (-at, size - at)]
     return call(
         ocean_kernel,
-        (rows, out_cols, width),
-        jnp.stack([-first_col, circle - first_col]).astype(jnp.int32),
-        centre,
-        north,
-        south,
+        (out_rows, out_cols, width),
+        jnp.stack(bounds).astype(jnp.int32),
+        *pieces,
         kern,
         gain,
         up,
         down,
         scratch=[
-            pltpu.VMEM((blocks, rows + 2 * REACH, cols, LANES), jnp.float32),
+            pltpu.VMEM((blocks, rows, cols, LANES), jnp.float32),
             pltpu.VMEM((blocks, 4, out_cols, LANES), jnp.float32),
         ],
         scalars=1,
@@ -485,8 +477,7 @@
     )
     spectrum, broad = lax.optimization_barrier((spectrum, broad))
     gathered = lax.all_to_all(spectrum, OWNERS, 0, 0, tiled=True)
-    north = shifted(broad[-REACH:], 1, 0)
-    south = shifted(broad[:REACH], -1, 0)
+    north, south = shifted(broad, 1, 0), shifted(broad, -1, 0)
     weights = jnp.concatenate(
         [*weighted, spec_real, -spec_imag, spec_imag, spec_real, *turned], axis=0
     )
@@ -513,7 +504,9 @@
     returned = lax.all_to_all(
         filtered.reshape(owners, lats, owned, width), OWNERS, 0, 0, tiled=True
     )
+    first_row = lax.axis_index((*LAT, "comp")) * sea_rows
     first_col = lax.axis_index(LON) * sea_cols
+    extent = (lat_total, circle)
     kernels = jnp.broadcast_to(
         ocean_kernel.astype(jnp.float32).reshape(2, STENCIL_TAPS**2, 1, sea_width),
         (2, STENCIL_TAPS**2, 8, sea_width),
@@ -521,16 +514,15 @@
     blocks = [
         (kernels[k], ocean_gain[k : k + 1], ocean_up[k], ocean_down[k]) for k in range(2)
     ]
-    first = ocean_block(first_col - LEAD, circle, broad, north, south, *blocks[0])
+    corner = (first_row - REACH, first_col - LEAD)
+    first = ocean_block(corner, extent, (north, broad, south), *blocks[0])
     returned, first = lax.optimization_barrier((returned, first))
     spatial = waves(
         (lon_count, lats, lon_dev, width), inverse, returned, lax.ppermute(returned, "comp", swap)
     )
-    north = shifted(first[-REACH:], 1, 0)
-    south = shifted(first[:REACH], -1, 0)
-    spatial, first, north, south = lax.optimization_barrier((spatial, first, north, south))
+    spatial, first = lax.optimization_barrier((spatial, first))
     spectral = lax.all_to_all(spatial, LON, 0, 0, tiled=True).reshape(lat_dev, lon_dev, width)
-    current = ocean_block(first_col, circle, first, north, south, *blocks[1])
+    current = ocean_block((first_row, first_col), extent, (first,), *blocks[1])
     ocean_out = jnp.where(wet_mask[:, :, None] == 1, current, ocean_state)
     spectral, ocean_out = lax.optimization_barrier((spectral, ocean_out))
     atm_out = epilogue(

time: 189 us -> 188 us (level)
  Pallas kernels: 48.5 us -> 59.2 us
  starting transfers between devices: 61.3 us -> 55 us
  local copies, waits for them, and re-layouts: 34 us -> 28.1 us
    pallas_call x6, Pallas kernels: 41 us -> 51.6 us  [call(): pl.pallas_call(kernel, out_shape=jax.ShapeDtypeStruct(shape, jnp.bfloat16...]
    all_to_all x1, waiting for transfers between devices: 13.5 us -> 5.61 us  [local(): lax.all_to_all(filtered.reshape(owners, lats, owned, width), OWNERS, 0, 0...]
    ppermute x6 -> x4, starting transfers between devices: 15.7 us -> 11.1 us  [shifted(): return lax.ppermute(block, ALL, pairs)]
    unnamed x58 -> x54, local copies, waits for them, and re-layouts: 14.2 us -> 10.1 us
    ppermute x6 -> x4, waiting for transfers between devices: 14.3 us -> 18.4 us  [shifted(): return lax.ppermute(block, ALL, pairs)]
    slice x2 -> x0, local copies, waits for them, and re-layouts: 3.16 us -> none  [the longest x1 2.14 us: local(): south = shifted(first[:REACH], -1, 0)]
    all_to_all x1, waiting for transfers between devices: 6.48 us -> 9.15 us  [local(): gathered = lax.all_to_all(spectrum, OWNERS, 0, 0, tiled=True)]
    broadcast_in_dim x4, local copies, waits for them, and re-layouts: 0.07 us -> 2.33 us  [local(): jnp.broadcast_to(ocean_kernel.astype(jnp.float32).reshape(2, STENCIL_TAPS...]
  transfers between devices with their start and end apart: 14 -> 12, of which waited for: 8 -> 10; matrix products, arithmetic and copies ran while one was open for 17% -> 16% of each run, Pallas kernels for 18% -> 22%
where the time goes in v6:
time: 188 us; the launch traced here: 187 us
  Pallas kernels  59.2 us (31%)
  starting transfers between devices  55 us (29%)
  waiting for transfers between devices  35.3 us (19%)
  local copies, waits for them, and re-layouts  28.1 us (15%)
  matrix products  4.28 us (2%)
  other arithmetic  3.45 us (2%)
    pallas_call x6, Pallas kernels, call(): pl.pallas_call(kernel, out_shape=jax.ShapeDtypeStruct(shape, jnp.bfloat16...  51.6 us
    ppermute x4, waiting for transfers between devices, shifted(): return lax.ppermute(block, ALL, pairs)  18.4 us
    all_to_all x1, starting transfers between devices, local(): gathered = lax.all_to_all(spectrum, OWNERS, 0, 0, tiled=True)  14.3 us
    all_to_all x1, starting transfers between devices, local(): lax.all_to_all(filtered.reshape(owners, lats, owned, width), OWNERS, 0, 0...  12.6 us
    ppermute x4, starting transfers between devices, shifted(): return lax.ppermute(block, ALL, pairs)  11.1 us
    unnamed x54, local copies, waits for them, and re-layouts  10.1 us
    all_to_all x1, waiting for transfers between devices, local(): gathered = lax.all_to_all(spectrum, OWNERS, 0, 0, tiled=True)  9.15 us
    pallas_call x1, Pallas kernels, epilogue(): pl.pallas_call(epilogue_kernel, grid=(lat_dev // rows,), out_shape=jax.Sh...  7.53 us
  transfers between devices with their start and end apart: 12, of which 10 were waited for; matrix products, arithmetic and copies ran while one was open for 16% of the time, Pallas kernels for 22%

profile of v6, /device:TPU:1, one launch (start us, length us, event | category | flops | bytes accessed | tf_op | source)
XLA Modules:
  0.0 186.5 jit_solution(5661784903225680499)
XLA Ops:
  3.1 3.3 %collective-permute-start = (bf16[12,64,32]{1,2,0:T(8,128)(2,1)S(1)}, bf16[12,64,32]{1,2,0:T(8,128)(2,1)S(1)}, u32[]{:S(2)}, u32[]{:S(2)}) collective-permute-start(bf16[12,64,32]{1,2,0:T(8,128)(2,1)S(1)} %broadcast_select_fusion.7), channel_id=1, source_target_pairs={{0,1},{1,0},{2,3},{3,2},{4,5},{5,4},{6,7},{7,6},{8,9},{9,8},{10,11... | collective-permute-start | bytes 147464 | tf_op jit(solution)/shard_map/ppermute | solution.py:442
  9.6 4.4 %all-to-all-start = ((bf16[8,3,64,384]{3,2,1,0:T(8,128)(2,1)}), bf16[8,3,64,384]{3,2,1,0:T(8,128)(2,1)}, u32[]{:S(2)}, u32[]{:S(2)}) async-start(bf16[8,3,64,384]{3,2,1,0:T(8,128)(2,1)} %bitcast.4), calls=%async_computation | async-start | bytes 2359296 | tf_op jit(solution)/shard_map/all_to_all | solution.py:455
  16.9 3.5 %collective-permute-start.2 = (bf16[12,16,256]{2,1,0:T(8,128)(2,1)S(1)}, bf16[12,16,256]{2,1,0:T(8,128)(2,1)S(1)}, u32[]{:S(2)}, u32[]{:S(2)}) collective-permute-start(bf16[12,16,256]{2,1,0:T(8,128)(2,1)S(1)} %get-tuple-element.36), channel_id=1, source_target_pairs={{0,2},{2,4},{4,6},{6,8},{8,10},{10,12},{12,14},{1,3},{3,5},{5,7},{... | collective-permute-start | bytes 294920 | tf_op jit(solution)/shard_map/ppermute | solution.py:384
  21.7 7.3 %collective-permute-done.2 = bf16[12,16,256]{2,1,0:T(8,128)(2,1)S(1)} collective-permute-done((bf16[12,16,256]{2,1,0:T(8,128)(2,1)S(1)}, bf16[12,16,256]{2,1,0:T(8,128)(2,1)S(1)}, u32[]{:S(2)}, u32[]{:S(2)}) %collective-permute-start.2) | collective-permute-done | bytes 98336 | tf_op jit(solution)/shard_map/ppermute | solution.py:384
  32.1 2.3 %dynamic-slice_bitcast_fusion.table_hbm = bf16[512,1024]{1,0:T(8,128)(2,1)} fusion(bf16[2,512,1024]{2,1,0:T(8,128)(2,1)} %constant.57.clone, s32[]{:T(128)S(6)} %select_n.50), kind=kLoop, calls=%fused_computation.6 | loop fusion | bytes 2097156 | tf_op jit(solution)/shard_map/jit(dynamic_index_in_dim)/squeeze | solution.py:421
  34.9 4.5 %shard_map.222 = bf16[128,3,4,384]{3,2,1,0:T(4,128)(2,1)} custom-call(bf16[512,1024]{1,0:T(8,128)(2,1)} %dynamic-slice_bitcast_fusion.table_hbm, bf16[8,3,64,384]{3,2,1,0:T(8,128)(2,1)} %all-to-all-done.own_hbm, bf16[8,3,64,384]{3,2,1,0:T(8,128)(2,1)} %collective-permute-done.4.other_hbm), custom_call_target="tpu_custom_call" | custom-call | tf_op jit(solution)/shard_map/pallas_call | solution.py:198
  39.5 14.3 %all-to-all-start.1 = ((bf16[128,3,4,384]{3,2,1,0:T(4,128)(2,1)}), bf16[128,3,4,384]{3,2,1,0:T(4,128)(2,1)}, u32[]{:S(2)}, u32[]{:S(2)}) async-start(bf16[128,3,4,384]{3,2,1,0:T(4,128)(2,1)} %shard_map.222), calls=%async_computation.1 | async-start | bytes 2359296 | tf_op jit(solution)/shard_map/all_to_all | solution.py:479
  56.8 1.9 %copy.29 = bf16[384,384]{1,0:T(8,128)(2,1)} copy(bf16[384,384]{0,1:T(8,128)(2,1)} %get-tuple-element.39) | data formatting | bytes 589824 | tf_op jit(solution)/shard_map/unstack | solution.py:482
  64.0 4.2 %collective-permute-start.5 = (bf16[12,160,256]{2,1,0:T(8,128)(2,1)S(1)}, bf16[12,160,256]{2,1,0:T(8,128)(2,1)}, u32[]{:S(2)}, u32[]{:S(2)}) collective-permute-start(bf16[12,160,256]{2,1,0:T(8,128)(2,1)S(1)} %pad_maximum_fusion.refs_1_), channel_id=1, source_target_pairs={{0,1},{2,3},{4,5},{6,7},{8,9},{10,11},{12,13},{14,15},{1,16},{3,18... | collective-permute-start | bytes 2949128 | tf_op jit(solution)/shard_map/ppermute | solution.py:384
  68.3 2.1 %collective-permute-start.6 = (bf16[12,160,256]{2,1,0:T(8,128)(2,1)S(1)}, bf16[12,160,256]{2,1,0:T(8,128)(2,1)}, u32[]{:S(2)}, u32[]{:S(2)}) collective-permute-start(bf16[12,160,256]{2,1,0:T(8,128)(2,1)S(1)} %pad_maximum_fusion.refs_1_), channel_id=1, source_target_pairs={{1,0},{3,2},{5,4},{7,6},{9,8},{11,10},{13,12},{15,14},{16,1},{18,3... | collective-permute-start | bytes 2949128 | tf_op jit(solution)/shard_map/ppermute | solution.py:384
  76.4 9.1 %all-to-all-done.1 = bf16[128,3,4,384]{3,2,1,0:T(4,128)(2,1)} async-done(((bf16[128,3,4,384]{3,2,1,0:T(4,128)(2,1)}), bf16[128,3,4,384]{3,2,1,0:T(4,128)(2,1)}, u32[]{:S(2)}, u32[]{:S(2)}) %all-to-all-start.1) | async-done | bytes 1179680 | tf_op jit(solution)/shard_map/all_to_all | solution.py:479
  85.5 6.8 %shard_map.223 = bf16[384,4,384]{2,1,0:T(4,128)(2,1)} custom-call(f32[1,384]{1,0:T(1,128)} %broadcast_in_dim.25.gain_ref, bf16[384,4,384]{2,1,0:T(4,128)(2,1)} %bitcast.7.spectrum_hbm, bf16[3072,384]{1,0:T(8,128)(2,1)} %fusion.2.weights_hbm), custom_call_target="tpu_custom_call" | custom-call | tf_op jit(solution)/shard_map/pallas_call | solution.py:198
  92.3 2.6 %collective-permute-done.5.refs_0_ = bf16[12,160,256]{2,1,0:T(8,128)(2,1)} collective-permute-done((bf16[12,160,256]{2,1,0:T(8,128)(2,1)S(1)}, bf16[12,160,256]{2,1,0:T(8,128)(2,1)}, u32[]{:S(2)}, u32[]{:S(2)}) %collective-permute-start.5) | collective-permute-done | bytes 983072 | tf_op jit(solution)/shard_map/ppermute | solution.py:384
  95.0 6.7 %collective-permute-done.6.refs_2_ = bf16[12,160,256]{2,1,0:T(8,128)(2,1)} collective-permute-done((bf16[12,160,256]{2,1,0:T(8,128)(2,1)S(1)}, bf16[12,160,256]{2,1,0:T(8,128)(2,1)}, u32[]{:S(2)}, u32[]{:S(2)}) %collective-permute-start.6) | collective-permute-done | bytes 983072 | tf_op jit(solution)/shard_map/ppermute | solution.py:384
  101.6 12.6 %all-to-all-start.2 = ((bf16[128,3,4,384]{3,2,1,0:T(4,128)(2,1)}), bf16[128,3,4,384]{3,2,1,0:T(4,128)(2,1)}, u32[]{:S(2)}, u32[]{:S(2)}) async-start(bf16[128,3,4,384]{3,2,1,0:T(4,128)(2,1)} %bitcast.59), calls=%async_computation.2 | async-start | bytes 2359296 | tf_op jit(solution)/shard_map/all_to_all | solution.py:504
  115.2 2.1 %slice_bitcast_fusion = (bf16[1024,256]{1,0:T(8,128)(2,1)}, bf16[1024,256]{1,0:T(8,128)(2,1)S(1)}) fusion(bf16[2,1024,256]{2,1,0:T(8,128)(2,1)} %param.40), kind=kLoop, calls=%fused_computation.11 | loop fusion | bytes 2097152 | tf_op jit(solution)/shard_map/squeeze | solution.py:515
  118.3 21.6 %shard_map.224.refs_0_ = bf16[24,144,256]{2,1,0:T(8,128)(2,1)S(1)} custom-call(s32[4]{0:T(128)S(1)} %pad_add_fusion.inside_ref, bf16[12,160,256]{2,1,0:T(8,128)(2,1)} %collective-permute-done.5.refs_0_, bf16[12,160,256]{2,1,0:T(8,128)(2,1)S(1)} %copy-done.3, bf16[12,160,256]{2,1,0:T(8,128)(2,1)} %collective-permute-done.6.refs_2_, ...), custom_call_target="tpu_custom_call" | custom-call | tf_op jit(solution)/shard_map/pallas_call | solution.py:198
  139.9 5.6 %all-to-all-done.2.own_hbm = bf16[128,3,4,384]{3,2,1,0:T(4,128)(2,1)} async-done(((bf16[128,3,4,384]{3,2,1,0:T(4,128)(2,1)}), bf16[128,3,4,384]{3,2,1,0:T(4,128)(2,1)}, u32[]{:S(2)}, u32[]{:S(2)}) %all-to-all-start.2) | async-done | bytes 1179680 | tf_op jit(solution)/shard_map/all_to_all | solution.py:504
  145.5 3.3 %collective-permute-start.7 = (bf16[128,3,4,384]{3,2,1,0:T(4,128)(2,1)}, bf16[128,3,4,384]{3,2,1,0:T(4,128)(2,1)}, u32[]{:S(2)}, u32[]{:S(2)}) collective-permute-start(bf16[128,3,4,384]{3,2,1,0:T(4,128)(2,1)} %all-to-all-done.2.own_hbm), channel_id=1, source_target_pairs={{0,1},{1,0},{2,3},{3,2},{4,5},{5,4},{6,7},{7,6},{8,9},{9,8},{10,11... | collective-permute-start | bytes 3538952 | tf_op jit(solution)/shard_map/ppermute | solution.py:521
  148.7 2.3 %dynamic-slice_bitcast_fusion.1.table_hbm = bf16[512,1024]{1,0:T(8,128)(2,1)} fusion(bf16[2,512,1024]{2,1,0:T(8,128)(2,1)} %constant.58.clone, s32[]{:T(128)S(6)} %select_n.50), kind=kLoop, calls=%fused_computation.7 | loop fusion | bytes 2097156 | tf_op jit(solution)/shard_map/jit(dynamic_index_in_dim)/squeeze | solution.py:422
  151.6 4.5 %shard_map.225 = bf16[8,3,64,384]{3,2,1,0:T(8,128)(2,1)} custom-call(bf16[512,1024]{1,0:T(8,128)(2,1)} %dynamic-slice_bitcast_fusion.1.table_hbm, bf16[128,3,4,384]{3,2,1,0:T(4,128)(2,1)} %all-to-all-done.2.own_hbm, bf16[128,3,4,384]{3,2,1,0:T(4,128)(2,1)} %collective-permute-done.7.other_hbm), custom_call_target="tpu_custom_call" | custom-call | tf_op jit(solution)/shard_map/pallas_call | solution.py:198
  156.1 4.3 %all-to-all-start.3 = ((bf16[8,3,64,384]{3,2,1,0:T(8,128)(2,1)}), bf16[8,3,64,384]{3,2,1,0:T(8,128)(2,1)}, u32[]{:S(2)}, u32[]{:S(2)}) async-start(bf16[8,3,64,384]{3,2,1,0:T(8,128)(2,1)} %shard_map.225), calls=%async_computation.3 | async-start | bytes 2359296 | tf_op jit(solution)/shard_map/all_to_all | solution.py:524
  164.9 12.5 %shard_map.226 = bf16[12,128,256]{2,1,0:T(8,128)(2,1)S(1)} custom-call(s32[4]{0:T(128)S(1)} %pad_add_fusion.1.inside_ref, bf16[24,144,256]{2,1,0:T(8,128)(2,1)S(1)} %shard_map.224.refs_0_, f32[49,8,256]{2,1,0:T(8,128)S(1)} %broadcast_in_dim.30.refs_1_, f32[1,256]{1,0:T(1,128)S(1)} %get-tuple-element.46.refs_2_, bf16[256,1024]{1,0:T(8,128)(2,1)S(1)} %copy-done.7, ...), custom_call_target="tpu_custom_call" | custom-call | tf_op jit(solution)/shard_map/pallas_call | solution.py:198
  179.0 7.5 %shard_map.227 = bf16[24,64,384]{2,1,0:T(8,128)(2,1)} custom-call(bf16[24,64,384]{2,1,0:T(8,128)(2,1)S(1)} %copy-done.1, bf16[1536,32]{1,0:T(8,128)(2,1)S(1)} %bitcast.56, bf16[24,64,384]{2,1,0:T(8,128)(2,1)} %bitcast.23.spectral_ref, bf16[32,384]{1,0:T(8,128)(2,1)S(1)} %copy-done.11, f32[1,384]{1,0:T(1,128)S(1)} %get-tuple-element.44.gain_ref, ...), custom_call_target="tpu_custom_call" | custom-call | tf_op jit(solution)/shard_map/pallas_call | solution.py:264
  (101 shorter events, 36.0 us)
Async XLA Ops:
  0.6 53.7 %copy-start = (bf16[2,384,384]{2,1,0:T(8,128)(2,1)S(1)}, bf16[2,384,384]{2,1,0:T(8,128)(2,1)}, u32[]{:S(2)}) copy-start(bf16[2,384,384]{2,1,0:T(8,128)(2,1)} %param.25) | copy-start | bytes 1769476
  0.6 7.1 %copy-start.1 = (bf16[24,64,384]{2,1,0:T(8,128)(2,1)S(1)}, bf16[24,64,384]{2,1,0:T(8,128)(2,1)}, u32[]{:S(2)}) copy-start(bf16[24,64,384]{2,1,0:T(8,128)(2,1)} %atm_ref.3) | copy-start | bytes 3538948
  0.7 7.1 %copy-start.10 = (bf16[32,384]{1,0:T(8,128)(2,1)S(1)}, bf16[32,384]{1,0:T(8,128)(2,1)}, u32[]{:S(2)}) copy-start(bf16[32,384]{1,0:T(8,128)(2,1)} %out_weight_ref.3) | copy-start | bytes 73732
  3.1 4.3 %collective-permute-start = (bf16[12,64,32]{1,2,0:T(8,128)(2,1)S(1)}, bf16[12,64,32]{1,2,0:T(8,128)(2,1)S(1)}, u32[]{:S(2)}, u32[]{:S(2)}) collective-permute-start(bf16[12,64,32]{1,2,0:T(8,128)(2,1)S(1)} %broadcast_select_fusion.7), channel_id=1, source_target_pairs={{0,1},{1,0},{2,3},{3,2},{4,5},{5,4},{6,7},{7,6},{8,9},{9,8},{10,11... | collective-permute-start | bytes 147464 | tf_op jit(solution)/shard_map/ppermute | solution.py:442
  9.6 21.3 %all-to-all-start = ((bf16[8,3,64,384]{3,2,1,0:T(8,128)(2,1)}), bf16[8,3,64,384]{3,2,1,0:T(8,128)(2,1)}, u32[]{:S(2)}, u32[]{:S(2)}) async-start(bf16[8,3,64,384]{3,2,1,0:T(8,128)(2,1)} %bitcast.4), calls=%async_computation | async-start | bytes 2359296 | tf_op jit(solution)/shard_map/all_to_all | solution.py:455
  14.9 1.4 collective-permute-start.1
  16.9 12.1 %collective-permute-start.2 = (bf16[12,16,256]{2,1,0:T(8,128)(2,1)S(1)}, bf16[12,16,256]{2,1,0:T(8,128)(2,1)S(1)}, u32[]{:S(2)}, u32[]{:S(2)}) collective-permute-start(bf16[12,16,256]{2,1,0:T(8,128)(2,1)S(1)} %get-tuple-element.36), channel_id=1, source_target_pairs={{0,2},{2,4},{4,6},{6,8},{8,10},{10,12},{12,14},{1,3},{3,5},{5,7},{... | collective-permute-start | bytes 294920 | tf_op jit(solution)/shard_map/ppermute | solution.py:384
  20.4 10.4 %collective-permute-start.3 = (bf16[12,16,256]{2,1,0:T(8,128)(2,1)S(1)}, bf16[12,16,256]{2,1,0:T(8,128)(2,1)S(1)}, u32[]{:S(2)}, u32[]{:S(2)}) collective-permute-start(bf16[12,16,256]{2,1,0:T(8,128)(2,1)S(1)} %get-tuple-element.37), channel_id=1, source_target_pairs={{2,0},{4,2},{6,4},{8,6},{10,8},{12,10},{14,12},{3,1},{5,3},{7,5},{... | collective-permute-start | bytes 294920 | tf_op jit(solution)/shard_map/ppermute | solution.py:384
  30.8 37.4 %copy-start.2 = (bf16[12,160,256]{2,1,0:T(8,128)(2,1)}, bf16[12,160,256]{2,1,0:T(8,128)(2,1)S(1)}, u32[]{:S(2)}) copy-start(bf16[12,160,256]{2,1,0:T(8,128)(2,1)S(1)} %pad_maximum_fusion.refs_1_) | copy-start | bytes 2949124
  30.8 4.1 %collective-permute-start.4 = (bf16[8,3,64,384]{3,2,1,0:T(8,128)(2,1)}, bf16[8,3,64,384]{3,2,1,0:T(8,128)(2,1)}, u32[]{:S(2)}, u32[]{:S(2)}) collective-permute-start(bf16[8,3,64,384]{3,2,1,0:T(8,128)(2,1)} %all-to-all-done.own_hbm), channel_id=1, source_target_pairs={{0,1},{1,0},{2,3},{3,2},{4,5},{5,4},{6,7},{7,6},{8,9},{9,8},{10,11... | collective-permute-start | bytes 3538952 | tf_op jit(solution)/shard_map/ppermute | solution.py:476
  39.5 14.3 %copy-start.22 = (f32[384]{0:T(512)S(1)}, f32[384]{0:T(512)}, u32[]{:S(2)}) copy-start(f32[384]{0:T(512)} %param.26) | copy-start | bytes 4612
  39.5 46.1 %all-to-all-start.1 = ((bf16[128,3,4,384]{3,2,1,0:T(4,128)(2,1)}), bf16[128,3,4,384]{3,2,1,0:T(4,128)(2,1)}, u32[]{:S(2)}, u32[]{:S(2)}) async-start(bf16[128,3,4,384]{3,2,1,0:T(4,128)(2,1)} %shard_map.222), calls=%async_computation.1 | async-start | bytes 2359296 | tf_op jit(solution)/shard_map/all_to_all | solution.py:479
  55.9 16.2 %copy-start.21 = (f32[384]{0:T(512)S(1)}, f32[384]{0:T(512)}, u32[]{:S(2)}) copy-start(f32[384]{0:T(512)} %param.29) | copy-start | bytes 4612
  60.5 12.1 %copy-start.14 = (bf16[384,384]{1,0:T(8,128)(2,1)S(1)}, bf16[384,384]{1,0:T(8,128)(2,1)}, u32[]{:S(2)}) copy-start(bf16[384,384]{1,0:T(8,128)(2,1)} %param.28) | copy-start | bytes 884740
  60.5 13.6 %copy-start.15 = (bf16[384,384]{1,0:T(8,128)(2,1)S(1)}, bf16[384,384]{1,0:T(8,128)(2,1)}, u32[]{:S(2)}) copy-start(bf16[384,384]{1,0:T(8,128)(2,1)} %param.27) | copy-start | bytes 884740
  64.0 30.9 %collective-permute-start.5 = (bf16[12,160,256]{2,1,0:T(8,128)(2,1)S(1)}, bf16[12,160,256]{2,1,0:T(8,128)(2,1)}, u32[]{:S(2)}, u32[]{:S(2)}) collective-permute-start(bf16[12,160,256]{2,1,0:T(8,128)(2,1)S(1)} %pad_maximum_fusion.refs_1_), channel_id=1, source_target_pairs={{0,1},{2,3},{4,5},{6,7},{8,9},{10,11},{12,13},{14,15},{1,16},{3,18... | collective-permute-start | bytes 2949128 | tf_op jit(solution)/shard_map/ppermute | solution.py:384
  68.3 33.4 %collective-permute-start.6 = (bf16[12,160,256]{2,1,0:T(8,128)(2,1)S(1)}, bf16[12,160,256]{2,1,0:T(8,128)(2,1)}, u32[]{:S(2)}, u32[]{:S(2)}) collective-permute-start(bf16[12,160,256]{2,1,0:T(8,128)(2,1)S(1)} %pad_maximum_fusion.refs_1_), channel_id=1, source_target_pairs={{1,0},{3,2},{5,4},{7,6},{9,8},{11,10},{13,12},{15,14},{16,1},{18,3... | collective-permute-start | bytes 2949128 | tf_op jit(solution)/shard_map/ppermute | solution.py:384
  92.3 22.0 %copy-start.17 = (bf16[2,7,7,256]{3,0,2,1:T(2,128)(2,1)S(1)}, bf16[2,7,7,256]{3,0,2,1:T(2,128)(2,1)}, u32[]{:S(2)}) copy-start(bf16[2,7,7,256]{3,0,2,1:T(2,128)(2,1)} %param.37) | copy-start | bytes 150532
  92.3 22.9 %copy-start.23 = (f32[2,256]{1,0:T(2,128)S(1)}, f32[2,256]{1,0:T(2,128)}, u32[]{:S(2)}) copy-start(f32[2,256]{1,0:T(2,128)} %param.38) | copy-start | bytes 6148
  101.6 15.7 %copy-start.16 = (bf16[2,256,1024]{2,1,0:T(8,128)(2,1)S(1)}, bf16[2,256,1024]{2,1,0:T(8,128)(2,1)}, u32[]{:S(2)}) copy-start(bf16[2,256,1024]{2,1,0:T(8,128)(2,1)} %param.39) | copy-start | bytes 3145732
  101.6 43.8 %all-to-all-start.2 = ((bf16[128,3,4,384]{3,2,1,0:T(4,128)(2,1)}), bf16[128,3,4,384]{3,2,1,0:T(4,128)(2,1)}, u32[]{:S(2)}, u32[]{:S(2)}) async-start(bf16[128,3,4,384]{3,2,1,0:T(4,128)(2,1)} %bitcast.59), calls=%async_computation.2 | async-start | bytes 2359296 | tf_op jit(solution)/shard_map/all_to_all | solution.py:504
  145.5 6.1 %collective-permute-start.7 = (bf16[128,3,4,384]{3,2,1,0:T(4,128)(2,1)}, bf16[128,3,4,384]{3,2,1,0:T(4,128)(2,1)}, u32[]{:S(2)}, u32[]{:S(2)}) collective-permute-start(bf16[128,3,4,384]{3,2,1,0:T(4,128)(2,1)} %all-to-all-done.2.own_hbm), channel_id=1, source_target_pairs={{0,1},{1,0},{2,3},{3,2},{4,5},{5,4},{6,7},{7,6},{8,9},{9,8},{10,11... | collective-permute-start | bytes 3538952 | tf_op jit(solution)/shard_map/ppermute | solution.py:521
  156.1 22.4 %all-to-all-start.3 = ((bf16[8,3,64,384]{3,2,1,0:T(8,128)(2,1)}), bf16[8,3,64,384]{3,2,1,0:T(8,128)(2,1)}, u32[]{:S(2)}, u32[]{:S(2)}) async-start(bf16[8,3,64,384]{3,2,1,0:T(8,128)(2,1)} %shard_map.225), calls=%async_computation.3 | async-start | bytes 2359296 | tf_op jit(solution)/shard_map/all_to_all | solution.py:524
  164.9 12.5 %copy-start.13 = (bf16[12,128,256]{2,1,0:T(8,128)(2,1)S(1)}, bf16[12,128,256]{2,1,0:T(8,128)(2,1)}, u32[]{:S(2)}) copy-start(bf16[12,128,256]{2,1,0:T(8,128)(2,1)} %param.23) | copy-start | bytes 2359300
  (12 other events, 38.1 us)
